TPU v7x, 256 devices: a whole 4x4x8 slice. The times are simulated.
256 devices in a mesh: expert: 32 (over z, x), tensor: 8 (over y, core).
Axes of the slice: x: 4, y: 4, z: 8, core: 2. Of those that a mesh axis runs over, the one named last changes fastest.
Arguments:
- attn_out: bfloat16 [4096, 4096], P('expert', 'tensor'), may hold values from -6 to 6
- residual: bfloat16 [4096, 4096], P('expert'), may hold values from -6 to 6
- o_weight: bfloat16 [4096, 4096], P('tensor'), may hold values from -0.09375 to 0.09375
- norm_gain: float32 [4096], replicated, may hold values from 0.5 to 1.5
- router_weight: bfloat16 [4096, 32], replicated, may hold values from -0.09375 to 0.09375
- expert_idx: int32 [4096, 8], P('expert'), may hold values from 0 to 31, all different within a row; in each aligned block of 16 rows (0 to 15, 16 to 31, ...) at most 6 rows name the same one
- combine: float32 [4096, 8], P('expert'), may hold values from 0.05 to 0.25
- w_gate: bfloat16 [32, 4096, 1536], P('expert', None, 'tensor'), may hold values from -0.09375 to 0.09375
- w_up: bfloat16 [32, 4096, 1536], P('expert', None, 'tensor'), may hold values from -0.09375 to 0.09375
- w_down: bfloat16 [32, 1536, 4096], P('expert', 'tensor'), may hold values from -0.15625 to 0.15625
Outputs:
- mixed: bfloat16 [4096, 4096], P('expert')
- router_logits: float32 [4096, 32], P('expert')
Inputs may be any that keep to these rules, and one draw needn't show every extreme that they name: `expert_idx`: each row names 8 different experts. In each aligned block of 16 tokens no expert is named by more than 6 tokens, a bound that some block reaches.
All inputs are finite; a program needn't handle non-finite values.
Results may differ from a plain program's by a relative error of at most 0.015.
Values may be sent and summed in bfloat16 or wider, within the bound.
No kernel may reach another device: no remote copies, remote signals or barrier semaphores. Data moves between devices by JAX's collectives and lax.ppermute only.
A program may use at most 128 MiB of HBM per device.

v0:
```python
import jax
import jax.numpy as jnp
from jax import lax
from jax.sharding import PartitionSpec as P

epsilon = 1e-06


def rms_scaled(stream, norm_gain):
    stream_wide = stream.astype(jnp.float32)
    scale = lax.rsqrt(jnp.mean(stream_wide * stream_wide, axis=-1, keepdims=True) + epsilon)
    return (stream_wide * scale * norm_gain).astype(jnp.bfloat16)


def slot_targets(chosen, expert_count, capacity):
    flat_ids = chosen.reshape(-1)
    one_hot = (flat_ids[:, None] == jnp.arange(expert_count, dtype=jnp.int32)[None, :]).astype(
        jnp.int32
    )
    slot_index = jnp.sum((jnp.cumsum(one_hot, axis=0) - 1) * one_hot, axis=1)
    return (flat_ids * capacity + slot_index).reshape(chosen.shape)


def selector(targets, slot_total):
    slots = jnp.arange(slot_total, dtype=jnp.int32)
    hits = jnp.any(slots[:, None, None] == targets[None, :, :], axis=2)
    return hits.astype(jnp.bfloat16)


def expert_hidden(rows_in, w_gate, w_up):
    flat_rows = rows_in.reshape(-1, rows_in.shape[-1])
    gate = jnp.dot(flat_rows, w_gate[0], preferred_element_type=jnp.float32)
    up_val = jnp.dot(flat_rows, w_up[0], preferred_element_type=jnp.float32)
    return (jax.nn.silu(gate) * up_val).astype(jnp.bfloat16)


def shards(
    attn_out,
    residual,
    o_weight,
    norm_gain,
    router_weight,
    expert_idx,
    combine,
    w_gate,
    w_up,
    w_down,
):
    tensor_size = lax.axis_size("tensor")
    tensor_rank = lax.axis_index("tensor")
    group_rows = residual.shape[0]
    width = residual.shape[1]
    rows_dev = group_rows // tensor_size
    expert_count = router_weight.shape[1]
    top_count = expert_idx.shape[1]
    capacity = min(rows_dev, max(2, 3 * rows_dev * top_count // (2 * expert_count)))
    slot_total = expert_count * capacity
    offset_mine = tensor_rank * rows_dev
    my_chosen = lax.dynamic_slice_in_dim(expert_idx, offset_mine, rows_dev, 0)
    my_combine = lax.dynamic_slice_in_dim(combine, offset_mine, rows_dev, 0)
    my_target = slot_targets(my_chosen, expert_count, capacity)
    projected = lax.psum(
        jnp.dot(attn_out, o_weight, preferred_element_type=jnp.float32).astype(jnp.bfloat16),
        "tensor",
    ).astype(jnp.float32)
    stream_all = (residual.astype(jnp.float32) + projected).astype(jnp.bfloat16)
    normed_all = rms_scaled(stream_all, norm_gain)
    stream = lax.dynamic_slice_in_dim(stream_all, offset_mine, rows_dev, 0)
    normed = lax.dynamic_slice_in_dim(normed_all, offset_mine, rows_dev, 0)
    block_chosen = expert_idx.reshape(tensor_size, rows_dev, top_count)
    all_targets = jax.vmap(lambda chosen: slot_targets(chosen, expert_count, capacity))(
        block_chosen
    )
    selectors = jax.vmap(lambda targets: selector(targets, slot_total))(all_targets)
    outbox = jnp.einsum(
        "bsr,brd->bsd",
        selectors,
        normed_all.reshape(tensor_size, rows_dev, width),
        preferred_element_type=jnp.float32,
    ).astype(jnp.bfloat16)
    outbox = outbox.reshape(tensor_size, expert_count, capacity, width)
    arrived = lax.all_to_all(outbox, "expert", split_axis=1, concat_axis=1, tiled=True)
    hidden = expert_hidden(arrived, w_gate, w_up)
    router_logits = jnp.dot(normed, router_weight, preferred_element_type=jnp.float32)
    summed = lax.psum_scatter(
        jnp.dot(hidden, w_down[0], preferred_element_type=jnp.float32).astype(jnp.bfloat16),
        "tensor",
        scatter_dimension=0,
        tiled=True,
    )
    expert_out = summed.reshape(expert_count, capacity, width)
    returned = lax.all_to_all(
        expert_out, "expert", split_axis=0, concat_axis=0, tiled=True
    ).reshape(slot_total, width)
    slots = jnp.arange(slot_total, dtype=jnp.int32)
    weight_matrix = jnp.sum(
        my_combine[:, :, None]
        * (my_target[:, :, None] == slots[None, None, :]).astype(jnp.float32),
        axis=1,
    )
    moe = jnp.dot(weight_matrix, returned.astype(jnp.float32), precision=lax.Precision.HIGHEST)
    mixed = (stream.astype(jnp.float32) + moe).astype(jnp.bfloat16)
    mixed_group, logits_group = (
        lax.all_gather(
            mixed.astype(jnp.float32).astype(jnp.bfloat16), "tensor", axis=0, tiled=True
        ).astype(jnp.float32),
        lax.all_gather(router_logits.astype(jnp.bfloat16), "tensor", axis=0, tiled=True).astype(
            router_logits.dtype
        ),
    )
    return (mixed_group.astype(jnp.bfloat16), logits_group)


def solution(mesh):
    in_specs = (
        P("expert", "tensor"),
        P("expert", None),
        P("tensor", None),
        P(),
        P(),
        P("expert", None),
        P("expert", None),
        P("expert", None, "tensor"),
        P("expert", None, "tensor"),
        P("expert", "tensor", None),
    )
    out_specs = (P("expert", None), P("expert", None))
    return jax.shard_map(shards, mesh=mesh, in_specs=in_specs, out_specs=out_specs, check_vma=False)
```

profile of v0, /device:TPU:1, one launch (start us, length us, event | category | flops | bytes accessed | tf_op | source)
XLA Modules:
  0.0 632.0 jit_solution(10479870324619481833)
XLA Ops:
  7.2 4.1 convolution_convert_fusion.2
  11.8 2.5 select_reduce_fusion
  14.4 0.4 fusion.15
  14.9 66.2 %all-reduce.2.cloned.1.call-done = bf16[128,4096]{1,0:T(8,128)(2,1)} async-done(((bf16[128,4096]{1,0:T(8,128)(2,1)}), bf16[128,4096]{1,0:T(8,128)(2,1)}) %all-reduce.2.cloned.1.call-update) | async-done | bytes 1048592 | tf_op jit(solution)/shard_map/psum | solution.py:62
  81.1 1.7 fusion.2
  83.1 0.6 copy-done.1
  83.7 3.7 convolution_convert_fusion.1
  87.4 16.4 %copy.39 = bf16[8,192,4096]{2,0,1:T(8,128)(2,1)S(1)} copy(bf16[8,192,4096]{2,1,0:T(8,128)(2,1)S(1)} %convolution_convert_fusion.1) | data formatting | bytes 25165824 | tf_op jit(solution)/shard_map/convert_element_type | solution.py:80
  103.8 281.2 %all_to_all.10 = bf16[8,32,6,4096]{3,0,2,1:T(8,128)(2,1)S(1)} all-to-all(bf16[8,32,6,4096]{3,0,2,1:T(8,128)(2,1)S(1)} %bitcast.23), channel_id=1, replica_groups=mesh['expert'=32,'tensor'=8] {'expert'}, dimensions={1} | all-to-all | bytes 25165824 | tf_op jit(solution)/shard_map/all_to_all | solution.py:82
  385.0 21.2 %copy.40 = bf16[8,32,6,4096]{3,2,1,0:T(8,128)(2,1)} copy(bf16[8,32,6,4096]{3,0,2,1:T(8,128)(2,1)S(1)} %all_to_all.10) | data formatting | bytes 25165824 | tf_op jit(solution)/shard_map/all_to_all | solution.py:82
  406.3 18.8 %reshape.53 = bf16[1536,4096]{1,0:T(8,128)(2,1)} reshape(bf16[8,32,6,4096]{3,2,1,0:T(8,128)(2,1)} %copy.40) | data formatting | bytes 25165824 | tf_op jit(solution)/shard_map/reshape | solution.py:31
  425.0 10.4 %fusion.8 = f32[1536,192]{0,1:T(8,128)} fusion(bf16[1536,4096]{1,0:T(8,128)(2,1)} %reshape.53, bf16[1,4096,192]{1,2,0:T(8,128)(2,1)} %param.17), kind=kOutput, calls=%fused_computation.15 | convolution fusion | flops 2415919104 | bytes 15335424 | tf_op jit(solution)/shard_map/dot_general | solution.py:32
  435.4 20.0 %convolution_convert_fusion = bf16[1536,4096]{1,0:T(8,128)(2,1)} fusion(bf16[1536,4096]{1,0:T(8,128)(2,1)} %reshape.53, bf16[1,192,4096]{2,1,0:T(8,128)(2,1)S(1)} %copy-done, bf16[1,4096,192]{1,2,0:T(8,128)(2,1)} %param.18, f32[1536,192]{0,1:T(8,128)} %fusion.8), kind=kOutput, calls=%fused_computation | convolution fusion | flops 4839899136 | bytes 29491200 | tf_op jit(solution)/shard_map/dot_general | solution.py:86
  455.5 75.8 %reduce-scatter.2.cloned.1.call-done = bf16[192,4096]{1,0:T(8,128)(2,1)} async-done(((bf16[1536,4096]{1,0:T(8,128)(2,1)}), bf16[192,4096]{1,0:T(8,128)(2,1)}) %reduce-scatter.2.cloned.1.call-update) | async-done | bytes 1572880 | tf_op jit(solution)/shard_map/reduce_scatter | solution.py:85
  531.3 3.5 reshape.54
  534.8 9.8 %all-to-all-start.1 = ((bf16[32,6,4096]{2,1,0:T(8,128)(2,1)}), bf16[32,6,4096]{2,1,0:T(8,128)(2,1)}, u32[]{:S(2)}, u32[]{:S(2)}) async-start(bf16[32,6,4096]{2,1,0:T(8,128)(2,1)} %reshape.54), calls=%async_computation.2 | async-start | bytes 4194304 | tf_op jit(solution)/shard_map/all_to_all | solution.py:92
  545.6 46.9 %all-to-all-done.1 = bf16[32,6,4096]{2,1,0:T(8,128)(2,1)} async-done(((bf16[32,6,4096]{2,1,0:T(8,128)(2,1)}), bf16[32,6,4096]{2,1,0:T(8,128)(2,1)}, u32[]{:S(2)}, u32[]{:S(2)}) %all-to-all-start.1) | async-done | bytes 1572896 | tf_op jit(solution)/shard_map/all_to_all | solution.py:92
  592.6 2.5 reshape.55
  595.1 2.3 fusion
  597.4 1.1 convolution_convert_fusion.3
  598.5 16.5 %all_gather.7 = bf16[128,32]{1,0:T(8,128)(2,1)S(1)} all-gather(bf16[16,32]{1,0:T(8,128)(2,1)S(1)} %convolution_convert_fusion.3), channel_id=1, replica_groups=mesh['expert'=32,'tensor'=8] {'tensor'}, dimensions={0}, use_global_device_ids=true | all-gather | bytes 9216 | tf_op jit(solution)/shard_map/all_gather | solution.py:107
  615.0 0.7 copy.41
  615.7 7.4 %all-gather.2.cloned.1.call-done = bf16[128,4096]{1,0:T(8,128)(2,1)} async-done(((bf16[16,4096]{1,0:T(8,128)(2,1)}), bf16[128,4096]{1,0:T(8,128)(2,1)}) %all-gather.2.cloned.1.call-update) | async-done | bytes 1048592 | tf_op jit(solution)/shard_map/all_gather | solution.py:104
  623.2 2.3 copy.45
  (40 shorter events, 1.9 us)
Async XLA Ops:
  7.2 428.2 %copy-start = (bf16[1,192,4096]{2,1,0:T(8,128)(2,1)S(1)}, bf16[1,192,4096]{2,1,0:T(8,128)(2,1)}, u32[]{:S(2)}) copy-start(bf16[1,192,4096]{2,1,0:T(8,128)(2,1)} %param.19) | copy-start | bytes 4718596
  7.2 4.2 copy-start.6
  7.2 73.9 %all-reduce.2.cloned.1.call-start = ((), (), s32[]{:S(2)}) async-start(), calls=%async_computation.3 | async-start | bytes 2097152 | tf_op jit(solution)/shard_map/psum | solution.py:62
  11.3 69.8 %copy-start.3 = (bf16[128,4096]{1,0:T(8,128)(2,1)S(1)}, bf16[128,4096]{1,0:T(8,128)(2,1)}, u32[]{:S(2)}) copy-start(bf16[128,4096]{1,0:T(8,128)(2,1)} %param.11) | copy-start | bytes 3145732
  11.3 71.5 %copy-start.5 = (f32[4096]{0:T(1024)S(1)}, f32[4096]{0:T(1024)}, u32[]{:S(2)}) copy-start(f32[4096]{0:T(1024)} %param.13) | copy-start | bytes 49156
  11.3 520.0 %reduce-scatter.2.cloned.1.call-start = ((), (), s32[]{:S(2)}) async-start(), calls=%async_computation.4 | async-start | bytes 14155776 | tf_op jit(solution)/shard_map/reduce_scatter | solution.py:85
  82.7 1.0 copy-start.1
  83.7 3.7 copy-start.2
  534.8 9.9 %copy-start.7 = (f32[128,8]{0,1:T(8,128)S(1)}, f32[128,8]{0,1:T(8,128)}, u32[]{:S(2)}) copy-start(f32[128,8]{0,1:T(8,128)} %param.16) | copy-start | bytes 12292
  534.8 57.8 %all-to-all-start.1 = ((bf16[32,6,4096]{2,1,0:T(8,128)(2,1)}), bf16[32,6,4096]{2,1,0:T(8,128)(2,1)}, u32[]{:S(2)}, u32[]{:S(2)}) async-start(bf16[32,6,4096]{2,1,0:T(8,128)(2,1)} %reshape.54), calls=%async_computation.2 | async-start | bytes 4194304 | tf_op jit(solution)/shard_map/all_to_all | solution.py:92
  544.6 78.6 %all-gather.2.cloned.1.call-start = ((), (), s32[]{:S(2)}) async-start(), calls=%async_computation.5 | async-start | bytes 1179648 | tf_op jit(solution)/shard_map/all_gather | solution.py:104
  545.6 51.8 %copy-start.4 = (bf16[4096,32]{0,1:T(8,128)(2,1)S(1)}, bf16[4096,32]{0,1:T(8,128)(2,1)}, u32[]{:S(2)}) copy-start(bf16[4096,32]{0,1:T(8,128)(2,1)} %param.14) | copy-start | bytes 786436
Sparse Core Ops, SparseCore 0:
  11.4 69.5 all-reduce.1
  455.6 75.6 reduce-scatter.1
  597.5 25.5 all-gather.1
where the time goes:
time: 633 us; the launch traced here: 632 us
  blocking collectives  298 us (47%)
  waiting for transfers between devices  196 us (31%)
  local copies, waits for them, and re-layouts  66.9 us (11%)
  matrix products  41.5 us (7%)
  between operations  13.9 us (2%)
  starting transfers between devices  9.91 us (2%)
    all_to_all x1, blocking collectives, shards(): lax.all_to_all(outbox, 'expert', split_axis=1, concat_axis=1, tiled=True)  281 us
    reduce_scatter x1, waiting for transfers between devices, shards(): lax.psum_scatter(jnp.dot(hidden, w_down[0], preferred_element_type=jnp.fl...  75.8 us
    psum x1, waiting for transfers between devices, shards(): lax.psum(jnp.dot(attn_out, o_weight, preferred_element_type=jnp.float32)....  66.2 us
    all_to_all x1, waiting for transfers between devices, shards(): lax.all_to_all(expert_out, 'expert', split_axis=0, concat_axis=0, tiled=T...  46.9 us
    all_to_all x1, local copies, waits for them, and re-layouts, shards(): lax.all_to_all(outbox, 'expert', split_axis=1, concat_axis=1, tiled=True)  21.2 us
    dot_general x1, matrix products, shards(): jnp.dot(hidden, w_down[0], preferred_element_type=jnp.float32)  20 us
    reshape x1, local copies, waits for them, and re-layouts, expert_hidden(): flat_rows = rows_in.reshape(-1, rows_in.shape[-1])  18.8 us
    all_gather x1, blocking collectives, shards(): lax.all_gather(router_logits.astype(jnp.bfloat16), 'tensor', axis=0, tile...  16.5 us
  transfers between devices with their start and end apart: 4, of which 4 were waited for; matrix products, arithmetic and copies ran while one was open for 1% of the time, Pallas kernels for 0%

commit v1 on v0

v1 whole, which is shorter than its diff:
```python
import jax
import jax.numpy as jnp
from jax import lax
from jax.experimental import pallas as pl
from jax.experimental.pallas import tpu as pltpu
from jax.sharding import PartitionSpec as P


epsilon = 1e-06
PIECES = 8
f32 = jnp.float32
bf16 = jnp.bfloat16


def slot_targets(chosen, expert_count, capacity):
    flat_ids = chosen.reshape(-1)
    one_hot = (flat_ids[:, None] == jnp.arange(expert_count, dtype=jnp.int32)[None, :]).astype(
        jnp.int32
    )
    slot_index = jnp.sum((jnp.cumsum(one_hot, axis=0) - 1) * one_hot, axis=1)
    return (flat_ids * capacity + slot_index).reshape(chosen.shape)


def swap_matrix(capacity):
    size = PIECES * PIECES * capacity
    row = lax.broadcasted_iota(jnp.int32, (size, size), 0)
    col = lax.broadcasted_iota(jnp.int32, (size, size), 1)
    stride = PIECES * capacity
    source = (row % stride) // capacity * stride + row // stride * capacity + row % capacity
    return (col == source).astype(bf16)


def pieces_to_rows(x):
    width = x.shape[1] // PIECES
    return jnp.concatenate([x[:, j * width : (j + 1) * width] for j in range(PIECES)], axis=0)


def front_kernel(parts, residual, gain, router, hits, outbox, stream_out, logits_out):
    total = parts[0].astype(f32)
    for i in range(1, parts.shape[0]):
        total = total + parts[i].astype(f32)
    stream = (residual[...].astype(f32) + total).astype(bf16)
    wide = stream.astype(f32)
    scale = lax.rsqrt(jnp.mean(wide * wide, axis=-1, keepdims=True) + epsilon)
    normed = (wide * scale * gain[...]).astype(bf16)
    stream_out[...] = pieces_to_rows(stream)
    logits_out[...] = lax.dot_general(
        normed, router[...], (((1,), (1,)), ((), ())), preferred_element_type=f32
    )
    outbox[...] = lax.dot_general(
        hits[...],
        pieces_to_rows(normed),
        (((0,), (0,)), ((), ())),
        preferred_element_type=f32,
    ).astype(bf16)


def front(parts, residual, gain, router, hits):
    _, rows, width = parts.shape
    piece = width // PIECES
    return pl.pallas_call(
        front_kernel,
        out_shape=(
            jax.ShapeDtypeStruct((hits.shape[1], piece), bf16),
            jax.ShapeDtypeStruct((rows * PIECES, piece), bf16),
            jax.ShapeDtypeStruct((rows, router.shape[0]), f32),
        ),
        compiler_params=pltpu.CompilerParams(vmem_limit_bytes=40 * 2**20),
        name="front",
    )(parts, residual, gain, router, hits)


def swap_kernel(x, swap, out):
    moved = jnp.dot(swap[...], x[...], preferred_element_type=f32).astype(bf16)
    out[...] = moved.reshape(out.shape)


def rows_by_piece(x, swap):
    size = swap.shape[0]
    steps = x.shape[0] // size
    width = x.shape[1]
    run = size // PIECES
    return pl.pallas_call(
        swap_kernel,
        grid=(steps,),
        in_specs=[
            pl.BlockSpec((size, width), lambda a: (a, 0)),
            pl.BlockSpec((size, size), lambda a: (0, 0)),
        ],
        out_specs=pl.BlockSpec((PIECES, run, width), lambda a: (0, a, 0)),
        out_shape=jax.ShapeDtypeStruct((PIECES, run * steps, width), bf16),
        name="rows_by_piece",
    )(x, swap)


def dot_last(a, b):
    return lax.dot_general(a, b, (((1,), (1,)), ((), ())), preferred_element_type=f32)


def up_kernel(x, w_gate, w_up, out):
    width = x.shape[3]
    gate = None
    for j in range(PIECES):
        part = x[0, j]
        columns = slice(j * width, (j + 1) * width)
        g = dot_last(part, w_gate[:, columns])
        u = dot_last(part, w_up[:, columns])
        gate, up = (g, u) if gate is None else (gate + g, up + u)
    out[0] = (gate / (1.0 + jnp.exp(-gate)) * up).astype(bf16)


def up_rows(x, w_gate, w_up):
    ranks, pieces, rows, width = x.shape
    units, depth = w_gate.shape
    return pl.pallas_call(
        up_kernel,
        grid=(ranks,),
        in_specs=[
            pl.BlockSpec((1, pieces, rows, width), lambda r: (r, 0, 0, 0)),
            pl.BlockSpec((units, depth), lambda r: (0, 0)),
            pl.BlockSpec((units, depth), lambda r: (0, 0)),
        ],
        out_specs=pl.BlockSpec((1, rows, units), lambda r: (r, 0, 0)),
        out_shape=jax.ShapeDtypeStruct((ranks, rows, units), bf16),
        compiler_params=pltpu.CompilerParams(vmem_limit_bytes=40 * 2**20),
        name="up_rows",
    )(x, w_gate, w_up)


def down_kernel(hidden, w_down, swap, out, held):
    j = pl.program_id(0)
    ranks, rows, units = hidden.shape
    total = None
    for r in range(ranks):
        part = jnp.dot(
            hidden[r], w_down[r * units : (r + 1) * units, :], preferred_element_type=f32
        )
        total = part if total is None else total + part
    held[j] = total.astype(bf16)

    @pl.when(j == PIECES - 1)
    def _():
        size = swap.shape[0]
        run = size // PIECES
        for a in range(rows // run):
            block = held[:, a * run : (a + 1) * run, :].reshape(size, held.shape[2])
            out[a * size : (a + 1) * size, :] = jnp.dot(
                swap[...], block, preferred_element_type=f32
            ).astype(bf16)


def down_rows(hidden, w_down, swap):
    ranks, rows, units = hidden.shape
    depth, width = w_down.shape
    piece = width // PIECES
    return pl.pallas_call(
        down_kernel,
        grid=(PIECES,),
        in_specs=[
            pl.BlockSpec((ranks, rows, units), lambda j: (0, 0, 0)),
            pl.BlockSpec((depth, piece), lambda j: (0, j)),
            pl.BlockSpec(swap.shape, lambda j: (0, 0)),
        ],
        out_specs=pl.BlockSpec((rows * PIECES, piece), lambda j: (0, 0)),
        out_shape=jax.ShapeDtypeStruct((rows * PIECES, piece), bf16),
        scratch_shapes=[pltpu.VMEM((PIECES, rows, piece), bf16)],
        compiler_params=pltpu.CompilerParams(vmem_limit_bytes=40 * 2**20),
        name="down_rows",
    )(hidden, w_down, swap)


def finish_kernel(returned, weights, stream, logits, out):
    high = weights[...].astype(bf16)
    low = (weights[...] - high.astype(f32)).astype(bf16)
    moe = jnp.dot(high, returned[...], preferred_element_type=f32) + jnp.dot(
        low, returned[...], preferred_element_type=f32
    )
    rows = stream.shape[0]
    out[0:rows, :] = (stream[...].astype(f32) + moe).astype(bf16)
    logit_high = logits[...].astype(bf16)
    logit_low = (logits[...] - logit_high.astype(f32)).astype(bf16)
    count = logits.shape[1]
    filler = jnp.zeros((logits.shape[0], out.shape[1] - 2 * count), bf16)
    out[rows:, :] = jnp.concatenate([logit_high, logit_low, filler], axis=1)


def finish(returned, weights, stream, logits):
    return pl.pallas_call(
        finish_kernel,
        out_shape=jax.ShapeDtypeStruct(
            (stream.shape[0] + logits.shape[0], stream.shape[1]), bf16
        ),
        compiler_params=pltpu.CompilerParams(vmem_limit_bytes=40 * 2**20),
        name="finish",
    )(returned, weights, stream, logits)


def routing(chosen, combine, expert_count, capacity):
    targets = slot_targets(chosen, expert_count, capacity)
    tokens = chosen.shape[0]
    total = expert_count * PIECES * capacity
    row = lax.broadcasted_iota(jnp.int32, (PIECES * tokens, total), 0)
    col = lax.broadcasted_iota(jnp.int32, (PIECES * tokens, total), 1)
    run = PIECES * capacity
    same_piece = row // tokens == (col % run) // capacity
    slot_of = col // run * capacity + col % capacity
    wanted = jnp.where(same_piece, slot_of, -1)
    targets = jnp.tile(targets, (PIECES, 1))
    combine = jnp.tile(combine, (PIECES, 1))
    weights = jnp.zeros((PIECES * tokens, total), f32)
    hits = jnp.zeros((PIECES * tokens, total), jnp.bool_)
    for k in range(chosen.shape[1]):
        match = wanted == targets[:, k : k + 1]
        weights = weights + jnp.where(match, combine[:, k : k + 1], 0.0)
        hits = hits | match
    return hits.astype(bf16), weights


def shards(
    attn_out,
    residual,
    o_weight,
    norm_gain,
    router_weight,
    expert_idx,
    combine,
    w_gate,
    w_up,
    w_down,
):
    ranks = lax.axis_size("tensor")
    rank = lax.axis_index("tensor")
    group_rows, width = residual.shape
    rows = group_rows // ranks
    piece = width // PIECES
    expert_count = router_weight.shape[1]
    top_count = expert_idx.shape[1]
    capacity = min(rows, max(2, 3 * rows * top_count // (2 * expert_count)))

    w_down_all = lax.all_gather(w_down[0], "tensor", axis=0, tiled=True)
    swap = swap_matrix(capacity)
    chosen = lax.dynamic_slice_in_dim(expert_idx, rank * rows, rows, 0)
    my_combine = lax.dynamic_slice_in_dim(combine, rank * rows, rows, 0)
    hits, weights = routing(chosen, my_combine, expert_count, capacity)
    my_residual = lax.dynamic_slice_in_dim(residual, rank * rows, rows, 0)

    partial = jnp.dot(attn_out, o_weight, preferred_element_type=f32).astype(bf16)
    parts = lax.all_to_all(partial, "tensor", split_axis=0, concat_axis=0, tiled=True)
    outbox, stream, logits = front(
        parts.reshape(ranks, rows, width),
        my_residual,
        norm_gain.reshape(1, width),
        router_weight.T,
        hits,
    )
    arrived = lax.all_to_all(outbox, "expert", split_axis=0, concat_axis=0, tiled=True)
    by_piece = rows_by_piece(arrived, swap)
    everyone = lax.all_gather(by_piece, "tensor", axis=0, tiled=False)
    hidden = up_rows(everyone, w_gate[0].T, w_up[0].T)
    my_hidden = lax.all_to_all(hidden, "tensor", split_axis=0, concat_axis=0, tiled=True)
    expert_out = down_rows(my_hidden, w_down_all, swap)
    returned = lax.all_to_all(expert_out, "expert", split_axis=0, concat_axis=0, tiled=True)
    packed = finish(returned, weights, stream, logits)
    gathered = lax.all_gather(packed, "tensor", axis=0, tiled=False)
    mixed = (
        gathered[:, : PIECES * rows]
        .reshape(ranks, PIECES, rows, piece)
        .transpose(0, 2, 1, 3)
        .reshape(group_rows, width)
    )
    tail = gathered[:, PIECES * rows :].astype(f32)
    logits_group = (tail[:, :, :expert_count] + tail[:, :, expert_count : 2 * expert_count]).reshape(
        group_rows, expert_count
    )
    return mixed, logits_group


def solution(mesh):
    in_specs = (
        P("expert", "tensor"),
        P("expert", None),
        P("tensor", None),
        P(),
        P(),
        P("expert", None),
        P("expert", None),
        P("expert", None, "tensor"),
        P("expert", None, "tensor"),
        P("expert", "tensor", None),
    )
    out_specs = (P("expert", None), P("expert", None))

    return jax.shard_map(shards, mesh=mesh, in_specs=in_specs, out_specs=out_specs, check_vma=False)
```

time: 633 us -> 333 us (0.53)
  blocking collectives: 298 us -> 0 us
  local copies, waits for them, and re-layouts: 66.9 us -> 9.66 us
  waiting for transfers between devices: 196 us -> 240 us
  matrix products: 41.5 us -> 4.03 us
  Pallas kernels: 0 us -> 28 us
  starting transfers between devices: 9.91 us -> 30.8 us
    all_to_all x1 -> x0, blocking collectives: 281 us -> none  [shards(): lax.all_to_all(outbox, 'expert', split_axis=1, concat_axis=1, tiled=True)]
    all_gather x1 -> x3, waiting for transfers between devices: 7.43 us -> 155 us  [the longest x1 67 us: shards(): everyone = lax.all_gather(by_piece, 'tensor', axis=0, tiled=False)]
    reduce_scatter x1 -> x0, waiting for transfers between devices: 75.8 us -> none  [shards(): lax.psum_scatter(jnp.dot(hidden, w_down[0], preferred_element_type=jnp.fl...]
    psum x1 -> x0, waiting for transfers between devices: 66.2 us -> none  [shards(): lax.psum(jnp.dot(attn_out, o_weight, preferred_element_type=jnp.float32)....]
    all_to_all x0 -> x3, waiting for transfers between devices: none -> 48.2 us  [the longest x1 35.5 us: shards(): lax.all_to_all(outbox, 'expert', split_axis=0, concat_axis=0, tiled=True)]
    dot_general x6 -> x1, matrix products: 41.5 us -> 4.03 us  [shards(): jnp.dot(attn_out, o_weight, preferred_element_type=f32).astype(bf16)]
    pallas_call x0 -> x5, Pallas kernels: none -> 28 us  [the longest x1 11.7 us: up_rows(): pl.pallas_call(up_kernel, grid=(ranks,), in_specs=[pl.BlockSpec((1, piece...]
    reshape x3 -> x1, local copies, waits for them, and re-layouts: 24.8 us -> 0.61 us  [shards(): mixed = gathered[:, :PIECES * rows].reshape(ranks, PIECES, rows, piece).t...]
  transfers between devices with their start and end apart: 4 -> 7, of which waited for: 4 -> 6; matrix products, arithmetic and copies ran while one was open for 1% -> 2% of each run, Pallas kernels for 0% -> 4%
where the time goes in v1:
time: 333 us
  waiting for transfers between devices  240 us (72%)
  starting transfers between devices  30.8 us (9%)
  Pallas kernels  28 us (8%)
  between operations  14.2 us (4%)
  local copies, waits for them, and re-layouts  9.66 us (3%)
  other arithmetic  5.92 us (2%)
  matrix products  4.03 us (1%)
    all_gather x1, waiting for transfers between devices, shards(): everyone = lax.all_gather(by_piece, 'tensor', axis=0, tiled=False)  67 us
    all_gather x1, waiting for transfers between devices, shards(): w_down_all = lax.all_gather(w_down[0], 'tensor', axis=0, tiled=True)  63.5 us
    all_to_all x1, waiting for transfers between devices, shards(): lax.all_to_all(expert_out, 'expert', split_axis=0, concat_axis=0, tiled=T...  36 us
    all_to_all x1, waiting for transfers between devices, shards(): lax.all_to_all(outbox, 'expert', split_axis=0, concat_axis=0, tiled=True)  35.5 us
    all_gather x1, waiting for transfers between devices, shards(): gathered = lax.all_gather(packed, 'tensor', axis=0, tiled=False)  24.6 us
    all_to_all x1, waiting for transfers between devices, shards(): lax.all_to_all(partial, 'tensor', split_axis=0, concat_axis=0, tiled=True)  12.7 us
    pallas_call x1, Pallas kernels, up_rows(): pl.pallas_call(up_kernel, grid=(ranks,), in_specs=[pl.BlockSpec((1, piece...  11.7 us
    all_to_all x1, starting transfers between devices, shards(): lax.all_to_all(outbox, 'expert', split_axis=0, concat_axis=0, tiled=True)  10.3 us
  transfers between devices with their start and end apart: 7, of which 6 were waited for; matrix products, arithmetic and copies ran while one was open for 2% of the time, Pallas kernels for 4%

profile of v1, /device:TPU:1, one launch (start us, length us, event | category | flops | bytes accessed | tf_op | source)
XLA Modules:
  0.0 332.6 jit_solution(6174685137040049520)
XLA Ops:
  7.2 4.0 %convolution_convert_fusion = bf16[128,4096]{1,0:T(8,128)(2,1)} fusion(bf16[128,512]{1,0:T(8,128)(2,1)} %param.10, bf16[512,4096]{1,0:T(8,128)(2,1)} %param.12), kind=kOutput, calls=%fused_computation | convolution fusion | flops 537395200 | bytes 5373952 | tf_op jit(solution)/shard_map/dot_general | solution.py:247
  11.2 6.8 %all-to-all-start = ((bf16[8,16,4096]{2,1,0:T(8,128)(2,1)}), bf16[8,16,4096]{2,1,0:T(8,128)(2,1)S(1)}, u32[]{:S(2)}, u32[]{:S(2)}) async-start(bf16[8,16,4096]{2,1,0:T(8,128)(2,1)} %bitcast.72), calls=%async_computation | async-start | bytes 2097152 | tf_op jit(solution)/shard_map/all_to_all | solution.py:248
  19.3 1.0 or_convert_fusion.hits
  20.4 12.7 %all-to-all-done.parts = bf16[8,16,4096]{2,1,0:T(8,128)(2,1)S(1)} async-done(((bf16[8,16,4096]{2,1,0:T(8,128)(2,1)}), bf16[8,16,4096]{2,1,0:T(8,128)(2,1)S(1)}, u32[]{:S(2)}, u32[]{:S(2)}) %all-to-all-start) | async-done | bytes 1048608 | tf_op jit(solution)/shard_map/all_to_all | solution.py:248
  33.9 1.2 copy-done.3
  35.2 10.3 %all-to-all-start.1 = ((bf16[32,48,512]{2,1,0:T(8,128)(2,1)}), bf16[32,48,512]{2,1,0:T(8,128)(2,1)S(1)}, u32[]{:S(2)}, u32[]{:S(2)}) async-start(bf16[32,48,512]{2,1,0:T(8,128)(2,1)} %bitcast.62), calls=%async_computation.1 | async-start | bytes 3145728 | tf_op jit(solution)/shard_map/all_to_all | solution.py:256
  45.7 1.8 fusion.18.swap
  47.4 35.5 %all-to-all-done.1 = bf16[32,48,512]{2,1,0:T(8,128)(2,1)S(1)} async-done(((bf16[32,48,512]{2,1,0:T(8,128)(2,1)}), bf16[32,48,512]{2,1,0:T(8,128)(2,1)S(1)}, u32[]{:S(2)}, u32[]{:S(2)}) %all-to-all-start.1) | async-done | bytes 1572896 | tf_op jit(solution)/shard_map/all_to_all | solution.py:256
  83.0 1.2 copy-done.8
  84.1 4.4 %rows_by_piece.1 = bf16[8,192,512]{2,1,0:T(8,128)(2,1)} custom-call(bf16[1536,512]{1,0:T(8,128)(2,1)} %bitcast.69, bf16[384,384]{1,0:T(8,128)(2,1)} %fusion.18.swap), custom_call_target="tpu_custom_call" | custom-call | tf_op jit(solution)/shard_map/rows_by_piece/pallas_call | solution.py:83
  89.3 67.0 %all-gather.7.cloned.1.call-done = bf16[64,192,512]{2,1,0:T(8,128)(2,1)} async-done(((bf16[8,192,512]{2,1,0:T(8,128)(2,1)}), bf16[64,192,512]{2,1,0:T(8,128)(2,1)}) %all-gather.7.cloned.1.call-update) | async-done | bytes 12582928 | tf_op jit(solution)/shard_map/all_gather | solution.py:258
  156.3 1.4 copy-done.5
  157.7 11.7 %up_rows.1 = bf16[8,192,192]{2,1,0:T(8,128)(2,1)} custom-call(bf16[8,8,192,512]{3,2,1,0:T(8,128)(2,1)} %bitcast.67, bf16[192,4096]{1,0:T(8,128)(2,1)S(1)} %bitcast.63, bf16[192,4096]{1,0:T(8,128)(2,1)S(1)} %bitcast.64), custom_call_target="tpu_custom_call" | custom-call | tf_op jit(solution)/shard_map/up_rows/pallas_call | solution.py:115
  169.5 3.9 %all-to-all-start.2 = ((bf16[8,192,192]{2,1,0:T(8,128)(2,1)}), bf16[8,192,192]{2,1,0:T(8,128)(2,1)S(1)}, u32[]{:S(2)}, u32[]{:S(2)}) async-start(bf16[8,192,192]{2,1,0:T(8,128)(2,1)} %up_rows.1), calls=%async_computation.2 | async-start | bytes 1572864 | tf_op jit(solution)/shard_map/all_to_all | solution.py:260
  173.3 63.5 %all-gather.9.cloned.1.call-done = bf16[1,1536,4096]{2,1,0:T(8,128)(2,1)} async-done(((bf16[1,192,4096]{2,1,0:T(8,128)(2,1)}), bf16[1,1536,4096]{2,1,0:T(8,128)(2,1)}) %all-gather.9.cloned.1.call-update) | async-done | bytes 12582928 | tf_op jit(solution)/shard_map/all_gather | solution.py:240
  236.8 9.8 %down_rows.1 = bf16[1536,512]{1,0:T(8,128)(2,1)S(1)} custom-call(bf16[8,192,192]{2,1,0:T(8,128)(2,1)S(1)} %all-to-all-done.2.hidden, bf16[1536,4096]{1,0:T(8,128)(2,1)} %bitcast.68, bf16[384,384]{1,0:T(8,128)(2,1)S(1)} %copy-done.2), custom_call_target="tpu_custom_call" | custom-call | tf_op jit(solution)/shard_map/down_rows/pallas_call | solution.py:156
  246.7 1.2 copy-done.1
  247.8 9.7 %all-to-all-start.3 = ((bf16[32,48,512]{2,1,0:T(8,128)(2,1)}), bf16[32,48,512]{2,1,0:T(8,128)(2,1)S(1)}, u32[]{:S(2)}, u32[]{:S(2)}) async-start(bf16[32,48,512]{2,1,0:T(8,128)(2,1)} %bitcast.61), calls=%async_computation.3 | async-start | bytes 3145728 | tf_op jit(solution)/shard_map/all_to_all | solution.py:262
  257.7 1.5 select_add_fusion.weights
  259.3 36.0 %all-to-all-done.3 = bf16[32,48,512]{2,1,0:T(8,128)(2,1)S(1)} async-done(((bf16[32,48,512]{2,1,0:T(8,128)(2,1)}), bf16[32,48,512]{2,1,0:T(8,128)(2,1)S(1)}, u32[]{:S(2)}, u32[]{:S(2)}) %all-to-all-start.3) | async-done | bytes 1572896 | tf_op jit(solution)/shard_map/all_to_all | solution.py:262
  295.2 1.3 finish.1
  296.5 24.6 %all-gather.11.cloned.1.call-done = bf16[1152,512]{1,0:T(8,128)(2,1)} async-done(((bf16[144,512]{1,0:T(8,128)(2,1)}), bf16[1152,512]{1,0:T(8,128)(2,1)}) %all-gather.11.cloned.1.call-update) | async-done | bytes 1179664 | tf_op jit(solution)/shard_map/all_gather | solution.py:264
  321.1 1.3 slice.80
  324.0 1.4 copy.25
  (97 shorter events, 5.4 us)
Async XLA Ops:
  11.2 21.8 %copy-start.6 = (bf16[4096,32]{0,1:T(8,128)(2,1)S(1)}, bf16[4096,32]{0,1:T(8,128)(2,1)}, u32[]{:S(2)}) copy-start(bf16[4096,32]{0,1:T(8,128)(2,1)} %param.14) | copy-start | bytes 786436
  11.2 21.8 %copy-start.7 = (f32[4096]{0:T(1024)S(1)}, f32[4096]{0:T(1024)}, u32[]{:S(2)}) copy-start(f32[4096]{0:T(1024)} %param.13) | copy-start | bytes 49156
  11.2 21.8 %all-to-all-start = ((bf16[8,16,4096]{2,1,0:T(8,128)(2,1)}), bf16[8,16,4096]{2,1,0:T(8,128)(2,1)S(1)}, u32[]{:S(2)}, u32[]{:S(2)}) async-start(bf16[8,16,4096]{2,1,0:T(8,128)(2,1)} %bitcast.72), calls=%async_computation | async-start | bytes 2097152 | tf_op jit(solution)/shard_map/all_to_all | solution.py:248
  18.0 17.0 %copy-start.10 = (s32[1536]{0:T(1024)}, s32[1536]{0:T(1024)S(1)}, u32[]{:S(2)}) copy-start(s32[1536]{0:T(1024)S(1)} %get-tuple-element.30) | copy-start | bytes 18436
  18.0 17.0 %copy-start.11 = (s32[1536]{0:T(1024)}, s32[1536]{0:T(1024)S(1)}, u32[]{:S(2)}) copy-start(s32[1536]{0:T(1024)S(1)} %get-tuple-element.31) | copy-start | bytes 18436
  18.1 17.0 %copy-start.12 = (s32[1536]{0:T(1024)}, s32[1536]{0:T(1024)S(1)}, u32[]{:S(2)}) copy-start(s32[1536]{0:T(1024)S(1)} %get-tuple-element.32) | copy-start | bytes 18436
  18.1 17.0 %copy-start.13 = (s32[1536]{0:T(1024)}, s32[1536]{0:T(1024)S(1)}, u32[]{:S(2)}) copy-start(s32[1536]{0:T(1024)S(1)} %get-tuple-element.33) | copy-start | bytes 18436
  18.1 17.0 %copy-start.14 = (pred[1536]{0:T(1024)(128)(4,1)}, pred[1536]{0:T(1024)(128)(4,1)S(1)}, u32[]{:S(2)}) copy-start(pred[1536]{0:T(1024)(128)(4,1)S(1)} %get-tuple-element.34) | copy-start | bytes 4612
  18.1 17.0 %copy-start.15 = (pred[1536]{0:T(1024)(128)(4,1)}, pred[1536]{0:T(1024)(128)(4,1)S(1)}, u32[]{:S(2)}) copy-start(pred[1536]{0:T(1024)(128)(4,1)S(1)} %get-tuple-element.35) | copy-start | bytes 4612
  18.1 17.0 %copy-start.27 = (s32[128]{0:T(128)}, s32[128]{0:T(128)S(1)}, u32[]{:S(2)}) copy-start(s32[128]{0:T(128)S(1)} %get-tuple-element.36) | copy-start | bytes 1540
  18.1 17.0 %copy-start.28 = (s32[128]{0:T(128)}, s32[128]{0:T(128)S(1)}, u32[]{:S(2)}) copy-start(s32[128]{0:T(128)S(1)} %get-tuple-element.37) | copy-start | bytes 1540
  18.2 16.9 %copy-start.16 = (pred[1536]{0:T(1024)(128)(4,1)}, pred[1536]{0:T(1024)(128)(4,1)S(1)}, u32[]{:S(2)}) copy-start(pred[1536]{0:T(1024)(128)(4,1)S(1)} %fusion.30) | copy-start | bytes 4612
  18.2 16.9 %copy-start.29 = (pred[128]{0:T(512)(128)(4,1)}, pred[128]{0:T(512)(128)(4,1)S(1)}, u32[]{:S(2)}) copy-start(pred[128]{0:T(512)(128)(4,1)S(1)} %compare_and_fusion) | copy-start | bytes 388
  19.2 15.9 %copy-start.17 = (s32[128]{0:T(128)}, s32[128]{0:T(128)S(1)}, u32[]{:S(2)}) copy-start(s32[128]{0:T(128)S(1)} %get-tuple-element.20) | copy-start | bytes 1540
  19.2 15.9 %copy-start.18 = (s32[128]{0:T(128)}, s32[128]{0:T(128)S(1)}, u32[]{:S(2)}) copy-start(s32[128]{0:T(128)S(1)} %get-tuple-element.21) | copy-start | bytes 1540
  19.2 15.9 %copy-start.19 = (s32[128]{0:T(128)}, s32[128]{0:T(128)S(1)}, u32[]{:S(2)}) copy-start(s32[128]{0:T(128)S(1)} %get-tuple-element.22) | copy-start | bytes 1540
  35.2 47.7 %all-to-all-start.1 = ((bf16[32,48,512]{2,1,0:T(8,128)(2,1)}), bf16[32,48,512]{2,1,0:T(8,128)(2,1)S(1)}, u32[]{:S(2)}, u32[]{:S(2)}) async-start(bf16[32,48,512]{2,1,0:T(8,128)(2,1)} %bitcast.62), calls=%async_computation.1 | async-start | bytes 3145728 | tf_op jit(solution)/shard_map/all_to_all | solution.py:256
  45.5 110.8 %all-gather.7.cloned.1.call-start = ((), (), s32[]{:S(2)}) async-start(), calls=%async_computation.4 | async-start | bytes 14155776 | tf_op jit(solution)/shard_map/all_gather | solution.py:258
  88.5 67.8 %copy-start.4 = (bf16[1,4096,192]{1,2,0:T(8,128)(2,1)S(1)}, bf16[1,4096,192]{1,2,0:T(8,128)(2,1)}, u32[]{:S(2)}) copy-start(bf16[1,4096,192]{1,2,0:T(8,128)(2,1)} %param.17) | copy-start | bytes 4718596
  88.5 148.3 %all-gather.9.cloned.1.call-start = ((), (), s32[]{:S(2)}) async-start(), calls=%async_computation.5 | async-start | bytes 14155776 | tf_op jit(solution)/shard_map/all_gather | solution.py:240
  169.5 67.4 %copy-start.2 = (bf16[384,384]{1,0:T(8,128)(2,1)S(1)}, bf16[384,384]{1,0:T(8,128)(2,1)}, u32[]{:S(2)}) copy-start(bf16[384,384]{1,0:T(8,128)(2,1)} %fusion.18.swap) | copy-start | bytes 884740
  169.5 67.4 %all-to-all-start.2 = ((bf16[8,192,192]{2,1,0:T(8,128)(2,1)}), bf16[8,192,192]{2,1,0:T(8,128)(2,1)S(1)}, u32[]{:S(2)}, u32[]{:S(2)}) async-start(bf16[8,192,192]{2,1,0:T(8,128)(2,1)} %up_rows.1), calls=%async_computation.2 | async-start | bytes 1572864 | tf_op jit(solution)/shard_map/all_to_all | solution.py:260
  247.8 47.4 %all-to-all-start.3 = ((bf16[32,48,512]{2,1,0:T(8,128)(2,1)}), bf16[32,48,512]{2,1,0:T(8,128)(2,1)S(1)}, u32[]{:S(2)}, u32[]{:S(2)}) async-start(bf16[32,48,512]{2,1,0:T(8,128)(2,1)} %bitcast.61), calls=%async_computation.3 | async-start | bytes 3145728 | tf_op jit(solution)/shard_map/all_to_all | solution.py:262
  257.5 63.6 %all-gather.11.cloned.1.call-start = ((), (), s32[]{:S(2)}) async-start(), calls=%async_computation.6 | async-start | bytes 1327104 | tf_op jit(solution)/shard_map/all_gather | solution.py:264
  (13 other events, 128.4 us)
Sparse Core Ops, SparseCore 0:
  88.7 67.5 all-gather.6
  158.1 78.6 all-gather.8
  296.6 24.4 all-gather.10

commit v2 on v1

v2 whole, which is shorter than its diff:
```python
import jax
import jax.numpy as jnp
from jax import lax
from jax.experimental import pallas as pl
from jax.experimental.pallas import tpu as pltpu
from jax.sharding import PartitionSpec as P


epsilon = 1e-06
PIECES = 8
HALVES = 2
CHIPS = 4
BATCH = 16
f32 = jnp.float32
bf16 = jnp.bfloat16
roomy = pltpu.CompilerParams(vmem_limit_bytes=44 * 2**20)


def slot_targets(chosen, expert_count, capacity):
    flat_ids = chosen.reshape(-1)
    one_hot = (flat_ids[:, None] == jnp.arange(expert_count, dtype=jnp.int32)[None, :]).astype(
        jnp.int32
    )
    slot_index = jnp.sum((jnp.cumsum(one_hot, axis=0) - 1) * one_hot, axis=1)
    return (flat_ids * capacity + slot_index).reshape(chosen.shape)


def reorder_matrix(outer, inner, run):
    size = outer * inner * run
    row = lax.broadcasted_iota(jnp.int32, (size, size), 0)
    col = lax.broadcasted_iota(jnp.int32, (size, size), 1)
    a = row // (inner * run)
    b = row % (inner * run) // run
    return (col == b * (outer * run) + a * run + row % run).astype(bf16)


def pieces_to_rows(x):
    width = x.shape[1] // PIECES
    return jnp.concatenate([x[:, j * width : (j + 1) * width] for j in range(PIECES)], axis=0)


def dot_last(a, b):
    return lax.dot_general(a, b, (((1,), (1,)), ((), ())), preferred_element_type=f32)


def dot_first(a, b):
    return lax.dot_general(a, b, (((0,), (0,)), ((), ())), preferred_element_type=f32)


def along(x, shift):
    pairs = [
        (2 * chip + core, 2 * ((chip + shift) % CHIPS) + core)
        for chip in range(CHIPS)
        for core in range(2)
    ]
    return lax.ppermute(x, "tensor", pairs)


def across(x):
    return lax.ppermute(x, "tensor", [(r, r ^ 1) for r in range(2 * CHIPS)])


def project_kernel(place, attn, weight, mine, theirs):
    rows = mine.shape[1]
    chip, core = place[0], place[1]

    def block(shift, other):
        rank = 2 * ((chip + shift) % CHIPS) + (core + other) % 2
        return attn[pl.ds(pl.multiple_of(rank * rows, rows), rows), :]

    ordered = [block(shift, other) for other in range(2) for shift in range(CHIPS)]
    total = jnp.dot(
        jnp.concatenate(ordered, axis=0), weight[...], preferred_element_type=f32
    ).astype(bf16)
    for i in range(CHIPS):
        mine[i] = total[i * rows : (i + 1) * rows, :]
        theirs[i] = total[(CHIPS + i) * rows : (CHIPS + i + 1) * rows, :]


def project(place, attn, weight):
    depth, width = weight.shape
    rows = attn.shape[0] // (2 * CHIPS)
    step = width // 4
    out = jax.ShapeDtypeStruct((CHIPS, rows, width), bf16)
    return pl.pallas_call(
        project_kernel,
        grid_spec=pltpu.PrefetchScalarGridSpec(
            num_scalar_prefetch=1,
            grid=(4,),
            in_specs=[
                pl.BlockSpec(attn.shape, lambda n, place: (0, 0)),
                pl.BlockSpec((depth, step), lambda n, place: (0, n)),
            ],
            out_specs=[pl.BlockSpec((CHIPS, rows, step), lambda n, place: (0, 0, n))] * 2,
        ),
        out_shape=(out, out),
        compiler_params=roomy,
        name="project",
    )(place, attn, weight)


def pair_kernel(mine, other, *outs):
    for i in range(CHIPS):
        outs[i][...] = (mine[i].astype(f32) + other[i].astype(f32)).astype(bf16)


def pair_sums(mine, other):
    out = jax.ShapeDtypeStruct(mine.shape[1:], bf16)
    return pl.pallas_call(
        pair_kernel, out_shape=(out,) * CHIPS, compiler_params=roomy, name="pair_sums"
    )(mine, other)


def front_kernel(place, p0, p1, p2, p3, residual, gain, router, shares0, shares1, *outs):
    outbox0, outbox1, stream_out, logits_out = outs
    rows = p0.shape[0]
    start = (2 * place[0] + place[1]) * rows
    total = (p0[...].astype(f32) + p1[...].astype(f32)) + (
        p2[...].astype(f32) + p3[...].astype(f32)
    )
    mine = residual[pl.ds(pl.multiple_of(start, rows), rows), :]
    stream = (mine.astype(f32) + total).astype(bf16)
    wide = stream.astype(f32)
    scale = lax.rsqrt(jnp.mean(wide * wide, axis=-1, keepdims=True) + epsilon)
    normed = (wide * scale * gain[...]).astype(bf16)
    stream_out[...] = pieces_to_rows(stream)
    logits_out[...] = dot_last(normed, router[...])
    by_piece = pieces_to_rows(normed)
    for shares, outbox in ((shares0, outbox0), (shares1, outbox1)):
        hits = (shares[...] != 0.0).astype(bf16)
        outbox[...] = dot_first(hits, by_piece).astype(bf16)


def front(place, parts, residual, gain, router, shares):
    rows, width = parts[0].shape
    piece = width // PIECES
    whole = pl.BlockSpec(memory_space=pltpu.VMEM)
    outbox = jax.ShapeDtypeStruct((shares[0].shape[1], piece), bf16)
    return pl.pallas_call(
        front_kernel,
        in_specs=[pl.BlockSpec(memory_space=pltpu.SMEM)] + [whole] * 9,
        out_shape=(
            outbox,
            outbox,
            jax.ShapeDtypeStruct((rows * PIECES, piece), bf16),
            jax.ShapeDtypeStruct((rows, router.shape[0]), f32),
        ),
        compiler_params=roomy,
        name="front",
    )(place, *parts, residual, gain, router, *shares)


def by_piece_kernel(x, order, low, high):
    moved = jnp.dot(order[...], x[...], preferred_element_type=f32)
    moved = moved.reshape((PIECES,) + low.shape[1:]).astype(bf16)
    low[...] = moved[: PIECES // 2]
    high[...] = moved[PIECES // 2 :]


def rows_by_piece(x, order):
    size = order.shape[0]
    steps = x.shape[0] // size
    width = x.shape[1]
    run = size // PIECES
    out = jax.ShapeDtypeStruct((PIECES // 2, run * steps, width), bf16)
    return pl.pallas_call(
        by_piece_kernel,
        grid=(steps,),
        in_specs=[
            pl.BlockSpec((size, width), lambda a: (a, 0)),
            pl.BlockSpec((size, size), lambda a: (0, 0)),
        ],
        out_specs=[pl.BlockSpec((PIECES // 2, run, width), lambda a: (0, a, 0))] * 2,
        out_shape=(out, out),
        name="rows_by_piece",
    )(x, order)


def up_kernel(*refs):
    lows, highs = refs[:CHIPS], refs[CHIPS : 2 * CHIPS]
    gate_own, gate_other, up_own, up_other = refs[2 * CHIPS : 2 * CHIPS + 4]
    outs = refs[2 * CHIPS + 5 : 3 * CHIPS + 5]
    gate, up = refs[3 * CHIPS + 5 :]
    j = pl.program_id(0)

    @pl.when(j == 0)
    def _():
        gate[...] = jnp.zeros_like(gate)
        up[...] = jnp.zeros_like(up)

    x = jnp.concatenate(
        [jnp.where(j < PIECES // 2, low[0], high[0]) for low, high in zip(lows, highs)], axis=0
    )
    gate[...] += dot_last(x, jnp.concatenate([gate_own[...], gate_other[...]], axis=0))
    up[...] += dot_last(x, jnp.concatenate([up_own[...], up_other[...]], axis=0))

    @pl.when(j == PIECES - 1)
    def _():
        g = gate[...]
        hidden = (g / (1.0 + jnp.exp(-g)) * up[...]).astype(bf16)
        rows = outs[0].shape[0]
        for i in range(CHIPS):
            outs[i][...] = hidden[i * rows : (i + 1) * rows, :]


def up_rows(lows, highs, weights, after):
    _, rows, width = lows[0].shape
    units = weights[0].shape[0]
    out = jax.ShapeDtypeStruct((rows, 2 * units), bf16)
    return pl.pallas_call(
        up_kernel,
        grid=(PIECES,),
        in_specs=[
            pl.BlockSpec((1, rows, width), lambda j: (jnp.minimum(j, PIECES // 2 - 1), 0, 0))
        ]
        * CHIPS
        + [pl.BlockSpec((1, rows, width), lambda j: (jnp.maximum(j - PIECES // 2, 0), 0, 0))]
        * CHIPS
        + [pl.BlockSpec((units, width), lambda j: (0, j))] * 4
        + [pl.BlockSpec(memory_space=pl.ANY)],
        out_specs=[pl.BlockSpec((rows, 2 * units), lambda j: (0, 0))] * CHIPS,
        out_shape=(out,) * CHIPS,
        scratch_shapes=[pltpu.VMEM((CHIPS * rows, 2 * units), f32)] * 2,
        compiler_params=roomy,
        name="up_rows",
    )(*lows, *highs, *weights, after)


def down_kernel(place, h0, h1, h2, h3, w_down, order, out, held):
    j = pl.program_id(0)
    chip, core = place[0], place[1]
    total = None
    for i, hidden in enumerate((h0, h1, h2, h3)):
        first = 2 * ((chip + i) % CHIPS)
        weight = jnp.concatenate([w_down[first + core], w_down[first + (core + 1) % 2]], axis=0)
        part = jnp.dot(hidden[...], weight, preferred_element_type=f32)
        total = part if total is None else total + part
    held[j] = total.astype(bf16)

    @pl.when(j == PIECES - 1)
    def _():
        size = order.shape[0]
        run = size // PIECES
        for a in range(held.shape[1] // run):
            block = held[:, a * run : (a + 1) * run, :].reshape(size, held.shape[2])
            out[a * size : (a + 1) * size, :] = dot_first(order[...], block).astype(bf16)


def down_rows(place, hidden, w_down, order):
    rows, units = hidden[0].shape
    ranks, depth, width = w_down.shape
    piece = width // PIECES
    return pl.pallas_call(
        down_kernel,
        grid_spec=pltpu.PrefetchScalarGridSpec(
            num_scalar_prefetch=1,
            grid=(PIECES,),
            in_specs=[pl.BlockSpec((rows, units), lambda j, place: (0, 0))] * CHIPS
            + [
                pl.BlockSpec((ranks, depth, piece), lambda j, place: (0, 0, j)),
                pl.BlockSpec(order.shape, lambda j, place: (0, 0)),
            ],
            out_specs=pl.BlockSpec((rows * PIECES, piece), lambda j, place: (0, 0)),
            scratch_shapes=[pltpu.VMEM((PIECES, rows, piece), bf16)],
        ),
        out_shape=jax.ShapeDtypeStruct((rows * PIECES, piece), bf16),
        compiler_params=roomy,
        name="down_rows",
    )(place, *hidden, w_down, order)


def finish_kernel(back0, back1, weights0, weights1, stream, logits, out):
    moe = stream[...].astype(f32)
    for back, weights in ((back0, weights0), (back1, weights1)):
        high = weights[...].astype(bf16)
        low = (weights[...] - high.astype(f32)).astype(bf16)
        moe = moe + (
            jnp.dot(high, back[...], preferred_element_type=f32)
            + jnp.dot(low, back[...], preferred_element_type=f32)
        )
    rows = stream.shape[0]
    out[0:rows, :] = moe.astype(bf16)
    logit_high = logits[...].astype(bf16)
    logit_low = (logits[...] - logit_high.astype(f32)).astype(bf16)
    filler = jnp.zeros((logits.shape[0], out.shape[1] - 2 * logits.shape[1]), bf16)
    out[rows:, :] = jnp.concatenate([logit_high, logit_low, filler], axis=1)


def finish(returned, weights, stream, logits):
    return pl.pallas_call(
        finish_kernel,
        out_shape=jax.ShapeDtypeStruct(
            (stream.shape[0] + logits.shape[0], stream.shape[1]), bf16
        ),
        compiler_params=roomy,
        name="finish",
    )(*returned, *weights, stream, logits)


def assemble_kernel(place, same_core, other_core, mixed, logits):
    rows = mixed.shape[0] // (2 * CHIPS)
    piece = same_core.shape[2]
    count = logits.shape[1]
    for other, blocks in enumerate((same_core, other_core)):
        for shift in range(CHIPS):
            rank = 2 * ((place[0] + CHIPS - shift) % CHIPS) + (place[1] + other) % 2
            at = pl.ds(pl.multiple_of(rank * rows, rows), rows)
            for j in range(PIECES):
                mixed[at, j * piece : (j + 1) * piece] = blocks[
                    shift, j * rows : (j + 1) * rows, :
                ]
            tail = blocks[shift, PIECES * rows :, :].astype(f32)
            logits[at, :] = tail[:, :count] + tail[:, count : 2 * count]


def assemble(place, same_core, other_core, expert_count):
    rows = same_core.shape[1] // (PIECES + 1)
    width = same_core.shape[2] * PIECES
    whole = pl.BlockSpec(memory_space=pltpu.VMEM)
    return pl.pallas_call(
        assemble_kernel,
        in_specs=[pl.BlockSpec(memory_space=pltpu.SMEM), whole, whole],
        out_shape=(
            jax.ShapeDtypeStruct((rows * 2 * CHIPS, width), bf16),
            jax.ShapeDtypeStruct((rows * 2 * CHIPS, expert_count), f32),
        ),
        compiler_params=roomy,
        name="assemble",
    )(place, same_core, other_core)


def routing(chosen, combine, expert_count, capacity):
    targets = slot_targets(chosen, expert_count, capacity)
    tokens = chosen.shape[0]
    slots = capacity // HALVES
    run = PIECES * slots
    total = expert_count * run
    row = lax.broadcasted_iota(jnp.int32, (PIECES * tokens, total), 0)
    col = lax.broadcasted_iota(jnp.int32, (PIECES * tokens, total), 1)
    same_piece = row // tokens == (col % run) // slots
    targets = jnp.tile(targets, (PIECES, 1))
    combine = jnp.tile(combine, (PIECES, 1))
    results = []
    for half in range(HALVES):
        slot_of = col // run * capacity + half * slots + col % slots
        wanted = jnp.where(same_piece, slot_of, -1)
        weights = jnp.zeros((PIECES * tokens, total), f32)
        for k in range(chosen.shape[1]):
            weights = jnp.where(wanted == targets[:, k : k + 1], combine[:, k : k + 1], weights)
        results.append(weights)
    return results


def shards(
    attn_out,
    residual,
    o_weight,
    norm_gain,
    router_weight,
    expert_idx,
    combine,
    w_gate,
    w_up,
    w_down,
):
    ranks = lax.axis_size("tensor")
    rank = lax.axis_index("tensor")
    place = jnp.stack([rank // 2, rank % 2]).astype(jnp.int32)
    group_rows, width = residual.shape
    rows = group_rows // ranks
    expert_count = router_weight.shape[1]
    top_count = expert_idx.shape[1]
    capacity = min(rows, max(2, 3 * rows * top_count // (2 * expert_count)))
    slots = capacity // HALVES

    w_down_all = lax.all_gather(w_down[0], "tensor", axis=0, tiled=False)
    gate_own, up_own = w_gate[0].T, w_up[0].T
    weights = (gate_own, across(gate_own), up_own, across(up_own))
    order = reorder_matrix(PIECES, BATCH, slots)
    chosen = lax.dynamic_slice_in_dim(expert_idx, rank * rows, rows, 0)
    my_combine = lax.dynamic_slice_in_dim(combine, rank * rows, rows, 0)
    shares = routing(chosen, my_combine, expert_count, capacity)

    mine, theirs = project(place, attn_out, o_weight)
    sums = pair_sums(mine, across(theirs))
    parts = (sums[0],) + tuple(along(sums[shift], shift) for shift in range(1, CHIPS))
    outbox0, outbox1, stream, logits = front(
        place, parts, residual, norm_gain.reshape(1, width), router_weight.T, shares
    )
    arrived = []
    for outbox in (outbox0, outbox1):
        arrived.append(lax.all_to_all(outbox, "expert", split_axis=0, concat_axis=0, tiled=True))
    own = [rows_by_piece(x, order) for x in arrived]
    returned = []
    for half, (low, high) in enumerate(own):
        low_up, high_down = along(low, 1), along(high, -1)
        high_up, low_down = along(high, 1), along(low, -1)
        low_far, high_far = along(low_up, 1), along(high_down, -1)
        hidden = up_rows(
            (low, low_up, low_far, low_down),
            (high, high_up, high_far, high_down),
            weights,
            own[1][0] if half == 0 else own[0][0],
        )
        units = (hidden[0],) + tuple(along(hidden[s], -s) for s in range(1, CHIPS))
        expert_out = down_rows(place, units, w_down_all, order)
        returned.append(
            lax.all_to_all(expert_out, "expert", split_axis=0, concat_axis=0, tiled=True)
        )
    packed = finish(returned, shares, stream, logits)
    same_core = jnp.stack([packed] + [along(packed, shift) for shift in range(1, CHIPS)])
    return assemble(place, same_core, across(same_core), expert_count)


def solution(mesh):
    in_specs = (
        P("expert", "tensor"),
        P("expert", None),
        P("tensor", None),
        P(),
        P(),
        P("expert", None),
        P("expert", None),
        P("expert", None, "tensor"),
        P("expert", None, "tensor"),
        P("expert", "tensor", None),
    )
    out_specs = (P("expert", None), P("expert", None))

    return jax.shard_map(shards, mesh=mesh, in_specs=in_specs, out_specs=out_specs, check_vma=False)
```

time: 333 us -> 258 us (0.77)
  waiting for transfers between devices: 240 us -> 81.8 us
  starting transfers between devices: 30.8 us -> 66.5 us
  blocking collectives: 0 us -> 24.1 us
  Pallas kernels: 28 us -> 46.5 us
  local copies, waits for them, and re-layouts: 9.66 us -> 19.8 us
  matrix products: 4.03 us -> 0 us
    all_gather x3 -> x1, waiting for transfers between devices: 155 us -> 0.01 us  [shards(): w_down_all = lax.all_gather(w_down[0], 'tensor', axis=0, tiled=False)]
    ppermute x0 -> x28, waiting for transfers between devices: none -> 61.7 us  [the longest x24 60 us: along(): return lax.ppermute(x, 'tensor', pairs)]
    ppermute x0 -> x28, starting transfers between devices: none -> 41.4 us  [the longest x24 26.1 us: along(): return lax.ppermute(x, 'tensor', pairs)]
    all_to_all x1, waiting for transfers between devices: 36 us -> 0.01 us  [shards(): lax.all_to_all(expert_out, 'expert', split_axis=0, concat_axis=0, tiled=T...]
    all_to_all x0 -> x1, blocking collectives: none -> 24.1 us  [shards(): lax.all_to_all(expert_out, 'expert', split_axis=0, concat_axis=0, tiled=T...]
    pallas_call x4 -> x10, Pallas kernels: 26.8 us -> 44.8 us  [the longest x2 18.6 us: down_rows(): pl.pallas_call(down_kernel, grid_spec=pltpu.PrefetchScalarGridSpec(num_sc...]
    all_to_all x1 -> x2, waiting for transfers between devices: 35.5 us -> 19.5 us  [shards(): lax.all_to_all(outbox, 'expert', split_axis=0, concat_axis=0, tiled=True)]
    all_to_all x2 -> x0, waiting for transfers between devices: 12.7 us -> none  [the longest x1 12.7 us: shards(): lax.all_to_all(partial, 'tensor', split_axis=0, concat_axis=0, tiled=True)]
  transfers between devices with their start and end apart: 7 -> 32, of which waited for: 6 -> 21; matrix products, arithmetic and copies ran while one was open for 2% -> 2% of each run, Pallas kernels for 4% -> 13%
where the time goes in v2:
time: 258 us; the launch traced here: 257 us
  waiting for transfers between devices  81.8 us (32%)
  starting transfers between devices  66.5 us (26%)
  Pallas kernels  46.5 us (18%)
  blocking collectives  24.1 us (9%)
  local copies, waits for them, and re-layouts  19.8 us (8%)
  between operations  14.4 us (6%)
  other arithmetic  3.31 us (1%)
    ppermute x24, waiting for transfers between devices, along(): return lax.ppermute(x, 'tensor', pairs)  60 us
    ppermute x24, starting transfers between devices, along(): return lax.ppermute(x, 'tensor', pairs)  26.1 us
    all_to_all x1, blocking collectives, shards(): lax.all_to_all(expert_out, 'expert', split_axis=0, concat_axis=0, tiled=T...  24.1 us
    all_to_all x2, waiting for transfers between devices, shards(): lax.all_to_all(outbox, 'expert', split_axis=0, concat_axis=0, tiled=True)  19.5 us
    pallas_call x2, Pallas kernels, down_rows(): pl.pallas_call(down_kernel, grid_spec=pltpu.PrefetchScalarGridSpec(num_sc...  18.6 us
    unnamed x67, local copies, waits for them, and re-layouts  18.5 us
    all_to_all x2, starting transfers between devices, shards(): lax.all_to_all(outbox, 'expert', split_axis=0, concat_axis=0, tiled=True)  16.3 us
    pallas_call x2, Pallas kernels, up_rows(): pl.pallas_call(up_kernel, grid=(PIECES,), in_specs=[pl.BlockSpec((1, rows...  15.7 us
  transfers between devices with their start and end apart: 32, of which 21 were waited for; matrix products, arithmetic and copies ran while one was open for 2% of the time, Pallas kernels for 13%

profile of v2, /device:TPU:1, one launch (start us, length us, event | category | flops | bytes accessed | tf_op | source)
XLA Modules:
  0.0 256.5 jit_solution(896278484312227114)
XLA Ops:
  12.5 3.3 %collective-permute-start = (bf16[4,16,4096]{2,1,0:T(8,128)(2,1)S(1)}, bf16[4,16,4096]{2,1,0:T(8,128)(2,1)S(1)}, u32[]{:S(2)}, u32[]{:S(2)}) collective-permute-start(bf16[4,16,4096]{2,1,0:T(8,128)(2,1)S(1)} %get-tuple-element.25), channel_id=1, source_target_pairs={{0,1},{1,0},{2,3},{3,2},{4,5},{5,4},{6,7},{7,6},{8,9},{9,8},{10,11... | collective-permute-start | bytes 1572872 | tf_op jit(solution)/shard_map/ppermute | solution.py:60
  21.4 2.8 %collective-permute-done.1.p1 = bf16[16,4096]{1,0:T(8,128)(2,1)S(1)} collective-permute-done((bf16[16,4096]{1,0:T(8,128)(2,1)S(1)}, bf16[16,4096]{1,0:T(8,128)(2,1)S(1)}, u32[]{:S(2)}, u32[]{:S(2)}) %collective-permute-start.1) | collective-permute-done | bytes 131104 | tf_op jit(solution)/shard_map/ppermute | solution.py:56
  32.0 10.4 %all-to-all-start.1 = ((bf16[32,24,512]{2,1,0:T(8,128)(2,1)}), bf16[32,24,512]{2,1,0:T(8,128)(2,1)}, u32[]{:S(2)}, u32[]{:S(2)}) async-start(bf16[32,24,512]{2,1,0:T(8,128)(2,1)} %bitcast.68), calls=%async_computation.1 | async-start | bytes 1572864 | tf_op jit(solution)/shard_map/all_to_all | solution.py:392
  44.0 19.5 %all-to-all-done.1 = bf16[32,24,512]{2,1,0:T(8,128)(2,1)} async-done(((bf16[32,24,512]{2,1,0:T(8,128)(2,1)}), bf16[32,24,512]{2,1,0:T(8,128)(2,1)}, u32[]{:S(2)}, u32[]{:S(2)}) %all-to-all-start.1) | async-done | bytes 786464 | tf_op jit(solution)/shard_map/all_to_all | solution.py:392
  63.5 5.9 %all-to-all-start = ((bf16[32,24,512]{2,1,0:T(8,128)(2,1)}), bf16[32,24,512]{2,1,0:T(8,128)(2,1)}, u32[]{:S(2)}, u32[]{:S(2)}) async-start(bf16[32,24,512]{2,1,0:T(8,128)(2,1)} %bitcast.67), calls=%async_computation | async-start | bytes 1572864 | tf_op jit(solution)/shard_map/all_to_all | solution.py:392
  71.3 2.6 %rows_by_piece.3 = (bf16[4,96,512]{2,1,0:T(8,128)(2,1)}, bf16[4,96,512]{2,1,0:T(8,128)(2,1)}) custom-call(bf16[768,512]{1,0:T(8,128)(2,1)} %bitcast.29.x, bf16[384,384]{1,0:T(8,128)(2,1)} %fusion.6.order), custom_call_target="tpu_custom_call" | custom-call | tf_op jit(solution)/shard_map/rows_by_piece/pallas_call | solution.py:166
  78.0 11.5 %collective-permute-done.15.refs_1_ = bf16[4,96,512]{2,1,0:T(8,128)(2,1)S(1)} collective-permute-done((bf16[4,96,512]{2,1,0:T(8,128)(2,1)}, bf16[4,96,512]{2,1,0:T(8,128)(2,1)S(1)}, u32[]{:S(2)}, u32[]{:S(2)}) %collective-permute-start.15) | collective-permute-done | bytes 393248 | tf_op jit(solution)/shard_map/ppermute | solution.py:56
  89.5 2.7 %collective-permute-start.20 = (bf16[4,96,512]{2,1,0:T(8,128)(2,1)}, bf16[4,96,512]{2,1,0:T(8,128)(2,1)}, u32[]{:S(2)}, u32[]{:S(2)}) collective-permute-start(bf16[4,96,512]{2,1,0:T(8,128)(2,1)} %collective-permute-done.19.refs_7_), channel_id=1, source_target_pairs={{0,6},{1,7},{2,0},{3,1},{4,2},{5,3},{6,4},{7,5},{8,14},{9,15},{10,... | collective-permute-start | bytes 1179656 | tf_op jit(solution)/shard_map/ppermute | solution.py:56
  92.2 2.6 %rows_by_piece.2 = (bf16[4,96,512]{2,1,0:T(8,128)(2,1)}, bf16[4,96,512]{2,1,0:T(8,128)(2,1)}) custom-call(bf16[768,512]{1,0:T(8,128)(2,1)} %bitcast.21.x, bf16[384,384]{1,0:T(8,128)(2,1)} %fusion.6.order), custom_call_target="tpu_custom_call" | custom-call | tf_op jit(solution)/shard_map/rows_by_piece/pallas_call | solution.py:166
  94.8 2.7 %collective-permute-done.17.refs_3_ = bf16[4,96,512]{2,1,0:T(8,128)(2,1)} collective-permute-done((bf16[4,96,512]{2,1,0:T(8,128)(2,1)}, bf16[4,96,512]{2,1,0:T(8,128)(2,1)}, u32[]{:S(2)}, u32[]{:S(2)}) %collective-permute-start.17) | collective-permute-done | bytes 393248 | tf_op jit(solution)/shard_map/ppermute | solution.py:56
  97.9 8.4 %collective-permute-done.16.refs_2_ = bf16[4,96,512]{2,1,0:T(8,128)(2,1)} collective-permute-done((bf16[4,96,512]{2,1,0:T(8,128)(2,1)S(1)}, bf16[4,96,512]{2,1,0:T(8,128)(2,1)}, u32[]{:S(2)}, u32[]{:S(2)}) %collective-permute-start.16) | collective-permute-done | bytes 393248 | tf_op jit(solution)/shard_map/ppermute | solution.py:56
  110.4 8.1 %up_rows.3 = (bf16[96,384]{1,0:T(8,128)(2,1)S(1)}, bf16[96,384]{1,0:T(8,128)(2,1)S(1)}, bf16[96,384]{1,0:T(8,128)(2,1)S(1)}, bf16[96,384]{1,0:T(8,128)(2,1)S(1)}) custom-call(bf16[4,96,512]{2,1,0:T(8,128)(2,1)S(1)} %copy-done.10, bf16[4,96,512]{2,1,0:T(8,128)(2,1)S(1)} %copy-done.20, bf16[4,96,512]{2,1,0:T(8,128)(2,1)} %collective-permute-done.16.refs_2_, ...), custom_call_target="tpu_custom_call" | custom-call | tf_op jit(solution)/shard_map/up_rows/pallas_call | solution.py:210
  129.7 9.3 %down_rows.3 = bf16[768,512]{1,0:T(8,128)(2,1)S(1)} custom-call(s32[2]{0:T(128)S(1)} %pad_add_fusion.place, bf16[96,384]{1,0:T(8,128)(2,1)S(1)} %get-tuple-element.40.h0, bf16[96,384]{1,0:T(8,128)(2,1)S(1)} %copy-done.26, bf16[96,384]{1,0:T(8,128)(2,1)S(1)} %copy-done.28, bf16[96,384]{1,0:T(8,128)(2,1)S(1)} %copy-done.30, ...), custom_call_target="tpu_custom_call" | custom-call | tf_op jit(solution)/shard_map/down_rows/pallas_call | solution.py:253
  139.9 8.7 %all-to-all-start.3 = ((bf16[32,24,512]{2,1,0:T(8,128)(2,1)}), bf16[32,24,512]{2,1,0:T(8,128)(2,1)}, u32[]{:S(2)}, u32[]{:S(2)}) async-start(bf16[32,24,512]{2,1,0:T(8,128)(2,1)} %bitcast.65), calls=%async_computation.3 | async-start | bytes 1572864 | tf_op jit(solution)/shard_map/all_to_all | solution.py:408
  152.8 4.7 %collective-permute-done.4.refs_1_ = bf16[4,96,512]{2,1,0:T(8,128)(2,1)S(1)} collective-permute-done((bf16[4,96,512]{2,1,0:T(8,128)(2,1)}, bf16[4,96,512]{2,1,0:T(8,128)(2,1)S(1)}, u32[]{:S(2)}, u32[]{:S(2)}) %collective-permute-start.4) | collective-permute-done | bytes 393248 | tf_op jit(solution)/shard_map/ppermute | solution.py:56
  157.5 2.7 %collective-permute-start.9 = (bf16[4,96,512]{2,1,0:T(8,128)(2,1)S(1)}, bf16[4,96,512]{2,1,0:T(8,128)(2,1)S(1)}, u32[]{:S(2)}, u32[]{:S(2)}) collective-permute-start(bf16[4,96,512]{2,1,0:T(8,128)(2,1)S(1)} %collective-permute-done.8.refs_7_), channel_id=1, source_target_pairs={{0,6},{1,7},{2,0},{3,1},{4,2},{5,3},{6,4},{7,5},{8,14},{9,15},{10,... | collective-permute-start | bytes 1179656 | tf_op jit(solution)/shard_map/ppermute | solution.py:56
  160.2 5.1 %collective-permute-done.6.refs_3_ = bf16[4,96,512]{2,1,0:T(8,128)(2,1)S(1)} collective-permute-done((bf16[4,96,512]{2,1,0:T(8,128)(2,1)}, bf16[4,96,512]{2,1,0:T(8,128)(2,1)S(1)}, u32[]{:S(2)}, u32[]{:S(2)}) %collective-permute-start.6) | collective-permute-done | bytes 393248 | tf_op jit(solution)/shard_map/ppermute | solution.py:56
  165.9 8.3 %collective-permute-done.5.refs_2_ = bf16[4,96,512]{2,1,0:T(8,128)(2,1)S(1)} collective-permute-done((bf16[4,96,512]{2,1,0:T(8,128)(2,1)S(1)}, bf16[4,96,512]{2,1,0:T(8,128)(2,1)S(1)}, u32[]{:S(2)}, u32[]{:S(2)}) %collective-permute-start.5) | collective-permute-done | bytes 393248 | tf_op jit(solution)/shard_map/ppermute | solution.py:56
  177.2 7.6 %up_rows.2 = (bf16[96,384]{1,0:T(8,128)(2,1)S(1)}, bf16[96,384]{1,0:T(8,128)(2,1)S(1)}, bf16[96,384]{1,0:T(8,128)(2,1)S(1)}, bf16[96,384]{1,0:T(8,128)(2,1)S(1)}) custom-call(bf16[4,96,512]{2,1,0:T(8,128)(2,1)S(1)} %copy-done.13, bf16[4,96,512]{2,1,0:T(8,128)(2,1)S(1)} %collective-permute-done.4.refs_1_, ...), custom_call_target="tpu_custom_call" | custom-call | tf_op jit(solution)/shard_map/up_rows/pallas_call | solution.py:210
  189.4 2.7 %collective-permute-done.13.h2 = bf16[96,384]{1,0:T(8,128)(2,1)S(1)} collective-permute-done((bf16[96,384]{1,0:T(8,128)(2,1)S(1)}, bf16[96,384]{1,0:T(8,128)(2,1)S(1)}, u32[]{:S(2)}, u32[]{:S(2)}) %collective-permute-start.13) | collective-permute-done | bytes 73760 | tf_op jit(solution)/shard_map/ppermute | solution.py:56
  192.6 9.3 %down_rows.2 = bf16[768,512]{1,0:T(8,128)(2,1)S(1)} custom-call(s32[2]{0:T(128)S(1)} %pad_add_fusion.place, bf16[96,384]{1,0:T(8,128)(2,1)S(1)} %get-tuple-element.35.h0, bf16[96,384]{1,0:T(8,128)(2,1)S(1)} %collective-permute-done.12.h1, bf16[96,384]{1,0:T(8,128)(2,1)S(1)} %collective-permute-done.13.h2, bf16[96,384]{1,0:T(8,128)(2,1)S(1)} %collective-permute-done.14.h3, ...), custom_call_target="tpu_custom_call" | custom-call | tf_op jit(solution)/shard_map/down_rows/pallas_call | solution.py:253
  201.9 24.1 %all_to_all.44 = bf16[32,24,512]{2,1,0:T(8,128)(2,1)S(1)} all-to-all(bf16[32,24,512]{2,1,0:T(8,128)(2,1)S(1)} %bitcast.66), channel_id=1, replica_groups=mesh['expert'=32,'tensor'=8] {'expert'}, dimensions={0} | all-to-all | bytes 1572864 | tf_op jit(solution)/shard_map/all_to_all | solution.py:408
  230.7 3.9 %collective-permute-done.24 = bf16[144,512]{1,0:T(8,128)(2,1)S(1)} collective-permute-done((bf16[144,512]{1,0:T(8,128)(2,1)S(1)}, bf16[144,512]{1,0:T(8,128)(2,1)S(1)}, u32[]{:S(2)}, u32[]{:S(2)}) %collective-permute-start.24) | collective-permute-done | bytes 147488 | tf_op jit(solution)/shard_map/ppermute | solution.py:56
  235.3 10.4 %collective-permute-start.27 = (bf16[4,144,512]{2,1,0:T(8,128)(2,1)S(1)}, bf16[4,144,512]{2,1,0:T(8,128)(2,1)S(1)}, u32[]{:S(2)}, u32[]{:S(2)}) collective-permute-start(bf16[4,144,512]{2,1,0:T(8,128)(2,1)S(1)} %pad_maximum_fusion.same_core), channel_id=1, source_target_pairs={{0,1},{1,0},{2,3},{3,2},{4,5},{5,4},{6,7},{7,6},{8,9},{9,8},{10,11... | collective-permute-start | bytes 1769480 | tf_op jit(solution)/shard_map/ppermute | solution.py:60
  (153 shorter events, 64.6 us)
Async XLA Ops:
  7.2 119.9 %all-gather.2.cloned.1.call-start = ((), (), s32[]{:S(2)}) async-start(), calls=%async_computation.4 | async-start | bytes 14155776 | tf_op jit(solution)/shard_map/all_gather | solution.py:376
  17.6 6.6 %collective-permute-start.1 = (bf16[16,4096]{1,0:T(8,128)(2,1)S(1)}, bf16[16,4096]{1,0:T(8,128)(2,1)S(1)}, u32[]{:S(2)}, u32[]{:S(2)}) collective-permute-start(bf16[16,4096]{1,0:T(8,128)(2,1)S(1)} %get-tuple-element.27), channel_id=1, source_target_pairs={{0,2},{1,3},{2,4},{3,5},{4,6},{5,7},{6,0},{7,1},{8,10},{9,11},{10,... | collective-permute-start | bytes 393224 | tf_op jit(solution)/shard_map/ppermute | solution.py:56
  17.7 8.4 %collective-permute-start.2 = (bf16[16,4096]{1,0:T(8,128)(2,1)S(1)}, bf16[16,4096]{1,0:T(8,128)(2,1)S(1)}, u32[]{:S(2)}, u32[]{:S(2)}) collective-permute-start(bf16[16,4096]{1,0:T(8,128)(2,1)S(1)} %get-tuple-element.28), channel_id=1, source_target_pairs={{0,4},{1,5},{2,6},{3,7},{4,0},{5,1},{6,2},{7,3},{8,12},{9,13},{10,... | collective-permute-start | bytes 393224 | tf_op jit(solution)/shard_map/ppermute | solution.py:56
  19.9 6.9 %collective-permute-start.3 = (bf16[16,4096]{1,0:T(8,128)(2,1)S(1)}, bf16[16,4096]{1,0:T(8,128)(2,1)S(1)}, u32[]{:S(2)}, u32[]{:S(2)}) collective-permute-start(bf16[16,4096]{1,0:T(8,128)(2,1)S(1)} %get-tuple-element.29), channel_id=1, source_target_pairs={{0,6},{1,7},{2,0},{3,1},{4,2},{5,3},{6,4},{7,5},{8,14},{9,15},{10,... | collective-permute-start | bytes 393224 | tf_op jit(solution)/shard_map/ppermute | solution.py:56
  32.0 31.5 %all-to-all-start.1 = ((bf16[32,24,512]{2,1,0:T(8,128)(2,1)}), bf16[32,24,512]{2,1,0:T(8,128)(2,1)}, u32[]{:S(2)}, u32[]{:S(2)}) async-start(bf16[32,24,512]{2,1,0:T(8,128)(2,1)} %bitcast.68), calls=%async_computation.1 | async-start | bytes 1572864 | tf_op jit(solution)/shard_map/all_to_all | solution.py:392
  42.4 34.9 %collective-permute-start.10 = (bf16[192,4096]{1,0:T(8,128)(2,1)S(1)}, bf16[192,4096]{1,0:T(8,128)(2,1)}, u32[]{:S(2)}, u32[]{:S(2)}) collective-permute-start(bf16[192,4096]{1,0:T(8,128)(2,1)S(1)} %bitcast.58), channel_id=1, source_target_pairs={{0,1},{1,0},{2,3},{3,2},{4,5},{5,4},{6,7},{7,6},{8,9},{9,8},{10,11... | collective-permute-start | bytes 4718600 | tf_op jit(solution)/shard_map/ppermute | solution.py:60
  43.9 50.9 %collective-permute-start.11 = (bf16[192,4096]{1,0:T(8,128)(2,1)S(1)}, bf16[192,4096]{1,0:T(8,128)(2,1)}, u32[]{:S(2)}, u32[]{:S(2)}) collective-permute-start(bf16[192,4096]{1,0:T(8,128)(2,1)S(1)} %bitcast.61), channel_id=1, source_target_pairs={{0,1},{1,0},{2,3},{3,2},{4,5},{5,4},{6,7},{7,6},{8,9},{9,8},{10,11... | collective-permute-start | bytes 4718600 | tf_op jit(solution)/shard_map/ppermute | solution.py:60
  63.5 28.7 %all-to-all-start = ((bf16[32,24,512]{2,1,0:T(8,128)(2,1)}), bf16[32,24,512]{2,1,0:T(8,128)(2,1)}, u32[]{:S(2)}, u32[]{:S(2)}) async-start(bf16[32,24,512]{2,1,0:T(8,128)(2,1)} %bitcast.67), calls=%async_computation | async-start | bytes 1572864 | tf_op jit(solution)/shard_map/all_to_all | solution.py:392
  73.9 15.6 %collective-permute-start.15 = (bf16[4,96,512]{2,1,0:T(8,128)(2,1)}, bf16[4,96,512]{2,1,0:T(8,128)(2,1)S(1)}, u32[]{:S(2)}, u32[]{:S(2)}) collective-permute-start(bf16[4,96,512]{2,1,0:T(8,128)(2,1)} %get-tuple-element.34.refs_12_.refs_0_), channel_id=1, source_target_pairs={{0,2},{1,3},{2,4},{3,5},{4,6},{5,7},{6,0},{7,1},{8,10},{9,11},{10,... | collective-permute-start | bytes 1179656 | tf_op jit(solution)/shard_map/ppermute | solution.py:56
  74.7 14.8 %collective-permute-start.19 = (bf16[4,96,512]{2,1,0:T(8,128)(2,1)}, bf16[4,96,512]{2,1,0:T(8,128)(2,1)}, u32[]{:S(2)}, u32[]{:S(2)}) collective-permute-start(bf16[4,96,512]{2,1,0:T(8,128)(2,1)} %get-tuple-element.39.refs_4_), channel_id=1, source_target_pairs={{0,6},{1,7},{2,0},{3,1},{4,2},{5,3},{6,4},{7,5},{8,14},{9,15},{10,... | collective-permute-start | bytes 1179656 | tf_op jit(solution)/shard_map/ppermute | solution.py:56
  76.6 21.0 %collective-permute-start.17 = (bf16[4,96,512]{2,1,0:T(8,128)(2,1)}, bf16[4,96,512]{2,1,0:T(8,128)(2,1)}, u32[]{:S(2)}, u32[]{:S(2)}) collective-permute-start(bf16[4,96,512]{2,1,0:T(8,128)(2,1)} %get-tuple-element.34.refs_12_.refs_0_), channel_id=1, source_target_pairs={{0,6},{1,7},{2,0},{3,1},{4,2},{5,3},{6,4},{7,5},{8,14},{9,15},{10,... | collective-permute-start | bytes 1179656 | tf_op jit(solution)/shard_map/ppermute | solution.py:56
  77.3 20.6 %collective-permute-start.18 = (bf16[4,96,512]{2,1,0:T(8,128)(2,1)}, bf16[4,96,512]{2,1,0:T(8,128)(2,1)}, u32[]{:S(2)}, u32[]{:S(2)}) collective-permute-start(bf16[4,96,512]{2,1,0:T(8,128)(2,1)} %get-tuple-element.39.refs_4_), channel_id=1, source_target_pairs={{0,2},{1,3},{2,4},{3,5},{4,6},{5,7},{6,0},{7,1},{8,10},{9,11},{10,... | collective-permute-start | bytes 1179656 | tf_op jit(solution)/shard_map/ppermute | solution.py:56
  89.5 16.9 %collective-permute-start.16 = (bf16[4,96,512]{2,1,0:T(8,128)(2,1)S(1)}, bf16[4,96,512]{2,1,0:T(8,128)(2,1)}, u32[]{:S(2)}, u32[]{:S(2)}) collective-permute-start(bf16[4,96,512]{2,1,0:T(8,128)(2,1)S(1)} %collective-permute-done.15.refs_1_), channel_id=1, source_target_pairs={{0,2},{1,3},{2,4},{3,5},{4,6},{5,7},{6,0},{7,1},{8,10},{9,11},{10,... | collective-permute-start | bytes 1179656 | tf_op jit(solution)/shard_map/ppermute | solution.py:56
  89.5 16.8 %collective-permute-start.20 = (bf16[4,96,512]{2,1,0:T(8,128)(2,1)}, bf16[4,96,512]{2,1,0:T(8,128)(2,1)}, u32[]{:S(2)}, u32[]{:S(2)}) collective-permute-start(bf16[4,96,512]{2,1,0:T(8,128)(2,1)} %collective-permute-done.19.refs_7_), channel_id=1, source_target_pairs={{0,6},{1,7},{2,0},{3,1},{4,2},{5,3},{6,4},{7,5},{8,14},{9,15},{10,... | collective-permute-start | bytes 1179656 | tf_op jit(solution)/shard_map/ppermute | solution.py:56
  139.9 62.0 %all-to-all-start.3 = ((bf16[32,24,512]{2,1,0:T(8,128)(2,1)}), bf16[32,24,512]{2,1,0:T(8,128)(2,1)}, u32[]{:S(2)}, u32[]{:S(2)}) async-start(bf16[32,24,512]{2,1,0:T(8,128)(2,1)} %bitcast.65), calls=%async_computation.3 | async-start | bytes 1572864 | tf_op jit(solution)/shard_map/all_to_all | solution.py:408
  148.6 8.9 %collective-permute-start.4 = (bf16[4,96,512]{2,1,0:T(8,128)(2,1)}, bf16[4,96,512]{2,1,0:T(8,128)(2,1)S(1)}, u32[]{:S(2)}, u32[]{:S(2)}) collective-permute-start(bf16[4,96,512]{2,1,0:T(8,128)(2,1)} %get-tuple-element.31.refs_0_.refs_12_), channel_id=1, source_target_pairs={{0,2},{1,3},{2,4},{3,5},{4,6},{5,7},{6,0},{7,1},{8,10},{9,11},{10,... | collective-permute-start | bytes 1179656 | tf_op jit(solution)/shard_map/ppermute | solution.py:56
  149.0 8.5 %collective-permute-start.8 = (bf16[4,96,512]{2,1,0:T(8,128)(2,1)}, bf16[4,96,512]{2,1,0:T(8,128)(2,1)S(1)}, u32[]{:S(2)}, u32[]{:S(2)}) collective-permute-start(bf16[4,96,512]{2,1,0:T(8,128)(2,1)} %get-tuple-element.32.refs_4_), channel_id=1, source_target_pairs={{0,6},{1,7},{2,0},{3,1},{4,2},{5,3},{6,4},{7,5},{8,14},{9,15},{10,... | collective-permute-start | bytes 1179656 | tf_op jit(solution)/shard_map/ppermute | solution.py:56
  151.3 13.9 %collective-permute-start.6 = (bf16[4,96,512]{2,1,0:T(8,128)(2,1)}, bf16[4,96,512]{2,1,0:T(8,128)(2,1)S(1)}, u32[]{:S(2)}, u32[]{:S(2)}) collective-permute-start(bf16[4,96,512]{2,1,0:T(8,128)(2,1)} %get-tuple-element.31.refs_0_.refs_12_), channel_id=1, source_target_pairs={{0,6},{1,7},{2,0},{3,1},{4,2},{5,3},{6,4},{7,5},{8,14},{9,15},{10,... | collective-permute-start | bytes 1179656 | tf_op jit(solution)/shard_map/ppermute | solution.py:56
  151.4 14.5 %collective-permute-start.7 = (bf16[4,96,512]{2,1,0:T(8,128)(2,1)}, bf16[4,96,512]{2,1,0:T(8,128)(2,1)S(1)}, u32[]{:S(2)}, u32[]{:S(2)}) collective-permute-start(bf16[4,96,512]{2,1,0:T(8,128)(2,1)} %get-tuple-element.32.refs_4_), channel_id=1, source_target_pairs={{0,2},{1,3},{2,4},{3,5},{4,6},{5,7},{6,0},{7,1},{8,10},{9,11},{10,... | collective-permute-start | bytes 1179656 | tf_op jit(solution)/shard_map/ppermute | solution.py:56
  157.5 16.7 %collective-permute-start.5 = (bf16[4,96,512]{2,1,0:T(8,128)(2,1)S(1)}, bf16[4,96,512]{2,1,0:T(8,128)(2,1)S(1)}, u32[]{:S(2)}, u32[]{:S(2)}) collective-permute-start(bf16[4,96,512]{2,1,0:T(8,128)(2,1)S(1)} %collective-permute-done.4.refs_1_), channel_id=1, source_target_pairs={{0,2},{1,3},{2,4},{3,5},{4,6},{5,7},{6,0},{7,1},{8,10},{9,11},{10,... | collective-permute-start | bytes 1179656 | tf_op jit(solution)/shard_map/ppermute | solution.py:56
  157.5 16.7 %collective-permute-start.9 = (bf16[4,96,512]{2,1,0:T(8,128)(2,1)S(1)}, bf16[4,96,512]{2,1,0:T(8,128)(2,1)S(1)}, u32[]{:S(2)}, u32[]{:S(2)}) collective-permute-start(bf16[4,96,512]{2,1,0:T(8,128)(2,1)S(1)} %collective-permute-done.8.refs_7_), channel_id=1, source_target_pairs={{0,6},{1,7},{2,0},{3,1},{4,2},{5,3},{6,4},{7,5},{8,14},{9,15},{10,... | collective-permute-start | bytes 1179656 | tf_op jit(solution)/shard_map/ppermute | solution.py:56
  227.8 6.9 %collective-permute-start.24 = (bf16[144,512]{1,0:T(8,128)(2,1)S(1)}, bf16[144,512]{1,0:T(8,128)(2,1)S(1)}, u32[]{:S(2)}, u32[]{:S(2)}) collective-permute-start(bf16[144,512]{1,0:T(8,128)(2,1)S(1)} %finish.1), channel_id=1, source_target_pairs={{0,2},{1,3},{2,4},{3,5},{4,6},{5,7},{6,0},{7,1},{8,10},{9,11},{10,... | collective-permute-start | bytes 442376 | tf_op jit(solution)/shard_map/ppermute | solution.py:56
  227.9 6.8 %collective-permute-start.25 = (bf16[144,512]{1,0:T(8,128)(2,1)S(1)}, bf16[144,512]{1,0:T(8,128)(2,1)S(1)}, u32[]{:S(2)}, u32[]{:S(2)}) collective-permute-start(bf16[144,512]{1,0:T(8,128)(2,1)S(1)} %finish.1), channel_id=1, source_target_pairs={{0,4},{1,5},{2,6},{3,7},{4,0},{5,1},{6,2},{7,3},{8,12},{9,13},{10,... | collective-permute-start | bytes 442376 | tf_op jit(solution)/shard_map/ppermute | solution.py:56
  235.3 12.1 %collective-permute-start.27 = (bf16[4,144,512]{2,1,0:T(8,128)(2,1)S(1)}, bf16[4,144,512]{2,1,0:T(8,128)(2,1)S(1)}, u32[]{:S(2)}, u32[]{:S(2)}) collective-permute-start(bf16[4,144,512]{2,1,0:T(8,128)(2,1)S(1)} %pad_maximum_fusion.same_core), channel_id=1, source_target_pairs={{0,1},{1,0},{2,3},{3,2},{4,5},{5,4},{6,7},{7,6},{8,9},{9,8},{10,11... | collective-permute-start | bytes 1769480 | tf_op jit(solution)/shard_map/ppermute | solution.py:60
  (41 other events, 260.3 us)
Sparse Core Ops, SparseCore 0:
  9.8 77.2 all-gather.1

commit v3 on v2

--- a/solution.py
+++ b/solution.py
@@ -13,7 +13,10 @@
 BATCH = 16
 f32 = jnp.float32
 bf16 = jnp.bfloat16
-roomy = pltpu.CompilerParams(vmem_limit_bytes=44 * 2**20)
+
+
+def space(mebibytes):
+    return pltpu.CompilerParams(vmem_limit_bytes=mebibytes * 2**20)
 
 
 def slot_targets(chosen, expert_count, capacity):
@@ -94,7 +97,7 @@
             out_specs=[pl.BlockSpec((CHIPS, rows, step), lambda n, place: (0, 0, n))] * 2,
         ),
         out_shape=(out, out),
-        compiler_params=roomy,
+        compiler_params=space(8),
         name="project",
     )(place, attn, weight)
 
@@ -107,11 +110,11 @@
 def pair_sums(mine, other):
     out = jax.ShapeDtypeStruct(mine.shape[1:], bf16)
     return pl.pallas_call(
-        pair_kernel, out_shape=(out,) * CHIPS, compiler_params=roomy, name="pair_sums"
+        pair_kernel, out_shape=(out,) * CHIPS, compiler_params=space(6), name="pair_sums"
     )(mine, other)
 
 
-def front_kernel(place, p0, p1, p2, p3, residual, gain, router, shares0, shares1, *outs):
+def front_kernel(place, p0, p1, p2, p3, residual, gain, router, shares0, shares1, _, *outs):
     outbox0, outbox1, stream_out, logits_out = outs
     rows = p0.shape[0]
     start = (2 * place[0] + place[1]) * rows
@@ -131,30 +134,30 @@
         outbox[...] = dot_first(hits, by_piece).astype(bf16)
 
 
-def front(place, parts, residual, gain, router, shares):
+def front(place, parts, residual, gain, router, shares, after):
     rows, width = parts[0].shape
     piece = width // PIECES
     whole = pl.BlockSpec(memory_space=pltpu.VMEM)
     outbox = jax.ShapeDtypeStruct((shares[0].shape[1], piece), bf16)
     return pl.pallas_call(
         front_kernel,
-        in_specs=[pl.BlockSpec(memory_space=pltpu.SMEM)] + [whole] * 9,
+        in_specs=[pl.BlockSpec(memory_space=pltpu.SMEM)]
+        + [whole] * 9
+        + [pl.BlockSpec(memory_space=pl.ANY)],
         out_shape=(
             outbox,
             outbox,
             jax.ShapeDtypeStruct((rows * PIECES, piece), bf16),
             jax.ShapeDtypeStruct((rows, router.shape[0]), f32),
         ),
-        compiler_params=roomy,
+        compiler_params=space(10),
         name="front",
-    )(place, *parts, residual, gain, router, *shares)
-
-
-def by_piece_kernel(x, order, low, high):
+    )(place, *parts, residual, gain, router, *shares, after)
+
+
+def by_piece_kernel(x, order, out):
     moved = jnp.dot(order[...], x[...], preferred_element_type=f32)
-    moved = moved.reshape((PIECES,) + low.shape[1:]).astype(bf16)
-    low[...] = moved[: PIECES // 2]
-    high[...] = moved[PIECES // 2 :]
+    out[...] = moved.reshape(out.shape).astype(bf16)
 
 
 def rows_by_piece(x, order):
@@ -162,7 +165,6 @@
     steps = x.shape[0] // size
     width = x.shape[1]
     run = size // PIECES
-    out = jax.ShapeDtypeStruct((PIECES // 2, run * steps, width), bf16)
     return pl.pallas_call(
         by_piece_kernel,
         grid=(steps,),
@@ -170,31 +172,31 @@
             pl.BlockSpec((size, width), lambda a: (a, 0)),
             pl.BlockSpec((size, size), lambda a: (0, 0)),
         ],
-        out_specs=[pl.BlockSpec((PIECES // 2, run, width), lambda a: (0, a, 0))] * 2,
-        out_shape=(out, out),
+        out_specs=pl.BlockSpec((PIECES, run, width), lambda a: (0, a, 0)),
+        out_shape=jax.ShapeDtypeStruct((PIECES, run * steps, width), bf16),
+        compiler_params=space(6),
         name="rows_by_piece",
     )(x, order)
 
 
-def up_kernel(*refs):
-    lows, highs = refs[:CHIPS], refs[CHIPS : 2 * CHIPS]
-    gate_own, gate_other, up_own, up_other = refs[2 * CHIPS : 2 * CHIPS + 4]
-    outs = refs[2 * CHIPS + 5 : 3 * CHIPS + 5]
-    gate, up = refs[3 * CHIPS + 5 :]
-    j = pl.program_id(0)
-
-    @pl.when(j == 0)
+def up_kernel(own, back, ahead, far_low, far_high, *refs):
+    gate_own, gate_other, up_own, up_other, _, *outs, gate, up = refs
+    step = pl.program_id(0)
+    width = own.shape[2]
+
+    @pl.when(step == 0)
     def _():
         gate[...] = jnp.zeros_like(gate)
         up[...] = jnp.zeros_like(up)
 
-    x = jnp.concatenate(
-        [jnp.where(j < PIECES // 2, low[0], high[0]) for low, high in zip(lows, highs)], axis=0
-    )
-    gate[...] += dot_last(x, jnp.concatenate([gate_own[...], gate_other[...]], axis=0))
-    up[...] += dot_last(x, jnp.concatenate([up_own[...], up_other[...]], axis=0))
-
-    @pl.when(j == PIECES - 1)
+    for q in range(own.shape[0]):
+        far = jnp.where(step == 0, far_low[q], far_high[q])
+        x = jnp.concatenate([own[q], back[q], far, ahead[q]], axis=0)
+        at = slice(q * width, (q + 1) * width)
+        gate[...] += dot_last(x, jnp.concatenate([gate_own[:, at], gate_other[:, at]], axis=0))
+        up[...] += dot_last(x, jnp.concatenate([up_own[:, at], up_other[:, at]], axis=0))
+
+    @pl.when(step == pl.num_programs(0) - 1)
     def _():
         g = gate[...]
         hidden = (g / (1.0 + jnp.exp(-g)) * up[...]).astype(bf16)
@@ -203,70 +205,67 @@
             outs[i][...] = hidden[i * rows : (i + 1) * rows, :]
 
 
-def up_rows(lows, highs, weights, after):
-    _, rows, width = lows[0].shape
+def up_rows(own, back, ahead, far, weights, after):
+    pieces, rows, width = own.shape
+    half = pieces // 2
     units = weights[0].shape[0]
     out = jax.ShapeDtypeStruct((rows, 2 * units), bf16)
     return pl.pallas_call(
         up_kernel,
-        grid=(PIECES,),
-        in_specs=[
-            pl.BlockSpec((1, rows, width), lambda j: (jnp.minimum(j, PIECES // 2 - 1), 0, 0))
-        ]
-        * CHIPS
-        + [pl.BlockSpec((1, rows, width), lambda j: (jnp.maximum(j - PIECES // 2, 0), 0, 0))]
-        * CHIPS
-        + [pl.BlockSpec((units, width), lambda j: (0, j))] * 4
+        grid=(2,),
+        in_specs=[pl.BlockSpec((half, rows, width), lambda j: (j, 0, 0))] * 3
+        + [pl.BlockSpec((half, rows, width), lambda j: (0, 0, 0))] * 2
+        + [pl.BlockSpec((units, half * width), lambda j: (0, j))] * 4
         + [pl.BlockSpec(memory_space=pl.ANY)],
         out_specs=[pl.BlockSpec((rows, 2 * units), lambda j: (0, 0))] * CHIPS,
         out_shape=(out,) * CHIPS,
         scratch_shapes=[pltpu.VMEM((CHIPS * rows, 2 * units), f32)] * 2,
-        compiler_params=roomy,
+        compiler_params=space(15),
         name="up_rows",
-    )(*lows, *highs, *weights, after)
-
-
-def down_kernel(place, h0, h1, h2, h3, w_down, order, out, held):
-    j = pl.program_id(0)
-    chip, core = place[0], place[1]
+    )(own, back, ahead, *far, *weights, after)
+
+
+def down_kernel(*refs):
+    hidden, refs = refs[:CHIPS], refs[CHIPS:]
+    weights, (order, out, held) = refs[: 2 * CHIPS], refs[2 * CHIPS :]
+    step = pl.program_id(0)
     total = None
-    for i, hidden in enumerate((h0, h1, h2, h3)):
-        first = 2 * ((chip + i) % CHIPS)
-        weight = jnp.concatenate([w_down[first + core], w_down[first + (core + 1) % 2]], axis=0)
-        part = jnp.dot(hidden[...], weight, preferred_element_type=f32)
+    for i in range(CHIPS):
+        weight = jnp.concatenate([weights[2 * i][...], weights[2 * i + 1][...]], axis=0)
+        part = jnp.dot(hidden[i][...], weight, preferred_element_type=f32)
         total = part if total is None else total + part
-    held[j] = total.astype(bf16)
-
-    @pl.when(j == PIECES - 1)
+    total = total.astype(bf16)
+    width = held.shape[2]
+    count = total.shape[1] // width
+    for q in range(count):
+        held[step * count + q] = total[:, q * width : (q + 1) * width]
+
+    @pl.when(step == pl.num_programs(0) - 1)
     def _():
         size = order.shape[0]
         run = size // PIECES
         for a in range(held.shape[1] // run):
-            block = held[:, a * run : (a + 1) * run, :].reshape(size, held.shape[2])
+            block = held[:, a * run : (a + 1) * run, :].reshape(size, width)
             out[a * size : (a + 1) * size, :] = dot_first(order[...], block).astype(bf16)
 
 
-def down_rows(place, hidden, w_down, order):
+def down_rows(hidden, weights, order):
     rows, units = hidden[0].shape
-    ranks, depth, width = w_down.shape
+    depth, width = weights[0].shape
     piece = width // PIECES
+    steps = 4
     return pl.pallas_call(
         down_kernel,
-        grid_spec=pltpu.PrefetchScalarGridSpec(
-            num_scalar_prefetch=1,
-            grid=(PIECES,),
-            in_specs=[pl.BlockSpec((rows, units), lambda j, place: (0, 0))] * CHIPS
-            + [
-                pl.BlockSpec((ranks, depth, piece), lambda j, place: (0, 0, j)),
-                pl.BlockSpec(order.shape, lambda j, place: (0, 0)),
-            ],
-            out_specs=pl.BlockSpec((rows * PIECES, piece), lambda j, place: (0, 0)),
-            scratch_shapes=[pltpu.VMEM((PIECES, rows, piece), bf16)],
-        ),
+        grid=(steps,),
+        in_specs=[pl.BlockSpec((rows, units), lambda j: (0, 0))] * CHIPS
+        + [pl.BlockSpec((depth, width // steps), lambda j: (0, j))] * (2 * CHIPS)
+        + [pl.BlockSpec(order.shape, lambda j: (0, 0))],
+        out_specs=pl.BlockSpec((rows * PIECES, piece), lambda j: (0, 0)),
         out_shape=jax.ShapeDtypeStruct((rows * PIECES, piece), bf16),
-        compiler_params=roomy,
+        scratch_shapes=[pltpu.VMEM((PIECES, rows, piece), bf16)],
+        compiler_params=space(11),
         name="down_rows",
-    )(place, *hidden, w_down, order)
+    )(*hidden, *weights, order)
 
 
 def finish_kernel(back0, back1, weights0, weights1, stream, logits, out):
@@ -292,7 +291,7 @@
         out_shape=jax.ShapeDtypeStruct(
             (stream.shape[0] + logits.shape[0], stream.shape[1]), bf16
         ),
-        compiler_params=roomy,
+        compiler_params=space(6),
         name="finish",
     )(*returned, *weights, stream, logits)
 
@@ -324,7 +323,7 @@
             jax.ShapeDtypeStruct((rows * 2 * CHIPS, width), bf16),
             jax.ShapeDtypeStruct((rows * 2 * CHIPS, expert_count), f32),
         ),
-        compiler_params=roomy,
+        compiler_params=space(6),
         name="assemble",
     )(place, same_core, other_core)
 
@@ -373,7 +372,7 @@
     capacity = min(rows, max(2, 3 * rows * top_count // (2 * expert_count)))
     slots = capacity // HALVES
 
-    w_down_all = lax.all_gather(w_down[0], "tensor", axis=0, tiled=False)
+    same_core = [w_down[0]] + [along(w_down[0], shift) for shift in range(1, CHIPS)]
     gate_own, up_own = w_gate[0].T, w_up[0].T
     weights = (gate_own, across(gate_own), up_own, across(up_own))
     order = reorder_matrix(PIECES, BATCH, slots)
@@ -384,26 +383,26 @@
     mine, theirs = project(place, attn_out, o_weight)
     sums = pair_sums(mine, across(theirs))
     parts = (sums[0],) + tuple(along(sums[shift], shift) for shift in range(1, CHIPS))
+    down_weights = []
+    for shift in range(CHIPS):
+        weight = same_core[-shift % CHIPS]
+        down_weights += [weight, across(weight)]
     outbox0, outbox1, stream, logits = front(
-        place, parts, residual, norm_gain.reshape(1, width), router_weight.T, shares
+        place, parts, residual, norm_gain.reshape(1, width), router_weight.T, shares, order
     )
     arrived = []
     for outbox in (outbox0, outbox1):
         arrived.append(lax.all_to_all(outbox, "expert", split_axis=0, concat_axis=0, tiled=True))
-    own = [rows_by_piece(x, order) for x in arrived]
+    own = []
+    for x in arrived:
+        own.append(rows_by_piece(x, order))
     returned = []
-    for half, (low, high) in enumerate(own):
-        low_up, high_down = along(low, 1), along(high, -1)
-        high_up, low_down = along(high, 1), along(low, -1)
-        low_far, high_far = along(low_up, 1), along(high_down, -1)
-        hidden = up_rows(
-            (low, low_up, low_far, low_down),
-            (high, high_up, high_far, high_down),
-            weights,
-            own[1][0] if half == 0 else own[0][0],
-        )
+    for half, mine in enumerate(own):
+        back, ahead = along(mine, 1), along(mine, -1)
+        far = (along(back[: PIECES // 2], 1), along(ahead[PIECES // 2 :], -1))
+        hidden = up_rows(mine, back, ahead, far, weights, own[1 - half])
         units = (hidden[0],) + tuple(along(hidden[s], -s) for s in range(1, CHIPS))
-        expert_out = down_rows(place, units, w_down_all, order)
+        expert_out = down_rows(units, down_weights, order)
         returned.append(
             lax.all_to_all(expert_out, "expert", split_axis=0, concat_axis=0, tiled=True)
         )

time: 258 us -> 278 us (1.078)
  starting transfers between devices: 66.5 us -> 106 us
  between operations: 14.4 us -> 1.07 us
  waiting for transfers between devices: 81.8 us -> 93.6 us
  Pallas kernels: 46.5 us -> 35.7 us
  local copies, waits for them, and re-layouts: 19.8 us -> 14.4 us
    ppermute x4 -> x8, starting transfers between devices: 15.3 us -> 52.5 us  [across(): return lax.ppermute(x, 'tensor', [(r, r ^ 1) for r in range(2 * CHIPS)])]
    ppermute x24 -> x23, waiting for transfers between devices: 60 us -> 75.7 us  [along(): return lax.ppermute(x, 'tensor', pairs)]
    unnamed x67 -> x43, local copies, waits for them, and re-layouts: 18.5 us -> 10.3 us
    pallas_call x5, Pallas kernels: 34.5 us -> 26.5 us  [the longest x2 13.7 us: down_rows(): pl.pallas_call(down_kernel, grid=(steps,), in_specs=[pl.BlockSpec((rows,...]
    pallas_call x2, Pallas kernels: 5.24 us -> 1.55 us  [rows_by_piece(): pl.pallas_call(by_piece_kernel, grid=(steps,), in_specs=[pl.BlockSpec((si...]
    all_to_all x2, starting transfers between devices: 16.3 us -> 19.9 us  [shards(): lax.all_to_all(outbox, 'expert', split_axis=0, concat_axis=0, tiled=True)]
    all_to_all x2, waiting for transfers between devices: 19.5 us -> 16.2 us  [shards(): lax.all_to_all(outbox, 'expert', split_axis=0, concat_axis=0, tiled=True)]
    slice x0 -> x4, local copies, waits for them, and re-layouts: none -> 2.85 us  [shards(): far = (along(back[:PIECES // 2], 1), along(ahead[PIECES // 2:], -1))]
  transfers between devices with their start and end apart: 32 -> 34, of which waited for: 21 -> 22; matrix products, arithmetic and copies ran while one was open for 2% -> 2% of each run, Pallas kernels for 13% -> 8%
where the time goes in v3:
time: 278 us; the launch traced here: 277 us
  starting transfers between devices  106 us (38%)
  waiting for transfers between devices  93.6 us (34%)
  Pallas kernels  35.7 us (13%)
  blocking collectives  24 us (9%)
  local copies, waits for them, and re-layouts  14.4 us (5%)
    ppermute x23, waiting for transfers between devices, along(): return lax.ppermute(x, 'tensor', pairs)  75.7 us
    ppermute x8, starting transfers between devices, across(): return lax.ppermute(x, 'tensor', [(r, r ^ 1) for r in range(2 * CHIPS)])  52.5 us
    ppermute x23, starting transfers between devices, along(): return lax.ppermute(x, 'tensor', pairs)  24.2 us
    all_to_all x1, blocking collectives, shards(): lax.all_to_all(expert_out, 'expert', split_axis=0, concat_axis=0, tiled=T...  24 us
    all_to_all x2, starting transfers between devices, shards(): lax.all_to_all(outbox, 'expert', split_axis=0, concat_axis=0, tiled=True)  19.9 us
    all_to_all x2, waiting for transfers between devices, shards(): lax.all_to_all(outbox, 'expert', split_axis=0, concat_axis=0, tiled=True)  16.2 us
    pallas_call x2, Pallas kernels, down_rows(): pl.pallas_call(down_kernel, grid=(steps,), in_specs=[pl.BlockSpec((rows,...  13.7 us
    pallas_call x2, Pallas kernels, up_rows(): pl.pallas_call(up_kernel, grid=(2,), in_specs=[pl.BlockSpec((half, rows,...  11.4 us
  transfers between devices with their start and end apart: 34, of which 22 were waited for; matrix products, arithmetic and copies ran while one was open for 2% of the time, Pallas kernels for 8%

profile of v3, /device:TPU:1, one launch (start us, length us, event | category | flops | bytes accessed | tf_op | source)
XLA Modules:
  0.0 277.2 jit_solution(305917578620423657)
XLA Ops:
  3.8 3.1 %project.1 = (bf16[4,16,4096]{2,1,0:T(8,128)(2,1)S(1)}, bf16[4,16,4096]{2,1,0:T(8,128)(2,1)}) custom-call(s32[2]{0:T(128)S(1)} %pad_add_fusion.place, bf16[128,512]{1,0:T(8,128)(2,1)S(1)} %copy-done.16, bf16[512,4096]{1,0:T(8,128)(2,1)S(1)} %copy-done.2), custom_call_target="tpu_custom_call" | custom-call | tf_op jit(solution)/shard_map/project/pallas_call | solution.py:88
  6.9 3.2 %collective-permute-start = (bf16[4,16,4096]{2,1,0:T(8,128)(2,1)}, bf16[4,16,4096]{2,1,0:T(8,128)(2,1)}, u32[]{:S(2)}, u32[]{:S(2)}) collective-permute-start(bf16[4,16,4096]{2,1,0:T(8,128)(2,1)} %get-tuple-element.21), channel_id=1, source_target_pairs={{0,1},{1,0},{2,3},{3,2},{4,5},{5,4},{6,7},{7,6},{8,9},{9,8},{10,11... | collective-permute-start | bytes 1572872 | tf_op jit(solution)/shard_map/ppermute | solution.py:63
  27.6 10.2 %all-to-all-start.1 = ((bf16[32,24,512]{2,1,0:T(8,128)(2,1)}), bf16[32,24,512]{2,1,0:T(8,128)(2,1)S(1)}, u32[]{:S(2)}, u32[]{:S(2)}) async-start(bf16[32,24,512]{2,1,0:T(8,128)(2,1)} %bitcast.68), calls=%async_computation.1 | async-start | bytes 1572864 | tf_op jit(solution)/shard_map/all_to_all | solution.py:395
  43.9 14.8 %all-to-all-done.1 = bf16[32,24,512]{2,1,0:T(8,128)(2,1)S(1)} async-done(((bf16[32,24,512]{2,1,0:T(8,128)(2,1)}), bf16[32,24,512]{2,1,0:T(8,128)(2,1)S(1)}, u32[]{:S(2)}, u32[]{:S(2)}) %all-to-all-start.1) | async-done | bytes 786464 | tf_op jit(solution)/shard_map/all_to_all | solution.py:395
  61.9 15.0 %collective-permute-done.18.refs_10_ = bf16[192,4096]{1,0:T(8,128)(2,1)} collective-permute-done((bf16[192,4096]{1,0:T(8,128)(2,1)}, bf16[192,4096]{1,0:T(8,128)(2,1)}, u32[]{:S(2)}, u32[]{:S(2)}) %collective-permute-start.18) | collective-permute-done | bytes 1572896 | tf_op jit(solution)/shard_map/ppermute | solution.py:59
  76.9 34.8 %collective-permute-start.13 = (bf16[192,4096]{1,0:T(8,128)(2,1)}, bf16[192,4096]{1,0:T(8,128)(2,1)}, u32[]{:S(2)}, u32[]{:S(2)}) collective-permute-start(bf16[192,4096]{1,0:T(8,128)(2,1)} %bitcast.30.refs_4_), channel_id=1, source_target_pairs={{0,1},{1,0},{2,3},{3,2},{4,5},{5,4},{6,7},{7,6},{8,9},{9,8},{10,11... | collective-permute-start | bytes 4718600 | tf_op jit(solution)/shard_map/ppermute | solution.py:63
  112.5 9.7 %all-to-all-start = ((bf16[32,24,512]{2,1,0:T(8,128)(2,1)}), bf16[32,24,512]{2,1,0:T(8,128)(2,1)S(1)}, u32[]{:S(2)}, u32[]{:S(2)}) async-start(bf16[32,24,512]{2,1,0:T(8,128)(2,1)} %bitcast.67), calls=%async_computation | async-start | bytes 1572864 | tf_op jit(solution)/shard_map/all_to_all | solution.py:395
  122.6 5.2 %collective-permute-done.21.ahead = bf16[8,96,512]{2,1,0:T(8,128)(2,1)} collective-permute-done((bf16[8,96,512]{2,1,0:T(8,128)(2,1)S(1)}, bf16[8,96,512]{2,1,0:T(8,128)(2,1)}, u32[]{:S(2)}, u32[]{:S(2)}) %collective-permute-start.21) | collective-permute-done | bytes 786464 | tf_op jit(solution)/shard_map/ppermute | solution.py:59
  130.0 2.4 collective-permute-start.23
  134.3 6.7 %collective-permute-done.23.far_high = bf16[4,96,512]{2,1,0:T(8,128)(2,1)S(1)} collective-permute-done((bf16[4,96,512]{2,1,0:T(8,128)(2,1)S(1)}, bf16[4,96,512]{2,1,0:T(8,128)(2,1)S(1)}, u32[]{:S(2)}, u32[]{:S(2)}) %collective-permute-start.23) | collective-permute-done | bytes 393248 | tf_op jit(solution)/shard_map/ppermute | solution.py:59
  147.1 6.9 %collective-permute-done.22.far_low = bf16[4,96,512]{2,1,0:T(8,128)(2,1)} collective-permute-done((bf16[4,96,512]{2,1,0:T(8,128)(2,1)}, bf16[4,96,512]{2,1,0:T(8,128)(2,1)}, u32[]{:S(2)}, u32[]{:S(2)}) %collective-permute-start.22) | collective-permute-done | bytes 393248 | tf_op jit(solution)/shard_map/ppermute | solution.py:59
  154.0 5.9 %up_rows.3 = (bf16[96,384]{1,0:T(8,128)(2,1)S(1)}, bf16[96,384]{1,0:T(8,128)(2,1)S(1)}, bf16[96,384]{1,0:T(8,128)(2,1)S(1)}, bf16[96,384]{1,0:T(8,128)(2,1)S(1)}) custom-call(bf16[8,96,512]{2,1,0:T(8,128)(2,1)S(1)} %rows_by_piece.3.refs_4_.own, bf16[8,96,512]{2,1,0:T(8,128)(2,1)} %collective-permute-done.20.back, ...), custom_call_target="tpu_custom_call" | custom-call | tf_op jit(solution)/shard_map/up_rows/pallas_call | solution.py:213
  163.2 2.8 %collective-permute-done.25.refs_2_ = bf16[96,384]{1,0:T(8,128)(2,1)S(1)} collective-permute-done((bf16[96,384]{1,0:T(8,128)(2,1)S(1)}, bf16[96,384]{1,0:T(8,128)(2,1)S(1)}, u32[]{:S(2)}, u32[]{:S(2)}) %collective-permute-start.25) | collective-permute-done | bytes 73760 | tf_op jit(solution)/shard_map/ppermute | solution.py:59
  166.5 6.9 %down_rows.3 = bf16[768,512]{1,0:T(8,128)(2,1)S(1)} custom-call(bf16[96,384]{1,0:T(8,128)(2,1)S(1)} %get-tuple-element.32.refs_0_, bf16[96,384]{1,0:T(8,128)(2,1)S(1)} %collective-permute-done.24.refs_1_, bf16[96,384]{1,0:T(8,128)(2,1)S(1)} %collective-permute-done.25.refs_2_, bf16[96,384]{1,0:T(8,128)(2,1)S(1)} %collective-permute-done.26.refs_3_, ...), custom_call_target="tpu_custom_call" | custom-call | tf_op jit(solution)/shard_map/down_rows/pallas_call | solution.py:257
  174.2 9.6 %all-to-all-start.3 = ((bf16[32,24,512]{2,1,0:T(8,128)(2,1)}), bf16[32,24,512]{2,1,0:T(8,128)(2,1)}, u32[]{:S(2)}, u32[]{:S(2)}) async-start(bf16[32,24,512]{2,1,0:T(8,128)(2,1)} %bitcast.65), calls=%async_computation.3 | async-start | bytes 1572864 | tf_op jit(solution)/shard_map/all_to_all | solution.py:407
  185.4 14.3 %collective-permute-done.5.ahead = bf16[8,96,512]{2,1,0:T(8,128)(2,1)S(1)} collective-permute-done((bf16[8,96,512]{2,1,0:T(8,128)(2,1)S(1)}, bf16[8,96,512]{2,1,0:T(8,128)(2,1)S(1)}, u32[]{:S(2)}, u32[]{:S(2)}) %collective-permute-start.5) | collective-permute-done | bytes 786464 | tf_op jit(solution)/shard_map/ppermute | solution.py:59
  199.7 2.5 collective-permute-start.7
  202.5 5.0 %collective-permute-done.7.far_high = bf16[4,96,512]{2,1,0:T(8,128)(2,1)S(1)} collective-permute-done((bf16[4,96,512]{2,1,0:T(8,128)(2,1)S(1)}, bf16[4,96,512]{2,1,0:T(8,128)(2,1)S(1)}, u32[]{:S(2)}, u32[]{:S(2)}) %collective-permute-start.7) | collective-permute-done | bytes 393248 | tf_op jit(solution)/shard_map/ppermute | solution.py:59
  207.5 2.8 %collective-permute-done.6.far_low = bf16[4,96,512]{2,1,0:T(8,128)(2,1)S(1)} collective-permute-done((bf16[4,96,512]{2,1,0:T(8,128)(2,1)S(1)}, bf16[4,96,512]{2,1,0:T(8,128)(2,1)S(1)}, u32[]{:S(2)}, u32[]{:S(2)}) %collective-permute-start.6) | collective-permute-done | bytes 393248 | tf_op jit(solution)/shard_map/ppermute | solution.py:59
  210.4 5.6 %up_rows.2 = (bf16[96,384]{1,0:T(8,128)(2,1)S(1)}, bf16[96,384]{1,0:T(8,128)(2,1)S(1)}, bf16[96,384]{1,0:T(8,128)(2,1)S(1)}, bf16[96,384]{1,0:T(8,128)(2,1)S(1)}) custom-call(bf16[8,96,512]{2,1,0:T(8,128)(2,1)S(1)} %rows_by_piece.2.own.refs_4_, bf16[8,96,512]{2,1,0:T(8,128)(2,1)S(1)} %collective-permute-done.4.back, ...), custom_call_target="tpu_custom_call" | custom-call | tf_op jit(solution)/shard_map/up_rows/pallas_call | solution.py:213
  221.6 6.8 %down_rows.2 = bf16[768,512]{1,0:T(8,128)(2,1)S(1)} custom-call(bf16[96,384]{1,0:T(8,128)(2,1)S(1)} %get-tuple-element.28.refs_0_, bf16[96,384]{1,0:T(8,128)(2,1)S(1)} %collective-permute-done.10.refs_1_, bf16[96,384]{1,0:T(8,128)(2,1)S(1)} %collective-permute-done.11.refs_2_, bf16[96,384]{1,0:T(8,128)(2,1)S(1)} %collective-permute-done.12.refs_3_, ...), custom_call_target="tpu_custom_call" | custom-call | tf_op jit(solution)/shard_map/down_rows/pallas_call | solution.py:257
  228.5 24.0 %all_to_all.44 = bf16[32,24,512]{2,1,0:T(8,128)(2,1)S(1)} all-to-all(bf16[32,24,512]{2,1,0:T(8,128)(2,1)S(1)} %bitcast.66), channel_id=1, replica_groups=mesh['expert'=32,'tensor'=8] {'expert'}, dimensions={0} | all-to-all | bytes 1572864 | tf_op jit(solution)/shard_map/all_to_all | solution.py:407
  258.6 2.8 collective-permute-done.28
  262.9 10.4 %collective-permute-start.30 = (bf16[4,144,512]{2,1,0:T(8,128)(2,1)S(1)}, bf16[4,144,512]{2,1,0:T(8,128)(2,1)S(1)}, u32[]{:S(2)}, u32[]{:S(2)}) collective-permute-start(bf16[4,144,512]{2,1,0:T(8,128)(2,1)S(1)} %pad_maximum_fusion.same_core), channel_id=1, source_target_pairs={{0,1},{1,0},{2,3},{3,2},{4,5},{5,4},{6,7},{7,6},{8,9},{9,8},{10,11... | collective-permute-start | bytes 1769480 | tf_op jit(solution)/shard_map/ppermute | solution.py:63
  (136 shorter events, 64.9 us)
Async XLA Ops:
  10.1 49.4 %collective-permute-start.8 = (bf16[192,4096]{1,0:T(8,128)(2,1)S(1)}, bf16[192,4096]{1,0:T(8,128)(2,1)}, u32[]{:S(2)}, u32[]{:S(2)}) collective-permute-start(bf16[192,4096]{1,0:T(8,128)(2,1)S(1)} %bitcast.59), channel_id=1, source_target_pairs={{0,1},{1,0},{2,3},{3,2},{4,5},{5,4},{6,7},{7,6},{8,9},{9,8},{10,11... | collective-permute-start | bytes 4718600 | tf_op jit(solution)/shard_map/ppermute | solution.py:63
  13.8 6.4 %collective-permute-start.1 = (bf16[16,4096]{1,0:T(8,128)(2,1)S(1)}, bf16[16,4096]{1,0:T(8,128)(2,1)S(1)}, u32[]{:S(2)}, u32[]{:S(2)}) collective-permute-start(bf16[16,4096]{1,0:T(8,128)(2,1)S(1)} %get-tuple-element.23), channel_id=1, source_target_pairs={{0,2},{1,3},{2,4},{3,5},{4,6},{5,7},{6,0},{7,1},{8,10},{9,11},{10,... | collective-permute-start | bytes 393224 | tf_op jit(solution)/shard_map/ppermute | solution.py:59
  13.8 8.2 %collective-permute-start.2 = (bf16[16,4096]{1,0:T(8,128)(2,1)S(1)}, bf16[16,4096]{1,0:T(8,128)(2,1)S(1)}, u32[]{:S(2)}, u32[]{:S(2)}) collective-permute-start(bf16[16,4096]{1,0:T(8,128)(2,1)S(1)} %get-tuple-element.24), channel_id=1, source_target_pairs={{0,4},{1,5},{2,6},{3,7},{4,0},{5,1},{6,2},{7,3},{8,12},{9,13},{10,... | collective-permute-start | bytes 393224 | tf_op jit(solution)/shard_map/ppermute | solution.py:59
  16.0 6.8 %collective-permute-start.3 = (bf16[16,4096]{1,0:T(8,128)(2,1)S(1)}, bf16[16,4096]{1,0:T(8,128)(2,1)S(1)}, u32[]{:S(2)}, u32[]{:S(2)}) collective-permute-start(bf16[16,4096]{1,0:T(8,128)(2,1)S(1)} %get-tuple-element.25), channel_id=1, source_target_pairs={{0,6},{1,7},{2,0},{3,1},{4,2},{5,3},{6,4},{7,5},{8,14},{9,15},{10,... | collective-permute-start | bytes 393224 | tf_op jit(solution)/shard_map/ppermute | solution.py:59
  27.6 31.1 %all-to-all-start.1 = ((bf16[32,24,512]{2,1,0:T(8,128)(2,1)}), bf16[32,24,512]{2,1,0:T(8,128)(2,1)S(1)}, u32[]{:S(2)}, u32[]{:S(2)}) async-start(bf16[32,24,512]{2,1,0:T(8,128)(2,1)} %bitcast.68), calls=%async_computation.1 | async-start | bytes 1572864 | tf_op jit(solution)/shard_map/all_to_all | solution.py:395
  37.9 24.1 %collective-permute-start.9 = (bf16[192,4096]{1,0:T(8,128)(2,1)}, bf16[192,4096]{1,0:T(8,128)(2,1)}, u32[]{:S(2)}, u32[]{:S(2)}) collective-permute-start(bf16[192,4096]{1,0:T(8,128)(2,1)} %bitcast.26.refs_2_), channel_id=1, source_target_pairs={{0,1},{1,0},{2,3},{3,2},{4,5},{5,4},{6,7},{7,6},{8,9},{9,8},{10,11... | collective-permute-start | bytes 4718600 | tf_op jit(solution)/shard_map/ppermute | solution.py:63
  39.5 37.4 %collective-permute-start.18 = (bf16[192,4096]{1,0:T(8,128)(2,1)}, bf16[192,4096]{1,0:T(8,128)(2,1)}, u32[]{:S(2)}, u32[]{:S(2)}) collective-permute-start(bf16[192,4096]{1,0:T(8,128)(2,1)} %bitcast.30.refs_4_), channel_id=1, source_target_pairs={{0,2},{1,3},{2,4},{3,5},{4,6},{5,7},{6,0},{7,1},{8,10},{9,11},{10,... | collective-permute-start | bytes 4718600 | tf_op jit(solution)/shard_map/ppermute | solution.py:59
  40.5 71.2 %collective-permute-start.16 = (bf16[192,4096]{1,0:T(8,128)(2,1)}, bf16[192,4096]{1,0:T(8,128)(2,1)}, u32[]{:S(2)}, u32[]{:S(2)}) collective-permute-start(bf16[192,4096]{1,0:T(8,128)(2,1)} %bitcast.30.refs_4_), channel_id=1, source_target_pairs={{0,4},{1,5},{2,6},{3,7},{4,0},{5,1},{6,2},{7,3},{8,12},{9,13},{10,... | collective-permute-start | bytes 4718600 | tf_op jit(solution)/shard_map/ppermute | solution.py:59
  42.6 79.6 %collective-permute-start.14 = (bf16[192,4096]{1,0:T(8,128)(2,1)}, bf16[192,4096]{1,0:T(8,128)(2,1)}, u32[]{:S(2)}, u32[]{:S(2)}) collective-permute-start(bf16[192,4096]{1,0:T(8,128)(2,1)} %bitcast.30.refs_4_), channel_id=1, source_target_pairs={{0,6},{1,7},{2,0},{3,1},{4,2},{5,3},{6,4},{7,5},{8,14},{9,15},{10,... | collective-permute-start | bytes 4718600 | tf_op jit(solution)/shard_map/ppermute | solution.py:59
  59.5 68.3 %collective-permute-start.21 = (bf16[8,96,512]{2,1,0:T(8,128)(2,1)S(1)}, bf16[8,96,512]{2,1,0:T(8,128)(2,1)}, u32[]{:S(2)}, u32[]{:S(2)}) collective-permute-start(bf16[8,96,512]{2,1,0:T(8,128)(2,1)S(1)} %rows_by_piece.3.refs_4_.own), channel_id=1, source_target_pairs={{0,6},{1,7},{2,0},{3,1},{4,2},{5,3},{6,4},{7,5},{8,14},{9,15},{10,... | collective-permute-start | bytes 2359304 | tf_op jit(solution)/shard_map/ppermute | solution.py:59
  61.9 68.1 %collective-permute-start.20 = (bf16[8,96,512]{2,1,0:T(8,128)(2,1)S(1)}, bf16[8,96,512]{2,1,0:T(8,128)(2,1)}, u32[]{:S(2)}, u32[]{:S(2)}) collective-permute-start(bf16[8,96,512]{2,1,0:T(8,128)(2,1)S(1)} %rows_by_piece.3.refs_4_.own), channel_id=1, source_target_pairs={{0,2},{1,3},{2,4},{3,5},{4,6},{5,7},{6,0},{7,1},{8,10},{9,11},{10,... | collective-permute-start | bytes 2359304 | tf_op jit(solution)/shard_map/ppermute | solution.py:59
  76.9 84.3 %collective-permute-start.13 = (bf16[192,4096]{1,0:T(8,128)(2,1)}, bf16[192,4096]{1,0:T(8,128)(2,1)}, u32[]{:S(2)}, u32[]{:S(2)}) collective-permute-start(bf16[192,4096]{1,0:T(8,128)(2,1)} %bitcast.30.refs_4_), channel_id=1, source_target_pairs={{0,1},{1,0},{2,3},{3,2},{4,5},{5,4},{6,7},{7,6},{8,9},{9,8},{10,11... | collective-permute-start | bytes 4718600 | tf_op jit(solution)/shard_map/ppermute | solution.py:63
  111.7 49.5 %collective-permute-start.19 = (bf16[192,4096]{1,0:T(8,128)(2,1)}, bf16[192,4096]{1,0:T(8,128)(2,1)}, u32[]{:S(2)}, u32[]{:S(2)}) collective-permute-start(bf16[192,4096]{1,0:T(8,128)(2,1)} %collective-permute-done.18.refs_10_), channel_id=1, source_target_pairs={{0,1},{1,0},{2,3},{3,2},{4,5},{5,4},{6,7},{7,6},{8,9},{9,8},{10,11... | collective-permute-start | bytes 4718600 | tf_op jit(solution)/shard_map/ppermute | solution.py:63
  112.5 31.8 %all-to-all-start = ((bf16[32,24,512]{2,1,0:T(8,128)(2,1)}), bf16[32,24,512]{2,1,0:T(8,128)(2,1)S(1)}, u32[]{:S(2)}, u32[]{:S(2)}) async-start(bf16[32,24,512]{2,1,0:T(8,128)(2,1)} %bitcast.67), calls=%async_computation | async-start | bytes 1572864 | tf_op jit(solution)/shard_map/all_to_all | solution.py:395
  122.2 39.6 %collective-permute-start.17 = (bf16[192,4096]{1,0:T(8,128)(2,1)}, bf16[192,4096]{1,0:T(8,128)(2,1)}, u32[]{:S(2)}, u32[]{:S(2)}) collective-permute-start(bf16[192,4096]{1,0:T(8,128)(2,1)} %collective-permute-done.16.refs_8_), channel_id=1, source_target_pairs={{0,1},{1,0},{2,3},{3,2},{4,5},{5,4},{6,7},{7,6},{8,9},{9,8},{10,11... | collective-permute-start | bytes 4718600 | tf_op jit(solution)/shard_map/ppermute | solution.py:63
  127.8 34.1 %collective-permute-start.15 = (bf16[192,4096]{1,0:T(8,128)(2,1)}, bf16[192,4096]{1,0:T(8,128)(2,1)}, u32[]{:S(2)}, u32[]{:S(2)}) collective-permute-start(bf16[192,4096]{1,0:T(8,128)(2,1)} %collective-permute-done.14.refs_6_), channel_id=1, source_target_pairs={{0,1},{1,0},{2,3},{3,2},{4,5},{5,4},{6,7},{7,6},{8,9},{9,8},{10,11... | collective-permute-start | bytes 4718600 | tf_op jit(solution)/shard_map/ppermute | solution.py:63
  130.0 10.9 %collective-permute-start.23 = (bf16[4,96,512]{2,1,0:T(8,128)(2,1)S(1)}, bf16[4,96,512]{2,1,0:T(8,128)(2,1)S(1)}, u32[]{:S(2)}, u32[]{:S(2)}) collective-permute-start(bf16[4,96,512]{2,1,0:T(8,128)(2,1)S(1)} %slice.99), channel_id=1, source_target_pairs={{0,6},{1,7},{2,0},{3,1},{4,2},{5,3},{6,4},{7,5},{8,14},{9,15},{10,... | collective-permute-start | bytes 1179656 | tf_op jit(solution)/shard_map/ppermute | solution.py:59
  141.7 12.3 %collective-permute-start.22 = (bf16[4,96,512]{2,1,0:T(8,128)(2,1)}, bf16[4,96,512]{2,1,0:T(8,128)(2,1)}, u32[]{:S(2)}, u32[]{:S(2)}) collective-permute-start(bf16[4,96,512]{2,1,0:T(8,128)(2,1)} %slice.98), channel_id=1, source_target_pairs={{0,2},{1,3},{2,4},{3,5},{4,6},{5,7},{6,0},{7,1},{8,10},{9,11},{10,... | collective-permute-start | bytes 1179656 | tf_op jit(solution)/shard_map/ppermute | solution.py:59
  174.2 54.3 %all-to-all-start.3 = ((bf16[32,24,512]{2,1,0:T(8,128)(2,1)}), bf16[32,24,512]{2,1,0:T(8,128)(2,1)}, u32[]{:S(2)}, u32[]{:S(2)}) async-start(bf16[32,24,512]{2,1,0:T(8,128)(2,1)} %bitcast.65), calls=%async_computation.3 | async-start | bytes 1572864 | tf_op jit(solution)/shard_map/all_to_all | solution.py:407
  183.8 15.8 %collective-permute-start.5 = (bf16[8,96,512]{2,1,0:T(8,128)(2,1)S(1)}, bf16[8,96,512]{2,1,0:T(8,128)(2,1)S(1)}, u32[]{:S(2)}, u32[]{:S(2)}) collective-permute-start(bf16[8,96,512]{2,1,0:T(8,128)(2,1)S(1)} %rows_by_piece.2.own.refs_4_), channel_id=1, source_target_pairs={{0,6},{1,7},{2,0},{3,1},{4,2},{5,3},{6,4},{7,5},{8,14},{9,15},{10,... | collective-permute-start | bytes 2359304 | tf_op jit(solution)/shard_map/ppermute | solution.py:59
  184.8 17.4 %collective-permute-start.4 = (bf16[8,96,512]{2,1,0:T(8,128)(2,1)S(1)}, bf16[8,96,512]{2,1,0:T(8,128)(2,1)S(1)}, u32[]{:S(2)}, u32[]{:S(2)}) collective-permute-start(bf16[8,96,512]{2,1,0:T(8,128)(2,1)S(1)} %rows_by_piece.2.own.refs_4_), channel_id=1, source_target_pairs={{0,2},{1,3},{2,4},{3,5},{4,6},{5,7},{6,0},{7,1},{8,10},{9,11},{10,... | collective-permute-start | bytes 2359304 | tf_op jit(solution)/shard_map/ppermute | solution.py:59
  199.7 7.8 %collective-permute-start.7 = (bf16[4,96,512]{2,1,0:T(8,128)(2,1)S(1)}, bf16[4,96,512]{2,1,0:T(8,128)(2,1)S(1)}, u32[]{:S(2)}, u32[]{:S(2)}) collective-permute-start(bf16[4,96,512]{2,1,0:T(8,128)(2,1)S(1)} %slice.97), channel_id=1, source_target_pairs={{0,6},{1,7},{2,0},{3,1},{4,2},{5,3},{6,4},{7,5},{8,14},{9,15},{10,... | collective-permute-start | bytes 1179656 | tf_op jit(solution)/shard_map/ppermute | solution.py:59
  202.2 8.1 %collective-permute-start.6 = (bf16[4,96,512]{2,1,0:T(8,128)(2,1)S(1)}, bf16[4,96,512]{2,1,0:T(8,128)(2,1)S(1)}, u32[]{:S(2)}, u32[]{:S(2)}) collective-permute-start(bf16[4,96,512]{2,1,0:T(8,128)(2,1)S(1)} %slice.96), channel_id=1, source_target_pairs={{0,2},{1,3},{2,4},{3,5},{4,6},{5,7},{6,0},{7,1},{8,10},{9,11},{10,... | collective-permute-start | bytes 1179656 | tf_op jit(solution)/shard_map/ppermute | solution.py:59
  262.9 12.0 %collective-permute-start.30 = (bf16[4,144,512]{2,1,0:T(8,128)(2,1)S(1)}, bf16[4,144,512]{2,1,0:T(8,128)(2,1)S(1)}, u32[]{:S(2)}, u32[]{:S(2)}) collective-permute-start(bf16[4,144,512]{2,1,0:T(8,128)(2,1)S(1)} %pad_maximum_fusion.same_core), channel_id=1, source_target_pairs={{0,1},{1,0},{2,3},{3,2},{4,5},{5,4},{6,7},{7,6},{8,9},{9,8},{10,11... | collective-permute-start | bytes 1769480 | tf_op jit(solution)/shard_map/ppermute | solution.py:63
  (31 other events, 218.0 us)

commit v4 on v3

--- a/solution.py
+++ b/solution.py
@@ -53,6 +53,15 @@
 def along(x, shift):
     pairs = [
         (2 * chip + core, 2 * ((chip + shift) % CHIPS) + core)
+        for chip in range(CHIPS)
+        for core in range(2)
+    ]
+    return lax.ppermute(x, "tensor", pairs)
+
+
+def around(x, sign):
+    pairs = [
+        (2 * chip + core, 2 * ((chip + (sign if core == 0 else -sign)) % CHIPS) + core)
         for chip in range(CHIPS)
         for core in range(2)
     ]
@@ -179,19 +188,18 @@
     )(x, order)
 
 
-def up_kernel(own, back, ahead, far_low, far_high, *refs):
-    gate_own, gate_other, up_own, up_other, _, *outs, gate, up = refs
+def up_kernel(r0, r1, r2, r3, gate_own, gate_other, up_own, up_other, *refs):
+    *outs, gate, up = refs
     step = pl.program_id(0)
-    width = own.shape[2]
+    width = r0.shape[2]
 
     @pl.when(step == 0)
     def _():
         gate[...] = jnp.zeros_like(gate)
         up[...] = jnp.zeros_like(up)
 
-    for q in range(own.shape[0]):
-        far = jnp.where(step == 0, far_low[q], far_high[q])
-        x = jnp.concatenate([own[q], back[q], far, ahead[q]], axis=0)
+    for q in range(r0.shape[0]):
+        x = jnp.concatenate([r0[q], r1[q], r2[q], r3[q]], axis=0)
         at = slice(q * width, (q + 1) * width)
         gate[...] += dot_last(x, jnp.concatenate([gate_own[:, at], gate_other[:, at]], axis=0))
         up[...] += dot_last(x, jnp.concatenate([up_own[:, at], up_other[:, at]], axis=0))
@@ -205,24 +213,22 @@
             outs[i][...] = hidden[i * rows : (i + 1) * rows, :]
 
 
-def up_rows(own, back, ahead, far, weights, after):
-    pieces, rows, width = own.shape
+def up_rows(sources, weights):
+    pieces, rows, width = sources[0].shape
     half = pieces // 2
     units = weights[0].shape[0]
     out = jax.ShapeDtypeStruct((rows, 2 * units), bf16)
     return pl.pallas_call(
         up_kernel,
         grid=(2,),
-        in_specs=[pl.BlockSpec((half, rows, width), lambda j: (j, 0, 0))] * 3
-        + [pl.BlockSpec((half, rows, width), lambda j: (0, 0, 0))] * 2
-        + [pl.BlockSpec((units, half * width), lambda j: (0, j))] * 4
-        + [pl.BlockSpec(memory_space=pl.ANY)],
+        in_specs=[pl.BlockSpec((half, rows, width), lambda j: (j, 0, 0))] * CHIPS
+        + [pl.BlockSpec((units, half * width), lambda j: (0, j))] * 4,
         out_specs=[pl.BlockSpec((rows, 2 * units), lambda j: (0, 0))] * CHIPS,
         out_shape=(out,) * CHIPS,
         scratch_shapes=[pltpu.VMEM((CHIPS * rows, 2 * units), f32)] * 2,
         compiler_params=space(15),
         name="up_rows",
-    )(own, back, ahead, *far, *weights, after)
+    )(*sources, *weights)
 
 
 def down_kernel(*refs):
@@ -372,7 +378,8 @@
     capacity = min(rows, max(2, 3 * rows * top_count // (2 * expert_count)))
     slots = capacity // HALVES
 
-    same_core = [w_down[0]] + [along(w_down[0], shift) for shift in range(1, CHIPS)]
+    down_next = around(w_down[0], 1)
+    down_far, down_last = around(down_next, 1), around(w_down[0], -1)
     gate_own, up_own = w_gate[0].T, w_up[0].T
     weights = (gate_own, across(gate_own), up_own, across(up_own))
     order = reorder_matrix(PIECES, BATCH, slots)
@@ -383,10 +390,16 @@
     mine, theirs = project(place, attn_out, o_weight)
     sums = pair_sums(mine, across(theirs))
     parts = (sums[0],) + tuple(along(sums[shift], shift) for shift in range(1, CHIPS))
-    down_weights = []
-    for shift in range(CHIPS):
-        weight = same_core[-shift % CHIPS]
-        down_weights += [weight, across(weight)]
+    down_weights = [
+        w_down[0],
+        across(w_down[0]),
+        down_next,
+        across(down_last),
+        down_far,
+        across(down_far),
+        down_last,
+        across(down_next),
+    ]
     outbox0, outbox1, stream, logits = front(
         place, parts, residual, norm_gain.reshape(1, width), router_weight.T, shares, order
     )
@@ -397,11 +410,17 @@
     for x in arrived:
         own.append(rows_by_piece(x, order))
     returned = []
-    for half, mine in enumerate(own):
-        back, ahead = along(mine, 1), along(mine, -1)
-        far = (along(back[: PIECES // 2], 1), along(ahead[PIECES // 2 :], -1))
-        hidden = up_rows(mine, back, ahead, far, weights, own[1 - half])
-        units = (hidden[0],) + tuple(along(hidden[s], -s) for s in range(1, CHIPS))
+    for mine in own:
+        following = around(mine, 1)
+        last = around(mine, -1)
+        far = around(following, 1)
+        hidden = up_rows((mine, following, far, last), weights)
+        units = (
+            hidden[0],
+            around(hidden[3], 1),
+            along(hidden[2], 2),
+            around(hidden[1], -1),
+        )
         expert_out = down_rows(units, down_weights, order)
         returned.append(
             lax.all_to_all(expert_out, "expert", split_axis=0, concat_axis=0, tiled=True)

time: 278 us -> 240 us (0.86)
  starting transfers between devices: 106 us -> 68 us
  local copies, waits for them, and re-layouts: 14.4 us -> 9.95 us
  blocking collectives: 24 us -> 27.2 us
    ppermute x0 -> x13, waiting for transfers between devices: none -> 52.1 us  [around(): return lax.ppermute(x, 'tensor', pairs)]
    ppermute x23 -> x8, waiting for transfers between devices: 75.7 us -> 27.5 us  [along(): return lax.ppermute(x, 'tensor', pairs)]
    ppermute x8, starting transfers between devices: 52.5 us -> 16 us  [across(): return lax.ppermute(x, 'tensor', [(r, r ^ 1) for r in range(2 * CHIPS)])]
    ppermute x0 -> x13, starting transfers between devices: none -> 21.6 us  [around(): return lax.ppermute(x, 'tensor', pairs)]
    ppermute x23 -> x8, starting transfers between devices: 24.2 us -> 5.5 us  [along(): return lax.ppermute(x, 'tensor', pairs)]
    all_to_all x2, starting transfers between devices: 19.9 us -> 15.5 us  [shards(): lax.all_to_all(outbox, 'expert', split_axis=0, concat_axis=0, tiled=True)]
    all_to_all x2, waiting for transfers between devices: 16.2 us -> 12.7 us  [shards(): lax.all_to_all(outbox, 'expert', split_axis=0, concat_axis=0, tiled=True)]
    pallas_call x2, Pallas kernels: 1.55 us -> 5.02 us  [rows_by_piece(): pl.pallas_call(by_piece_kernel, grid=(steps,), in_specs=[pl.BlockSpec((si...]
  transfers between devices with their start and end apart: 34 -> 32, of which waited for: 22 -> 19; matrix products, arithmetic and copies ran while one was open for 2% -> 1% of each run, Pallas kernels for 8% -> 13%
where the time goes in v4:
time: 240 us; the launch traced here: 239 us
  waiting for transfers between devices  93.9 us (39%)
  starting transfers between devices  68 us (28%)
  Pallas kernels  37 us (15%)
  blocking collectives  27.2 us (11%)
  local copies, waits for them, and re-layouts  9.95 us (4%)
    ppermute x13, waiting for transfers between devices, around(): return lax.ppermute(x, 'tensor', pairs)  52.1 us
    ppermute x8, waiting for transfers between devices, along(): return lax.ppermute(x, 'tensor', pairs)  27.5 us
    all_to_all x1, blocking collectives, shards(): lax.all_to_all(expert_out, 'expert', split_axis=0, concat_axis=0, tiled=T...  27.2 us
    ppermute x13, starting transfers between devices, around(): return lax.ppermute(x, 'tensor', pairs)  21.6 us
    ppermute x8, starting transfers between devices, across(): return lax.ppermute(x, 'tensor', [(r, r ^ 1) for r in range(2 * CHIPS)])  16 us
    all_to_all x2, starting transfers between devices, shards(): lax.all_to_all(outbox, 'expert', split_axis=0, concat_axis=0, tiled=True)  15.5 us
    pallas_call x2, Pallas kernels, down_rows(): pl.pallas_call(down_kernel, grid=(steps,), in_specs=[pl.BlockSpec((rows,...  13.7 us
    all_to_all x2, waiting for transfers between devices, shards(): lax.all_to_all(outbox, 'expert', split_axis=0, concat_axis=0, tiled=True)  12.7 us
  transfers between devices with their start and end apart: 32, of which 19 were waited for; matrix products, arithmetic and copies ran while one was open for 1% of the time, Pallas kernels for 13%

profile of v4, /device:TPU:1, one launch (start us, length us, event | category | flops | bytes accessed | tf_op | source)
XLA Modules:
  0.0 239.3 jit_solution(6832545251712776142)
XLA Ops:
  6.0 3.3 %collective-permute-start = (bf16[4,16,4096]{2,1,0:T(8,128)(2,1)S(1)}, bf16[4,16,4096]{2,1,0:T(8,128)(2,1)S(1)}, u32[]{:S(2)}, u32[]{:S(2)}) collective-permute-start(bf16[4,16,4096]{2,1,0:T(8,128)(2,1)S(1)} %get-tuple-element.21), channel_id=1, source_target_pairs={{0,1},{1,0},{2,3},{3,2},{4,5},{5,4},{6,7},{7,6},{8,9},{9,8},{10,11... | collective-permute-start | bytes 1572872 | tf_op jit(solution)/shard_map/ppermute | solution.py:72
  16.4 4.2 %collective-permute-done.1.p1 = bf16[16,4096]{1,0:T(8,128)(2,1)S(1)} collective-permute-done((bf16[16,4096]{1,0:T(8,128)(2,1)S(1)}, bf16[16,4096]{1,0:T(8,128)(2,1)S(1)}, u32[]{:S(2)}, u32[]{:S(2)}) %collective-permute-start.1) | collective-permute-done | bytes 131104 | tf_op jit(solution)/shard_map/ppermute | solution.py:59
  21.0 13.8 %collective-permute-done.3.p3 = bf16[16,4096]{1,0:T(8,128)(2,1)S(1)} collective-permute-done((bf16[16,4096]{1,0:T(8,128)(2,1)S(1)}, bf16[16,4096]{1,0:T(8,128)(2,1)S(1)}, u32[]{:S(2)}, u32[]{:S(2)}) %collective-permute-start.3) | collective-permute-done | bytes 131104 | tf_op jit(solution)/shard_map/ppermute | solution.py:59
  40.7 9.9 %all-to-all-start.2 = ((bf16[32,24,512]{2,1,0:T(8,128)(2,1)}), bf16[32,24,512]{2,1,0:T(8,128)(2,1)}, u32[]{:S(2)}, u32[]{:S(2)}) async-start(bf16[32,24,512]{2,1,0:T(8,128)(2,1)} %bitcast.69), calls=%async_computation.2 | async-start | bytes 1572864 | tf_op jit(solution)/shard_map/all_to_all | solution.py:408
  50.7 3.2 %collective-permute-start.7 = (bf16[192,4096]{1,0:T(8,128)(2,1)S(1)}, bf16[192,4096]{1,0:T(8,128)(2,1)}, u32[]{:S(2)}, u32[]{:S(2)}) collective-permute-start(bf16[192,4096]{1,0:T(8,128)(2,1)S(1)} %bitcast.59), channel_id=1, source_target_pairs={{0,1},{1,0},{2,3},{3,2},{4,5},{5,4},{6,7},{7,6},{8,9},{9,8},{10,11... | collective-permute-start | bytes 4718600 | tf_op jit(solution)/shard_map/ppermute | solution.py:72
  54.0 2.7 %collective-permute-start.16 = (bf16[192,4096]{1,0:T(8,128)(2,1)}, bf16[192,4096]{1,0:T(8,128)(2,1)}, u32[]{:S(2)}, u32[]{:S(2)}) collective-permute-start(bf16[192,4096]{1,0:T(8,128)(2,1)} %collective-permute-done.13.refs_6_), channel_id=1, source_target_pairs={{0,2},{1,7},{2,4},{3,1},{4,6},{5,3},{6,0},{7,5},{8,10},{9,15},{10,... | collective-permute-start | bytes 4718600 | tf_op jit(solution)/shard_map/ppermute | solution.py:68
  56.7 12.7 %all-to-all-done.2 = bf16[32,24,512]{2,1,0:T(8,128)(2,1)} async-done(((bf16[32,24,512]{2,1,0:T(8,128)(2,1)}), bf16[32,24,512]{2,1,0:T(8,128)(2,1)}, u32[]{:S(2)}, u32[]{:S(2)}) %all-to-all-start.2) | async-done | bytes 786464 | tf_op jit(solution)/shard_map/all_to_all | solution.py:408
  71.9 4.1 %collective-permute-start.21 = (bf16[8,96,512]{2,1,0:T(8,128)(2,1)}, bf16[8,96,512]{2,1,0:T(8,128)(2,1)}, u32[]{:S(2)}, u32[]{:S(2)}) collective-permute-start(bf16[8,96,512]{2,1,0:T(8,128)(2,1)} %rows_by_piece.3.r0), channel_id=1, source_target_pairs={{0,6},{1,3},{2,0},{3,5},{4,2},{5,7},{6,4},{7,1},{8,14},{9,11},{10,... | collective-permute-start | bytes 2359304 | tf_op jit(solution)/shard_map/ppermute | solution.py:68
  78.3 5.5 %all-to-all-start = ((bf16[32,24,512]{2,1,0:T(8,128)(2,1)}), bf16[32,24,512]{2,1,0:T(8,128)(2,1)}, u32[]{:S(2)}, u32[]{:S(2)}) async-start(bf16[32,24,512]{2,1,0:T(8,128)(2,1)} %bitcast.68), calls=%async_computation | async-start | bytes 1572864 | tf_op jit(solution)/shard_map/all_to_all | solution.py:408
  84.6 6.1 %collective-permute-done.14.refs_10_ = bf16[192,4096]{1,0:T(8,128)(2,1)} collective-permute-done((bf16[192,4096]{1,0:T(8,128)(2,1)}, bf16[192,4096]{1,0:T(8,128)(2,1)}, u32[]{:S(2)}, u32[]{:S(2)}) %collective-permute-start.14) | collective-permute-done | bytes 1572896 | tf_op jit(solution)/shard_map/ppermute | solution.py:68
  92.0 15.6 %collective-permute-done.21.r3 = bf16[8,96,512]{2,1,0:T(8,128)(2,1)} collective-permute-done((bf16[8,96,512]{2,1,0:T(8,128)(2,1)}, bf16[8,96,512]{2,1,0:T(8,128)(2,1)}, u32[]{:S(2)}, u32[]{:S(2)}) %collective-permute-start.21) | collective-permute-done | bytes 786464 | tf_op jit(solution)/shard_map/ppermute | solution.py:68
  112.0 7.6 %collective-permute-done.20.r2 = bf16[8,96,512]{2,1,0:T(8,128)(2,1)} collective-permute-done((bf16[8,96,512]{2,1,0:T(8,128)(2,1)}, bf16[8,96,512]{2,1,0:T(8,128)(2,1)}, u32[]{:S(2)}, u32[]{:S(2)}) %collective-permute-start.20) | collective-permute-done | bytes 786464 | tf_op jit(solution)/shard_map/ppermute | solution.py:68
  121.8 5.8 %up_rows.3 = (bf16[96,384]{1,0:T(8,128)(2,1)S(1)}, bf16[96,384]{1,0:T(8,128)(2,1)S(1)}, bf16[96,384]{1,0:T(8,128)(2,1)S(1)}, bf16[96,384]{1,0:T(8,128)(2,1)S(1)}) custom-call(bf16[8,96,512]{2,1,0:T(8,128)(2,1)} %rows_by_piece.3.r0, bf16[8,96,512]{2,1,0:T(8,128)(2,1)} %collective-permute-done.19.r1, bf16[8,96,512]{2,1,0:T(8,128)(2,1)} %collective-permute-done.20.r2, ...), custom_call_target="tpu_custom_call" | custom-call | tf_op jit(solution)/shard_map/up_rows/pallas_call | solution.py:221
  129.2 3.3 %collective-permute-done.22.refs_1_ = bf16[96,384]{1,0:T(8,128)(2,1)S(1)} collective-permute-done((bf16[96,384]{1,0:T(8,128)(2,1)S(1)}, bf16[96,384]{1,0:T(8,128)(2,1)S(1)}, u32[]{:S(2)}, u32[]{:S(2)}) %collective-permute-start.22) | collective-permute-done | bytes 73760 | tf_op jit(solution)/shard_map/ppermute | solution.py:68
  134.9 6.9 %down_rows.3 = bf16[768,512]{1,0:T(8,128)(2,1)S(1)} custom-call(bf16[96,384]{1,0:T(8,128)(2,1)S(1)} %get-tuple-element.32.refs_0_, bf16[96,384]{1,0:T(8,128)(2,1)S(1)} %collective-permute-done.22.refs_1_, bf16[96,384]{1,0:T(8,128)(2,1)S(1)} %collective-permute-done.23.refs_2_, bf16[96,384]{1,0:T(8,128)(2,1)S(1)} %collective-permute-done.24.refs_3_, ...), custom_call_target="tpu_custom_call" | custom-call | tf_op jit(solution)/shard_map/down_rows/pallas_call | solution.py:263
  142.7 9.4 %all-to-all-start.3 = ((bf16[32,24,512]{2,1,0:T(8,128)(2,1)}), bf16[32,24,512]{2,1,0:T(8,128)(2,1)}, u32[]{:S(2)}, u32[]{:S(2)}) async-start(bf16[32,24,512]{2,1,0:T(8,128)(2,1)} %bitcast.66), calls=%async_computation.3 | async-start | bytes 1572864 | tf_op jit(solution)/shard_map/all_to_all | solution.py:426
  152.3 2.5 %collective-permute-start.5 = (bf16[8,96,512]{2,1,0:T(8,128)(2,1)}, bf16[8,96,512]{2,1,0:T(8,128)(2,1)S(1)}, u32[]{:S(2)}, u32[]{:S(2)}) collective-permute-start(bf16[8,96,512]{2,1,0:T(8,128)(2,1)} %collective-permute-done.4.r1), channel_id=1, source_target_pairs={{0,2},{1,7},{2,4},{3,1},{4,6},{5,3},{6,0},{7,5},{8,10},{9,15},{10,... | collective-permute-start | bytes 2359304 | tf_op jit(solution)/shard_map/ppermute | solution.py:68
  154.9 13.0 %collective-permute-done.6.r3 = bf16[8,96,512]{2,1,0:T(8,128)(2,1)S(1)} collective-permute-done((bf16[8,96,512]{2,1,0:T(8,128)(2,1)}, bf16[8,96,512]{2,1,0:T(8,128)(2,1)S(1)}, u32[]{:S(2)}, u32[]{:S(2)}) %collective-permute-start.6) | collective-permute-done | bytes 786464 | tf_op jit(solution)/shard_map/ppermute | solution.py:68
  170.2 5.5 %up_rows.2 = (bf16[96,384]{1,0:T(8,128)(2,1)S(1)}, bf16[96,384]{1,0:T(8,128)(2,1)S(1)}, bf16[96,384]{1,0:T(8,128)(2,1)S(1)}, bf16[96,384]{1,0:T(8,128)(2,1)S(1)}) custom-call(bf16[8,96,512]{2,1,0:T(8,128)(2,1)} %rows_by_piece.2.r0, bf16[8,96,512]{2,1,0:T(8,128)(2,1)} %collective-permute-done.4.r1, bf16[8,96,512]{2,1,0:T(8,128)(2,1)S(1)} %collective-permute-done.5.r2, ...), custom_call_target="tpu_custom_call" | custom-call | tf_op jit(solution)/shard_map/up_rows/pallas_call | solution.py:221
  175.7 3.7 %collective-permute-start.9 = (bf16[96,384]{1,0:T(8,128)(2,1)S(1)}, bf16[96,384]{1,0:T(8,128)(2,1)S(1)}, u32[]{:S(2)}, u32[]{:S(2)}) collective-permute-start(bf16[96,384]{1,0:T(8,128)(2,1)S(1)} %get-tuple-element.28), channel_id=1, source_target_pairs={{0,2},{1,7},{2,4},{3,1},{4,6},{5,3},{6,0},{7,5},{8,10},{9,15},{10,... | collective-permute-start | bytes 221192 | tf_op jit(solution)/shard_map/ppermute | solution.py:68
  181.5 2.7 %collective-permute-done.10.refs_2_ = bf16[96,384]{1,0:T(8,128)(2,1)S(1)} collective-permute-done((bf16[96,384]{1,0:T(8,128)(2,1)S(1)}, bf16[96,384]{1,0:T(8,128)(2,1)S(1)}, u32[]{:S(2)}, u32[]{:S(2)}) %collective-permute-start.10) | collective-permute-done | bytes 73760 | tf_op jit(solution)/shard_map/ppermute | solution.py:59
  185.4 6.8 %down_rows.2 = bf16[768,512]{1,0:T(8,128)(2,1)S(1)} custom-call(bf16[96,384]{1,0:T(8,128)(2,1)S(1)} %get-tuple-element.27.refs_0_, bf16[96,384]{1,0:T(8,128)(2,1)S(1)} %collective-permute-done.9.refs_1_, bf16[96,384]{1,0:T(8,128)(2,1)S(1)} %collective-permute-done.10.refs_2_, bf16[96,384]{1,0:T(8,128)(2,1)S(1)} %collective-permute-done.11.refs_3_, ...), custom_call_target="tpu_custom_call" | custom-call | tf_op jit(solution)/shard_map/down_rows/pallas_call | solution.py:263
  192.2 27.2 %all_to_all.44 = bf16[32,24,512]{2,1,0:T(8,128)(2,1)S(1)} all-to-all(bf16[32,24,512]{2,1,0:T(8,128)(2,1)S(1)} %bitcast.67), channel_id=1, replica_groups=mesh['expert'=32,'tensor'=8] {'expert'}, dimensions={0} | all-to-all | bytes 1572864 | tf_op jit(solution)/shard_map/all_to_all | solution.py:426
  228.5 6.9 %collective-permute-start.28 = (bf16[4,144,512]{2,1,0:T(8,128)(2,1)S(1)}, bf16[4,144,512]{2,1,0:T(8,128)(2,1)S(1)}, u32[]{:S(2)}, u32[]{:S(2)}) collective-permute-start(bf16[4,144,512]{2,1,0:T(8,128)(2,1)S(1)} %pad_maximum_fusion.same_core), channel_id=1, source_target_pairs={{0,1},{1,0},{2,3},{3,2},{4,5},{5,4},{6,7},{7,6},{8,9},{9,8},{10,11... | collective-permute-start | bytes 1769480 | tf_op jit(solution)/shard_map/ppermute | solution.py:72
  (122 shorter events, 55.7 us)
Async XLA Ops:
  6.0 6.5 %collective-permute-start = (bf16[4,16,4096]{2,1,0:T(8,128)(2,1)S(1)}, bf16[4,16,4096]{2,1,0:T(8,128)(2,1)S(1)}, u32[]{:S(2)}, u32[]{:S(2)}) collective-permute-start(bf16[4,16,4096]{2,1,0:T(8,128)(2,1)S(1)} %get-tuple-element.21), channel_id=1, source_target_pairs={{0,1},{1,0},{2,3},{3,2},{4,5},{5,4},{6,7},{7,6},{8,9},{9,8},{10,11... | collective-permute-start | bytes 1572872 | tf_op jit(solution)/shard_map/ppermute | solution.py:72
  9.3 44.7 %collective-permute-start.13 = (bf16[192,4096]{1,0:T(8,128)(2,1)}, bf16[192,4096]{1,0:T(8,128)(2,1)}, u32[]{:S(2)}, u32[]{:S(2)}) collective-permute-start(bf16[192,4096]{1,0:T(8,128)(2,1)} %bitcast.28.refs_4_), channel_id=1, source_target_pairs={{0,2},{1,7},{2,4},{3,1},{4,6},{5,3},{6,0},{7,5},{8,10},{9,15},{10,... | collective-permute-start | bytes 4718600 | tf_op jit(solution)/shard_map/ppermute | solution.py:68
  12.7 7.9 %collective-permute-start.1 = (bf16[16,4096]{1,0:T(8,128)(2,1)S(1)}, bf16[16,4096]{1,0:T(8,128)(2,1)S(1)}, u32[]{:S(2)}, u32[]{:S(2)}) collective-permute-start(bf16[16,4096]{1,0:T(8,128)(2,1)S(1)} %get-tuple-element.23), channel_id=1, source_target_pairs={{0,2},{1,3},{2,4},{3,5},{4,6},{5,7},{6,0},{7,1},{8,10},{9,11},{10,... | collective-permute-start | bytes 393224 | tf_op jit(solution)/shard_map/ppermute | solution.py:59
  13.2 7.8 %collective-permute-start.2 = (bf16[16,4096]{1,0:T(8,128)(2,1)S(1)}, bf16[16,4096]{1,0:T(8,128)(2,1)S(1)}, u32[]{:S(2)}, u32[]{:S(2)}) collective-permute-start(bf16[16,4096]{1,0:T(8,128)(2,1)S(1)} %get-tuple-element.24), channel_id=1, source_target_pairs={{0,4},{1,5},{2,6},{3,7},{4,0},{5,1},{6,2},{7,3},{8,12},{9,13},{10,... | collective-permute-start | bytes 393224 | tf_op jit(solution)/shard_map/ppermute | solution.py:59
  14.4 20.4 %collective-permute-start.3 = (bf16[16,4096]{1,0:T(8,128)(2,1)S(1)}, bf16[16,4096]{1,0:T(8,128)(2,1)S(1)}, u32[]{:S(2)}, u32[]{:S(2)}) collective-permute-start(bf16[16,4096]{1,0:T(8,128)(2,1)S(1)} %get-tuple-element.25), channel_id=1, source_target_pairs={{0,6},{1,7},{2,0},{3,1},{4,2},{5,3},{6,4},{7,5},{8,14},{9,15},{10,... | collective-permute-start | bytes 393224 | tf_op jit(solution)/shard_map/ppermute | solution.py:59
  40.7 28.6 %all-to-all-start.2 = ((bf16[32,24,512]{2,1,0:T(8,128)(2,1)}), bf16[32,24,512]{2,1,0:T(8,128)(2,1)}, u32[]{:S(2)}, u32[]{:S(2)}) async-start(bf16[32,24,512]{2,1,0:T(8,128)(2,1)} %bitcast.69), calls=%async_computation.2 | async-start | bytes 1572864 | tf_op jit(solution)/shard_map/all_to_all | solution.py:408
  50.7 25.4 %collective-permute-start.7 = (bf16[192,4096]{1,0:T(8,128)(2,1)S(1)}, bf16[192,4096]{1,0:T(8,128)(2,1)}, u32[]{:S(2)}, u32[]{:S(2)}) collective-permute-start(bf16[192,4096]{1,0:T(8,128)(2,1)S(1)} %bitcast.59), channel_id=1, source_target_pairs={{0,1},{1,0},{2,3},{3,2},{4,5},{5,4},{6,7},{7,6},{8,9},{9,8},{10,11... | collective-permute-start | bytes 4718600 | tf_op jit(solution)/shard_map/ppermute | solution.py:72
  53.9 30.0 %collective-permute-start.8 = (bf16[192,4096]{1,0:T(8,128)(2,1)S(1)}, bf16[192,4096]{1,0:T(8,128)(2,1)}, u32[]{:S(2)}, u32[]{:S(2)}) collective-permute-start(bf16[192,4096]{1,0:T(8,128)(2,1)S(1)} %bitcast.62), channel_id=1, source_target_pairs={{0,1},{1,0},{2,3},{3,2},{4,5},{5,4},{6,7},{7,6},{8,9},{9,8},{10,11... | collective-permute-start | bytes 4718600 | tf_op jit(solution)/shard_map/ppermute | solution.py:72
  54.0 36.7 %collective-permute-start.14 = (bf16[192,4096]{1,0:T(8,128)(2,1)}, bf16[192,4096]{1,0:T(8,128)(2,1)}, u32[]{:S(2)}, u32[]{:S(2)}) collective-permute-start(bf16[192,4096]{1,0:T(8,128)(2,1)} %bitcast.28.refs_4_), channel_id=1, source_target_pairs={{0,6},{1,3},{2,0},{3,5},{4,2},{5,7},{6,4},{7,1},{8,14},{9,11},{10,... | collective-permute-start | bytes 4718600 | tf_op jit(solution)/shard_map/ppermute | solution.py:68
  54.0 54.0 %collective-permute-start.16 = (bf16[192,4096]{1,0:T(8,128)(2,1)}, bf16[192,4096]{1,0:T(8,128)(2,1)}, u32[]{:S(2)}, u32[]{:S(2)}) collective-permute-start(bf16[192,4096]{1,0:T(8,128)(2,1)} %collective-permute-done.13.refs_6_), channel_id=1, source_target_pairs={{0,2},{1,7},{2,4},{3,1},{4,6},{5,3},{6,0},{7,5},{8,10},{9,15},{10,... | collective-permute-start | bytes 4718600 | tf_op jit(solution)/shard_map/ppermute | solution.py:68
  71.9 35.7 %collective-permute-start.21 = (bf16[8,96,512]{2,1,0:T(8,128)(2,1)}, bf16[8,96,512]{2,1,0:T(8,128)(2,1)}, u32[]{:S(2)}, u32[]{:S(2)}) collective-permute-start(bf16[8,96,512]{2,1,0:T(8,128)(2,1)} %rows_by_piece.3.r0), channel_id=1, source_target_pairs={{0,6},{1,3},{2,0},{3,5},{4,2},{5,7},{6,4},{7,1},{8,14},{9,11},{10,... | collective-permute-start | bytes 2359304 | tf_op jit(solution)/shard_map/ppermute | solution.py:68
  76.0 32.1 %collective-permute-start.19 = (bf16[8,96,512]{2,1,0:T(8,128)(2,1)}, bf16[8,96,512]{2,1,0:T(8,128)(2,1)}, u32[]{:S(2)}, u32[]{:S(2)}) collective-permute-start(bf16[8,96,512]{2,1,0:T(8,128)(2,1)} %rows_by_piece.3.r0), channel_id=1, source_target_pairs={{0,2},{1,7},{2,4},{3,1},{4,6},{5,3},{6,0},{7,5},{8,10},{9,15},{10,... | collective-permute-start | bytes 2359304 | tf_op jit(solution)/shard_map/ppermute | solution.py:68
  78.3 31.1 %all-to-all-start = ((bf16[32,24,512]{2,1,0:T(8,128)(2,1)}), bf16[32,24,512]{2,1,0:T(8,128)(2,1)}, u32[]{:S(2)}, u32[]{:S(2)}) async-start(bf16[32,24,512]{2,1,0:T(8,128)(2,1)} %bitcast.68), calls=%async_computation | async-start | bytes 1572864 | tf_op jit(solution)/shard_map/all_to_all | solution.py:408
  83.9 43.7 %collective-permute-start.12 = (bf16[192,4096]{1,0:T(8,128)(2,1)}, bf16[192,4096]{1,0:T(8,128)(2,1)}, u32[]{:S(2)}, u32[]{:S(2)}) collective-permute-start(bf16[192,4096]{1,0:T(8,128)(2,1)} %bitcast.28.refs_4_), channel_id=1, source_target_pairs={{0,1},{1,0},{2,3},{3,2},{4,5},{5,4},{6,7},{7,6},{8,9},{9,8},{10,11... | collective-permute-start | bytes 4718600 | tf_op jit(solution)/shard_map/ppermute | solution.py:72
  90.7 37.0 %collective-permute-start.15 = (bf16[192,4096]{1,0:T(8,128)(2,1)}, bf16[192,4096]{1,0:T(8,128)(2,1)}, u32[]{:S(2)}, u32[]{:S(2)}) collective-permute-start(bf16[192,4096]{1,0:T(8,128)(2,1)} %collective-permute-done.14.refs_10_), channel_id=1, source_target_pairs={{0,1},{1,0},{2,3},{3,2},{4,5},{5,4},{6,7},{7,6},{8,9},{9,8},{10,11... | collective-permute-start | bytes 4718600 | tf_op jit(solution)/shard_map/ppermute | solution.py:72
  107.6 21.1 %collective-permute-start.18 = (bf16[192,4096]{1,0:T(8,128)(2,1)}, bf16[192,4096]{1,0:T(8,128)(2,1)}, u32[]{:S(2)}, u32[]{:S(2)}) collective-permute-start(bf16[192,4096]{1,0:T(8,128)(2,1)} %collective-permute-done.13.refs_6_), channel_id=1, source_target_pairs={{0,1},{1,0},{2,3},{3,2},{4,5},{5,4},{6,7},{7,6},{8,9},{9,8},{10,11... | collective-permute-start | bytes 4718600 | tf_op jit(solution)/shard_map/ppermute | solution.py:72
  108.0 26.9 %collective-permute-start.17 = (bf16[192,4096]{1,0:T(8,128)(2,1)}, bf16[192,4096]{1,0:T(8,128)(2,1)}, u32[]{:S(2)}, u32[]{:S(2)}) collective-permute-start(bf16[192,4096]{1,0:T(8,128)(2,1)} %collective-permute-done.16.refs_8_), channel_id=1, source_target_pairs={{0,1},{1,0},{2,3},{3,2},{4,5},{5,4},{6,7},{7,6},{8,9},{9,8},{10,11... | collective-permute-start | bytes 4718600 | tf_op jit(solution)/shard_map/ppermute | solution.py:72
  108.1 11.5 %collective-permute-start.20 = (bf16[8,96,512]{2,1,0:T(8,128)(2,1)}, bf16[8,96,512]{2,1,0:T(8,128)(2,1)}, u32[]{:S(2)}, u32[]{:S(2)}) collective-permute-start(bf16[8,96,512]{2,1,0:T(8,128)(2,1)} %collective-permute-done.19.r1), channel_id=1, source_target_pairs={{0,2},{1,7},{2,4},{3,1},{4,6},{5,3},{6,0},{7,5},{8,10},{9,15},{10,... | collective-permute-start | bytes 2359304 | tf_op jit(solution)/shard_map/ppermute | solution.py:68
  119.6 32.8 %collective-permute-start.4 = (bf16[8,96,512]{2,1,0:T(8,128)(2,1)}, bf16[8,96,512]{2,1,0:T(8,128)(2,1)}, u32[]{:S(2)}, u32[]{:S(2)}) collective-permute-start(bf16[8,96,512]{2,1,0:T(8,128)(2,1)} %rows_by_piece.2.r0), channel_id=1, source_target_pairs={{0,2},{1,7},{2,4},{3,1},{4,6},{5,3},{6,0},{7,5},{8,10},{9,15},{10,... | collective-permute-start | bytes 2359304 | tf_op jit(solution)/shard_map/ppermute | solution.py:68
  142.7 49.6 %all-to-all-start.3 = ((bf16[32,24,512]{2,1,0:T(8,128)(2,1)}), bf16[32,24,512]{2,1,0:T(8,128)(2,1)}, u32[]{:S(2)}, u32[]{:S(2)}) async-start(bf16[32,24,512]{2,1,0:T(8,128)(2,1)} %bitcast.66), calls=%async_computation.3 | async-start | bytes 1572864 | tf_op jit(solution)/shard_map/all_to_all | solution.py:426
  152.1 15.8 %collective-permute-start.6 = (bf16[8,96,512]{2,1,0:T(8,128)(2,1)}, bf16[8,96,512]{2,1,0:T(8,128)(2,1)S(1)}, u32[]{:S(2)}, u32[]{:S(2)}) collective-permute-start(bf16[8,96,512]{2,1,0:T(8,128)(2,1)} %rows_by_piece.2.r0), channel_id=1, source_target_pairs={{0,6},{1,3},{2,0},{3,5},{4,2},{5,7},{6,4},{7,1},{8,14},{9,11},{10,... | collective-permute-start | bytes 2359304 | tf_op jit(solution)/shard_map/ppermute | solution.py:68
  152.3 17.9 %collective-permute-start.5 = (bf16[8,96,512]{2,1,0:T(8,128)(2,1)}, bf16[8,96,512]{2,1,0:T(8,128)(2,1)S(1)}, u32[]{:S(2)}, u32[]{:S(2)}) collective-permute-start(bf16[8,96,512]{2,1,0:T(8,128)(2,1)} %collective-permute-done.4.r1), channel_id=1, source_target_pairs={{0,2},{1,7},{2,4},{3,1},{4,6},{5,3},{6,0},{7,5},{8,10},{9,15},{10,... | collective-permute-start | bytes 2359304 | tf_op jit(solution)/shard_map/ppermute | solution.py:68
  221.4 7.1 %collective-permute-start.25 = (bf16[144,512]{1,0:T(8,128)(2,1)S(1)}, bf16[144,512]{1,0:T(8,128)(2,1)S(1)}, u32[]{:S(2)}, u32[]{:S(2)}) collective-permute-start(bf16[144,512]{1,0:T(8,128)(2,1)S(1)} %finish.1), channel_id=1, source_target_pairs={{0,2},{1,3},{2,4},{3,5},{4,6},{5,7},{6,0},{7,1},{8,10},{9,11},{10,... | collective-permute-start | bytes 442376 | tf_op jit(solution)/shard_map/ppermute | solution.py:59
  228.5 8.5 %collective-permute-start.28 = (bf16[4,144,512]{2,1,0:T(8,128)(2,1)S(1)}, bf16[4,144,512]{2,1,0:T(8,128)(2,1)S(1)}, u32[]{:S(2)}, u32[]{:S(2)}) collective-permute-start(bf16[4,144,512]{2,1,0:T(8,128)(2,1)S(1)} %pad_maximum_fusion.same_core), channel_id=1, source_target_pairs={{0,1},{1,0},{2,3},{3,2},{4,5},{5,4},{6,7},{7,6},{8,9},{9,8},{10,11... | collective-permute-start | bytes 1769480 | tf_op jit(solution)/shard_map/ppermute | solution.py:72
  (26 other events, 261.3 us)

commit v5 on v4

--- a/solution.py
+++ b/solution.py
@@ -378,8 +378,8 @@
     capacity = min(rows, max(2, 3 * rows * top_count // (2 * expert_count)))
     slots = capacity // HALVES
 
-    down_next = around(w_down[0], 1)
-    down_far, down_last = around(down_next, 1), around(w_down[0], -1)
+    down_next, down_last = around(w_down[0], 1), around(w_down[0], -1)
+    down_far = around(down_next, 1)
     gate_own, up_own = w_gate[0].T, w_up[0].T
     weights = (gate_own, across(gate_own), up_own, across(up_own))
     order = reorder_matrix(PIECES, BATCH, slots)
@@ -390,15 +390,17 @@
     mine, theirs = project(place, attn_out, o_weight)
     sums = pair_sums(mine, across(theirs))
     parts = (sums[0],) + tuple(along(sums[shift], shift) for shift in range(1, CHIPS))
+    other_own, other_next, other_last = (across(w_down[0]), across(down_last), across(down_next))
+    other_far = across(down_far)
     down_weights = [
         w_down[0],
-        across(w_down[0]),
+        other_own,
         down_next,
-        across(down_last),
+        other_next,
         down_far,
-        across(down_far),
+        other_far,
         down_last,
-        across(down_next),
+        other_last,
     ]
     outbox0, outbox1, stream, logits = front(
         place, parts, residual, norm_gain.reshape(1, width), router_weight.T, shares, order

time: 240 us -> 240 us (level)
  no operation moved by 1% of the time
where the time goes in v5:
time: 240 us; the launch traced here: 239 us
  waiting for transfers between devices  93.9 us (39%)
  starting transfers between devices  68 us (28%)
  Pallas kernels  37 us (15%)
  blocking collectives  27.2 us (11%)
  local copies, waits for them, and re-layouts  9.95 us (4%)
    ppermute x13, waiting for transfers between devices, around(): return lax.ppermute(x, 'tensor', pairs)  52.1 us
    ppermute x8, waiting for transfers between devices, along(): return lax.ppermute(x, 'tensor', pairs)  27.5 us
    all_to_all x1, blocking collectives, shards(): lax.all_to_all(expert_out, 'expert', split_axis=0, concat_axis=0, tiled=T...  27.2 us
    ppermute x13, starting transfers between devices, around(): return lax.ppermute(x, 'tensor', pairs)  21.6 us
    ppermute x8, starting transfers between devices, across(): return lax.ppermute(x, 'tensor', [(r, r ^ 1) for r in range(2 * CHIPS)])  16 us
    all_to_all x2, starting transfers between devices, shards(): lax.all_to_all(outbox, 'expert', split_axis=0, concat_axis=0, tiled=True)  15.5 us
    pallas_call x2, Pallas kernels, down_rows(): pl.pallas_call(down_kernel, grid=(steps,), in_specs=[pl.BlockSpec((rows,...  13.7 us
    all_to_all x2, waiting for transfers between devices, shards(): lax.all_to_all(outbox, 'expert', split_axis=0, concat_axis=0, tiled=True)  12.7 us
  transfers between devices with their start and end apart: 32, of which 19 were waited for; matrix products, arithmetic and copies ran while one was open for 1% of the time, Pallas kernels for 13%

profile of v5, /device:TPU:1, one launch (start us, length us, event | category | flops | bytes accessed | tf_op | source)
XLA Modules:
  0.0 239.3 jit_solution(6832545251712776142)
XLA Ops:
  6.0 3.3 %collective-permute-start = (bf16[4,16,4096]{2,1,0:T(8,128)(2,1)S(1)}, bf16[4,16,4096]{2,1,0:T(8,128)(2,1)S(1)}, u32[]{:S(2)}, u32[]{:S(2)}) collective-permute-start(bf16[4,16,4096]{2,1,0:T(8,128)(2,1)S(1)} %get-tuple-element.21), channel_id=1, source_target_pairs={{0,1},{1,0},{2,3},{3,2},{4,5},{5,4},{6,7},{7,6},{8,9},{9,8},{10,11... | collective-permute-start | bytes 1572872 | tf_op jit(solution)/shard_map/ppermute | solution.py:72
  16.4 4.2 %collective-permute-done.1.p1 = bf16[16,4096]{1,0:T(8,128)(2,1)S(1)} collective-permute-done((bf16[16,4096]{1,0:T(8,128)(2,1)S(1)}, bf16[16,4096]{1,0:T(8,128)(2,1)S(1)}, u32[]{:S(2)}, u32[]{:S(2)}) %collective-permute-start.1) | collective-permute-done | bytes 131104 | tf_op jit(solution)/shard_map/ppermute | solution.py:59
  21.0 13.8 %collective-permute-done.3.p3 = bf16[16,4096]{1,0:T(8,128)(2,1)S(1)} collective-permute-done((bf16[16,4096]{1,0:T(8,128)(2,1)S(1)}, bf16[16,4096]{1,0:T(8,128)(2,1)S(1)}, u32[]{:S(2)}, u32[]{:S(2)}) %collective-permute-start.3) | collective-permute-done | bytes 131104 | tf_op jit(solution)/shard_map/ppermute | solution.py:59
  40.7 9.9 %all-to-all-start.2 = ((bf16[32,24,512]{2,1,0:T(8,128)(2,1)}), bf16[32,24,512]{2,1,0:T(8,128)(2,1)}, u32[]{:S(2)}, u32[]{:S(2)}) async-start(bf16[32,24,512]{2,1,0:T(8,128)(2,1)} %bitcast.69), calls=%async_computation.2 | async-start | bytes 1572864 | tf_op jit(solution)/shard_map/all_to_all | solution.py:410
  50.7 3.2 %collective-permute-start.7 = (bf16[192,4096]{1,0:T(8,128)(2,1)S(1)}, bf16[192,4096]{1,0:T(8,128)(2,1)}, u32[]{:S(2)}, u32[]{:S(2)}) collective-permute-start(bf16[192,4096]{1,0:T(8,128)(2,1)S(1)} %bitcast.59), channel_id=1, source_target_pairs={{0,1},{1,0},{2,3},{3,2},{4,5},{5,4},{6,7},{7,6},{8,9},{9,8},{10,11... | collective-permute-start | bytes 4718600 | tf_op jit(solution)/shard_map/ppermute | solution.py:72
  54.0 2.7 %collective-permute-start.16 = (bf16[192,4096]{1,0:T(8,128)(2,1)}, bf16[192,4096]{1,0:T(8,128)(2,1)}, u32[]{:S(2)}, u32[]{:S(2)}) collective-permute-start(bf16[192,4096]{1,0:T(8,128)(2,1)} %collective-permute-done.13.refs_6_), channel_id=1, source_target_pairs={{0,2},{1,7},{2,4},{3,1},{4,6},{5,3},{6,0},{7,5},{8,10},{9,15},{10,... | collective-permute-start | bytes 4718600 | tf_op jit(solution)/shard_map/ppermute | solution.py:68
  56.7 12.7 %all-to-all-done.2 = bf16[32,24,512]{2,1,0:T(8,128)(2,1)} async-done(((bf16[32,24,512]{2,1,0:T(8,128)(2,1)}), bf16[32,24,512]{2,1,0:T(8,128)(2,1)}, u32[]{:S(2)}, u32[]{:S(2)}) %all-to-all-start.2) | async-done | bytes 786464 | tf_op jit(solution)/shard_map/all_to_all | solution.py:410
  71.9 4.1 %collective-permute-start.21 = (bf16[8,96,512]{2,1,0:T(8,128)(2,1)}, bf16[8,96,512]{2,1,0:T(8,128)(2,1)}, u32[]{:S(2)}, u32[]{:S(2)}) collective-permute-start(bf16[8,96,512]{2,1,0:T(8,128)(2,1)} %rows_by_piece.3.r0), channel_id=1, source_target_pairs={{0,6},{1,3},{2,0},{3,5},{4,2},{5,7},{6,4},{7,1},{8,14},{9,11},{10,... | collective-permute-start | bytes 2359304 | tf_op jit(solution)/shard_map/ppermute | solution.py:68
  78.3 5.5 %all-to-all-start = ((bf16[32,24,512]{2,1,0:T(8,128)(2,1)}), bf16[32,24,512]{2,1,0:T(8,128)(2,1)}, u32[]{:S(2)}, u32[]{:S(2)}) async-start(bf16[32,24,512]{2,1,0:T(8,128)(2,1)} %bitcast.68), calls=%async_computation | async-start | bytes 1572864 | tf_op jit(solution)/shard_map/all_to_all | solution.py:410
  84.6 6.1 %collective-permute-done.14.refs_10_ = bf16[192,4096]{1,0:T(8,128)(2,1)} collective-permute-done((bf16[192,4096]{1,0:T(8,128)(2,1)}, bf16[192,4096]{1,0:T(8,128)(2,1)}, u32[]{:S(2)}, u32[]{:S(2)}) %collective-permute-start.14) | collective-permute-done | bytes 1572896 | tf_op jit(solution)/shard_map/ppermute | solution.py:68
  92.0 15.6 %collective-permute-done.21.r3 = bf16[8,96,512]{2,1,0:T(8,128)(2,1)} collective-permute-done((bf16[8,96,512]{2,1,0:T(8,128)(2,1)}, bf16[8,96,512]{2,1,0:T(8,128)(2,1)}, u32[]{:S(2)}, u32[]{:S(2)}) %collective-permute-start.21) | collective-permute-done | bytes 786464 | tf_op jit(solution)/shard_map/ppermute | solution.py:68
  112.0 7.6 %collective-permute-done.20.r2 = bf16[8,96,512]{2,1,0:T(8,128)(2,1)} collective-permute-done((bf16[8,96,512]{2,1,0:T(8,128)(2,1)}, bf16[8,96,512]{2,1,0:T(8,128)(2,1)}, u32[]{:S(2)}, u32[]{:S(2)}) %collective-permute-start.20) | collective-permute-done | bytes 786464 | tf_op jit(solution)/shard_map/ppermute | solution.py:68
  121.8 5.8 %up_rows.3 = (bf16[96,384]{1,0:T(8,128)(2,1)S(1)}, bf16[96,384]{1,0:T(8,128)(2,1)S(1)}, bf16[96,384]{1,0:T(8,128)(2,1)S(1)}, bf16[96,384]{1,0:T(8,128)(2,1)S(1)}) custom-call(bf16[8,96,512]{2,1,0:T(8,128)(2,1)} %rows_by_piece.3.r0, bf16[8,96,512]{2,1,0:T(8,128)(2,1)} %collective-permute-done.19.r1, bf16[8,96,512]{2,1,0:T(8,128)(2,1)} %collective-permute-done.20.r2, ...), custom_call_target="tpu_custom_call" | custom-call | tf_op jit(solution)/shard_map/up_rows/pallas_call | solution.py:221
  129.2 3.3 %collective-permute-done.22.refs_1_ = bf16[96,384]{1,0:T(8,128)(2,1)S(1)} collective-permute-done((bf16[96,384]{1,0:T(8,128)(2,1)S(1)}, bf16[96,384]{1,0:T(8,128)(2,1)S(1)}, u32[]{:S(2)}, u32[]{:S(2)}) %collective-permute-start.22) | collective-permute-done | bytes 73760 | tf_op jit(solution)/shard_map/ppermute | solution.py:68
  134.9 6.9 %down_rows.3 = bf16[768,512]{1,0:T(8,128)(2,1)S(1)} custom-call(bf16[96,384]{1,0:T(8,128)(2,1)S(1)} %get-tuple-element.32.refs_0_, bf16[96,384]{1,0:T(8,128)(2,1)S(1)} %collective-permute-done.22.refs_1_, bf16[96,384]{1,0:T(8,128)(2,1)S(1)} %collective-permute-done.23.refs_2_, bf16[96,384]{1,0:T(8,128)(2,1)S(1)} %collective-permute-done.24.refs_3_, ...), custom_call_target="tpu_custom_call" | custom-call | tf_op jit(solution)/shard_map/down_rows/pallas_call | solution.py:263
  142.7 9.4 %all-to-all-start.3 = ((bf16[32,24,512]{2,1,0:T(8,128)(2,1)}), bf16[32,24,512]{2,1,0:T(8,128)(2,1)}, u32[]{:S(2)}, u32[]{:S(2)}) async-start(bf16[32,24,512]{2,1,0:T(8,128)(2,1)} %bitcast.66), calls=%async_computation.3 | async-start | bytes 1572864 | tf_op jit(solution)/shard_map/all_to_all | solution.py:428
  152.3 2.5 %collective-permute-start.5 = (bf16[8,96,512]{2,1,0:T(8,128)(2,1)}, bf16[8,96,512]{2,1,0:T(8,128)(2,1)S(1)}, u32[]{:S(2)}, u32[]{:S(2)}) collective-permute-start(bf16[8,96,512]{2,1,0:T(8,128)(2,1)} %collective-permute-done.4.r1), channel_id=1, source_target_pairs={{0,2},{1,7},{2,4},{3,1},{4,6},{5,3},{6,0},{7,5},{8,10},{9,15},{10,... | collective-permute-start | bytes 2359304 | tf_op jit(solution)/shard_map/ppermute | solution.py:68
  154.9 13.0 %collective-permute-done.6.r3 = bf16[8,96,512]{2,1,0:T(8,128)(2,1)S(1)} collective-permute-done((bf16[8,96,512]{2,1,0:T(8,128)(2,1)}, bf16[8,96,512]{2,1,0:T(8,128)(2,1)S(1)}, u32[]{:S(2)}, u32[]{:S(2)}) %collective-permute-start.6) | collective-permute-done | bytes 786464 | tf_op jit(solution)/shard_map/ppermute | solution.py:68
  170.2 5.5 %up_rows.2 = (bf16[96,384]{1,0:T(8,128)(2,1)S(1)}, bf16[96,384]{1,0:T(8,128)(2,1)S(1)}, bf16[96,384]{1,0:T(8,128)(2,1)S(1)}, bf16[96,384]{1,0:T(8,128)(2,1)S(1)}) custom-call(bf16[8,96,512]{2,1,0:T(8,128)(2,1)} %rows_by_piece.2.r0, bf16[8,96,512]{2,1,0:T(8,128)(2,1)} %collective-permute-done.4.r1, bf16[8,96,512]{2,1,0:T(8,128)(2,1)S(1)} %collective-permute-done.5.r2, ...), custom_call_target="tpu_custom_call" | custom-call | tf_op jit(solution)/shard_map/up_rows/pallas_call | solution.py:221
  175.7 3.7 %collective-permute-start.9 = (bf16[96,384]{1,0:T(8,128)(2,1)S(1)}, bf16[96,384]{1,0:T(8,128)(2,1)S(1)}, u32[]{:S(2)}, u32[]{:S(2)}) collective-permute-start(bf16[96,384]{1,0:T(8,128)(2,1)S(1)} %get-tuple-element.28), channel_id=1, source_target_pairs={{0,2},{1,7},{2,4},{3,1},{4,6},{5,3},{6,0},{7,5},{8,10},{9,15},{10,... | collective-permute-start | bytes 221192 | tf_op jit(solution)/shard_map/ppermute | solution.py:68
  181.5 2.7 %collective-permute-done.10.refs_2_ = bf16[96,384]{1,0:T(8,128)(2,1)S(1)} collective-permute-done((bf16[96,384]{1,0:T(8,128)(2,1)S(1)}, bf16[96,384]{1,0:T(8,128)(2,1)S(1)}, u32[]{:S(2)}, u32[]{:S(2)}) %collective-permute-start.10) | collective-permute-done | bytes 73760 | tf_op jit(solution)/shard_map/ppermute | solution.py:59
  185.4 6.8 %down_rows.2 = bf16[768,512]{1,0:T(8,128)(2,1)S(1)} custom-call(bf16[96,384]{1,0:T(8,128)(2,1)S(1)} %get-tuple-element.27.refs_0_, bf16[96,384]{1,0:T(8,128)(2,1)S(1)} %collective-permute-done.9.refs_1_, bf16[96,384]{1,0:T(8,128)(2,1)S(1)} %collective-permute-done.10.refs_2_, bf16[96,384]{1,0:T(8,128)(2,1)S(1)} %collective-permute-done.11.refs_3_, ...), custom_call_target="tpu_custom_call" | custom-call | tf_op jit(solution)/shard_map/down_rows/pallas_call | solution.py:263
  192.2 27.2 %all_to_all.44 = bf16[32,24,512]{2,1,0:T(8,128)(2,1)S(1)} all-to-all(bf16[32,24,512]{2,1,0:T(8,128)(2,1)S(1)} %bitcast.67), channel_id=1, replica_groups=mesh['expert'=32,'tensor'=8] {'expert'}, dimensions={0} | all-to-all | bytes 1572864 | tf_op jit(solution)/shard_map/all_to_all | solution.py:428
  228.5 6.9 %collective-permute-start.28 = (bf16[4,144,512]{2,1,0:T(8,128)(2,1)S(1)}, bf16[4,144,512]{2,1,0:T(8,128)(2,1)S(1)}, u32[]{:S(2)}, u32[]{:S(2)}) collective-permute-start(bf16[4,144,512]{2,1,0:T(8,128)(2,1)S(1)} %pad_maximum_fusion.same_core), channel_id=1, source_target_pairs={{0,1},{1,0},{2,3},{3,2},{4,5},{5,4},{6,7},{7,6},{8,9},{9,8},{10,11... | collective-permute-start | bytes 1769480 | tf_op jit(solution)/shard_map/ppermute | solution.py:72
  (122 shorter events, 55.7 us)
Async XLA Ops:
  6.0 6.5 %collective-permute-start = (bf16[4,16,4096]{2,1,0:T(8,128)(2,1)S(1)}, bf16[4,16,4096]{2,1,0:T(8,128)(2,1)S(1)}, u32[]{:S(2)}, u32[]{:S(2)}) collective-permute-start(bf16[4,16,4096]{2,1,0:T(8,128)(2,1)S(1)} %get-tuple-element.21), channel_id=1, source_target_pairs={{0,1},{1,0},{2,3},{3,2},{4,5},{5,4},{6,7},{7,6},{8,9},{9,8},{10,11... | collective-permute-start | bytes 1572872 | tf_op jit(solution)/shard_map/ppermute | solution.py:72
  9.3 44.7 %collective-permute-start.13 = (bf16[192,4096]{1,0:T(8,128)(2,1)}, bf16[192,4096]{1,0:T(8,128)(2,1)}, u32[]{:S(2)}, u32[]{:S(2)}) collective-permute-start(bf16[192,4096]{1,0:T(8,128)(2,1)} %bitcast.28.refs_4_), channel_id=1, source_target_pairs={{0,2},{1,7},{2,4},{3,1},{4,6},{5,3},{6,0},{7,5},{8,10},{9,15},{10,... | collective-permute-start | bytes 4718600 | tf_op jit(solution)/shard_map/ppermute | solution.py:68
  12.7 7.9 %collective-permute-start.1 = (bf16[16,4096]{1,0:T(8,128)(2,1)S(1)}, bf16[16,4096]{1,0:T(8,128)(2,1)S(1)}, u32[]{:S(2)}, u32[]{:S(2)}) collective-permute-start(bf16[16,4096]{1,0:T(8,128)(2,1)S(1)} %get-tuple-element.23), channel_id=1, source_target_pairs={{0,2},{1,3},{2,4},{3,5},{4,6},{5,7},{6,0},{7,1},{8,10},{9,11},{10,... | collective-permute-start | bytes 393224 | tf_op jit(solution)/shard_map/ppermute | solution.py:59
  13.2 7.8 %collective-permute-start.2 = (bf16[16,4096]{1,0:T(8,128)(2,1)S(1)}, bf16[16,4096]{1,0:T(8,128)(2,1)S(1)}, u32[]{:S(2)}, u32[]{:S(2)}) collective-permute-start(bf16[16,4096]{1,0:T(8,128)(2,1)S(1)} %get-tuple-element.24), channel_id=1, source_target_pairs={{0,4},{1,5},{2,6},{3,7},{4,0},{5,1},{6,2},{7,3},{8,12},{9,13},{10,... | collective-permute-start | bytes 393224 | tf_op jit(solution)/shard_map/ppermute | solution.py:59
  14.4 20.4 %collective-permute-start.3 = (bf16[16,4096]{1,0:T(8,128)(2,1)S(1)}, bf16[16,4096]{1,0:T(8,128)(2,1)S(1)}, u32[]{:S(2)}, u32[]{:S(2)}) collective-permute-start(bf16[16,4096]{1,0:T(8,128)(2,1)S(1)} %get-tuple-element.25), channel_id=1, source_target_pairs={{0,6},{1,7},{2,0},{3,1},{4,2},{5,3},{6,4},{7,5},{8,14},{9,15},{10,... | collective-permute-start | bytes 393224 | tf_op jit(solution)/shard_map/ppermute | solution.py:59
  40.7 28.6 %all-to-all-start.2 = ((bf16[32,24,512]{2,1,0:T(8,128)(2,1)}), bf16[32,24,512]{2,1,0:T(8,128)(2,1)}, u32[]{:S(2)}, u32[]{:S(2)}) async-start(bf16[32,24,512]{2,1,0:T(8,128)(2,1)} %bitcast.69), calls=%async_computation.2 | async-start | bytes 1572864 | tf_op jit(solution)/shard_map/all_to_all | solution.py:410
  50.7 25.4 %collective-permute-start.7 = (bf16[192,4096]{1,0:T(8,128)(2,1)S(1)}, bf16[192,4096]{1,0:T(8,128)(2,1)}, u32[]{:S(2)}, u32[]{:S(2)}) collective-permute-start(bf16[192,4096]{1,0:T(8,128)(2,1)S(1)} %bitcast.59), channel_id=1, source_target_pairs={{0,1},{1,0},{2,3},{3,2},{4,5},{5,4},{6,7},{7,6},{8,9},{9,8},{10,11... | collective-permute-start | bytes 4718600 | tf_op jit(solution)/shard_map/ppermute | solution.py:72
  53.9 30.0 %collective-permute-start.8 = (bf16[192,4096]{1,0:T(8,128)(2,1)S(1)}, bf16[192,4096]{1,0:T(8,128)(2,1)}, u32[]{:S(2)}, u32[]{:S(2)}) collective-permute-start(bf16[192,4096]{1,0:T(8,128)(2,1)S(1)} %bitcast.62), channel_id=1, source_target_pairs={{0,1},{1,0},{2,3},{3,2},{4,5},{5,4},{6,7},{7,6},{8,9},{9,8},{10,11... | collective-permute-start | bytes 4718600 | tf_op jit(solution)/shard_map/ppermute | solution.py:72
  54.0 36.7 %collective-permute-start.14 = (bf16[192,4096]{1,0:T(8,128)(2,1)}, bf16[192,4096]{1,0:T(8,128)(2,1)}, u32[]{:S(2)}, u32[]{:S(2)}) collective-permute-start(bf16[192,4096]{1,0:T(8,128)(2,1)} %bitcast.28.refs_4_), channel_id=1, source_target_pairs={{0,6},{1,3},{2,0},{3,5},{4,2},{5,7},{6,4},{7,1},{8,14},{9,11},{10,... | collective-permute-start | bytes 4718600 | tf_op jit(solution)/shard_map/ppermute | solution.py:68
  54.0 54.0 %collective-permute-start.16 = (bf16[192,4096]{1,0:T(8,128)(2,1)}, bf16[192,4096]{1,0:T(8,128)(2,1)}, u32[]{:S(2)}, u32[]{:S(2)}) collective-permute-start(bf16[192,4096]{1,0:T(8,128)(2,1)} %collective-permute-done.13.refs_6_), channel_id=1, source_target_pairs={{0,2},{1,7},{2,4},{3,1},{4,6},{5,3},{6,0},{7,5},{8,10},{9,15},{10,... | collective-permute-start | bytes 4718600 | tf_op jit(solution)/shard_map/ppermute | solution.py:68
  71.9 35.7 %collective-permute-start.21 = (bf16[8,96,512]{2,1,0:T(8,128)(2,1)}, bf16[8,96,512]{2,1,0:T(8,128)(2,1)}, u32[]{:S(2)}, u32[]{:S(2)}) collective-permute-start(bf16[8,96,512]{2,1,0:T(8,128)(2,1)} %rows_by_piece.3.r0), channel_id=1, source_target_pairs={{0,6},{1,3},{2,0},{3,5},{4,2},{5,7},{6,4},{7,1},{8,14},{9,11},{10,... | collective-permute-start | bytes 2359304 | tf_op jit(solution)/shard_map/ppermute | solution.py:68
  76.0 32.1 %collective-permute-start.19 = (bf16[8,96,512]{2,1,0:T(8,128)(2,1)}, bf16[8,96,512]{2,1,0:T(8,128)(2,1)}, u32[]{:S(2)}, u32[]{:S(2)}) collective-permute-start(bf16[8,96,512]{2,1,0:T(8,128)(2,1)} %rows_by_piece.3.r0), channel_id=1, source_target_pairs={{0,2},{1,7},{2,4},{3,1},{4,6},{5,3},{6,0},{7,5},{8,10},{9,15},{10,... | collective-permute-start | bytes 2359304 | tf_op jit(solution)/shard_map/ppermute | solution.py:68
  78.3 31.1 %all-to-all-start = ((bf16[32,24,512]{2,1,0:T(8,128)(2,1)}), bf16[32,24,512]{2,1,0:T(8,128)(2,1)}, u32[]{:S(2)}, u32[]{:S(2)}) async-start(bf16[32,24,512]{2,1,0:T(8,128)(2,1)} %bitcast.68), calls=%async_computation | async-start | bytes 1572864 | tf_op jit(solution)/shard_map/all_to_all | solution.py:410
  83.9 43.7 %collective-permute-start.12 = (bf16[192,4096]{1,0:T(8,128)(2,1)}, bf16[192,4096]{1,0:T(8,128)(2,1)}, u32[]{:S(2)}, u32[]{:S(2)}) collective-permute-start(bf16[192,4096]{1,0:T(8,128)(2,1)} %bitcast.28.refs_4_), channel_id=1, source_target_pairs={{0,1},{1,0},{2,3},{3,2},{4,5},{5,4},{6,7},{7,6},{8,9},{9,8},{10,11... | collective-permute-start | bytes 4718600 | tf_op jit(solution)/shard_map/ppermute | solution.py:72
  90.7 37.0 %collective-permute-start.15 = (bf16[192,4096]{1,0:T(8,128)(2,1)}, bf16[192,4096]{1,0:T(8,128)(2,1)}, u32[]{:S(2)}, u32[]{:S(2)}) collective-permute-start(bf16[192,4096]{1,0:T(8,128)(2,1)} %collective-permute-done.14.refs_10_), channel_id=1, source_target_pairs={{0,1},{1,0},{2,3},{3,2},{4,5},{5,4},{6,7},{7,6},{8,9},{9,8},{10,11... | collective-permute-start | bytes 4718600 | tf_op jit(solution)/shard_map/ppermute | solution.py:72
  107.6 21.1 %collective-permute-start.18 = (bf16[192,4096]{1,0:T(8,128)(2,1)}, bf16[192,4096]{1,0:T(8,128)(2,1)}, u32[]{:S(2)}, u32[]{:S(2)}) collective-permute-start(bf16[192,4096]{1,0:T(8,128)(2,1)} %collective-permute-done.13.refs_6_), channel_id=1, source_target_pairs={{0,1},{1,0},{2,3},{3,2},{4,5},{5,4},{6,7},{7,6},{8,9},{9,8},{10,11... | collective-permute-start | bytes 4718600 | tf_op jit(solution)/shard_map/ppermute | solution.py:72
  108.0 26.9 %collective-permute-start.17 = (bf16[192,4096]{1,0:T(8,128)(2,1)}, bf16[192,4096]{1,0:T(8,128)(2,1)}, u32[]{:S(2)}, u32[]{:S(2)}) collective-permute-start(bf16[192,4096]{1,0:T(8,128)(2,1)} %collective-permute-done.16.refs_8_), channel_id=1, source_target_pairs={{0,1},{1,0},{2,3},{3,2},{4,5},{5,4},{6,7},{7,6},{8,9},{9,8},{10,11... | collective-permute-start | bytes 4718600 | tf_op jit(solution)/shard_map/ppermute | solution.py:72
  108.1 11.5 %collective-permute-start.20 = (bf16[8,96,512]{2,1,0:T(8,128)(2,1)}, bf16[8,96,512]{2,1,0:T(8,128)(2,1)}, u32[]{:S(2)}, u32[]{:S(2)}) collective-permute-start(bf16[8,96,512]{2,1,0:T(8,128)(2,1)} %collective-permute-done.19.r1), channel_id=1, source_target_pairs={{0,2},{1,7},{2,4},{3,1},{4,6},{5,3},{6,0},{7,5},{8,10},{9,15},{10,... | collective-permute-start | bytes 2359304 | tf_op jit(solution)/shard_map/ppermute | solution.py:68
  119.6 32.8 %collective-permute-start.4 = (bf16[8,96,512]{2,1,0:T(8,128)(2,1)}, bf16[8,96,512]{2,1,0:T(8,128)(2,1)}, u32[]{:S(2)}, u32[]{:S(2)}) collective-permute-start(bf16[8,96,512]{2,1,0:T(8,128)(2,1)} %rows_by_piece.2.r0), channel_id=1, source_target_pairs={{0,2},{1,7},{2,4},{3,1},{4,6},{5,3},{6,0},{7,5},{8,10},{9,15},{10,... | collective-permute-start | bytes 2359304 | tf_op jit(solution)/shard_map/ppermute | solution.py:68
  142.7 49.6 %all-to-all-start.3 = ((bf16[32,24,512]{2,1,0:T(8,128)(2,1)}), bf16[32,24,512]{2,1,0:T(8,128)(2,1)}, u32[]{:S(2)}, u32[]{:S(2)}) async-start(bf16[32,24,512]{2,1,0:T(8,128)(2,1)} %bitcast.66), calls=%async_computation.3 | async-start | bytes 1572864 | tf_op jit(solution)/shard_map/all_to_all | solution.py:428
  152.1 15.8 %collective-permute-start.6 = (bf16[8,96,512]{2,1,0:T(8,128)(2,1)}, bf16[8,96,512]{2,1,0:T(8,128)(2,1)S(1)}, u32[]{:S(2)}, u32[]{:S(2)}) collective-permute-start(bf16[8,96,512]{2,1,0:T(8,128)(2,1)} %rows_by_piece.2.r0), channel_id=1, source_target_pairs={{0,6},{1,3},{2,0},{3,5},{4,2},{5,7},{6,4},{7,1},{8,14},{9,11},{10,... | collective-permute-start | bytes 2359304 | tf_op jit(solution)/shard_map/ppermute | solution.py:68
  152.3 17.9 %collective-permute-start.5 = (bf16[8,96,512]{2,1,0:T(8,128)(2,1)}, bf16[8,96,512]{2,1,0:T(8,128)(2,1)S(1)}, u32[]{:S(2)}, u32[]{:S(2)}) collective-permute-start(bf16[8,96,512]{2,1,0:T(8,128)(2,1)} %collective-permute-done.4.r1), channel_id=1, source_target_pairs={{0,2},{1,7},{2,4},{3,1},{4,6},{5,3},{6,0},{7,5},{8,10},{9,15},{10,... | collective-permute-start | bytes 2359304 | tf_op jit(solution)/shard_map/ppermute | solution.py:68
  221.4 7.1 %collective-permute-start.25 = (bf16[144,512]{1,0:T(8,128)(2,1)S(1)}, bf16[144,512]{1,0:T(8,128)(2,1)S(1)}, u32[]{:S(2)}, u32[]{:S(2)}) collective-permute-start(bf16[144,512]{1,0:T(8,128)(2,1)S(1)} %finish.1), channel_id=1, source_target_pairs={{0,2},{1,3},{2,4},{3,5},{4,6},{5,7},{6,0},{7,1},{8,10},{9,11},{10,... | collective-permute-start | bytes 442376 | tf_op jit(solution)/shard_map/ppermute | solution.py:59
  228.5 8.5 %collective-permute-start.28 = (bf16[4,144,512]{2,1,0:T(8,128)(2,1)S(1)}, bf16[4,144,512]{2,1,0:T(8,128)(2,1)S(1)}, u32[]{:S(2)}, u32[]{:S(2)}) collective-permute-start(bf16[4,144,512]{2,1,0:T(8,128)(2,1)S(1)} %pad_maximum_fusion.same_core), channel_id=1, source_target_pairs={{0,1},{1,0},{2,3},{3,2},{4,5},{5,4},{6,7},{7,6},{8,9},{9,8},{10,11... | collective-permute-start | bytes 1769480 | tf_op jit(solution)/shard_map/ppermute | solution.py:72
  (26 other events, 261.3 us)
